TPU v7x, 256 devices: a whole 4x4x8 slice. The times are simulated.
256 devices in a mesh: gx: 16 (over y, z_lo, core), gy: 4 (over x), gz: 4 (over z_hi).
Axes of the slice: x: 4, y: 4, z: 8 (z_hi: 4, z_lo: 2; z = z_hi * 2 + z_lo), core: 2. Of those that a mesh axis runs over, the one named last changes fastest.
Arguments:
- features: bfloat16 [32, 64, 16, 1024], P(None, 'gx', 'gy', 'gz'), may hold values from -6 to 6
- conv_one: bfloat16 [32, 864], replicated, may hold values from -0.3125 to 0.3125
- conv_two: bfloat16 [32, 864], replicated, may hold values from -0.3125 to 0.3125
- conv_three: bfloat16 [64, 864], replicated, may hold values from -0.3125 to 0.3125
- conv_four: bfloat16 [64, 1728], replicated, may hold values from -0.21875 to 0.21875
- depth_one: bfloat16 [64, 27], replicated, may hold values from -1.25 to 1.25
- point_one: bfloat16 [128, 64], replicated, may hold values from -1 to 1
- depth_two: bfloat16 [128, 27], replicated, may hold values from -1.25 to 1.25
- point_two: bfloat16 [128, 128], replicated, may hold values from -0.75 to 0.75
- conv_five: bfloat16 [64, 5184], replicated, may hold values from -0.125 to 0.125
- conv_six: bfloat16 [32, 2592], replicated, may hold values from -0.125 to 0.125
Outputs:
- decoded: bfloat16 [32, 64, 16, 1024], P(None, 'gx', 'gy', 'gz')
All inputs are finite; a program needn't handle non-finite values.
Results may differ from a plain program's by a relative error of at most 0.015.
Values may be sent and summed in bfloat16 or wider, within the bound.
No kernel may reach another device: no remote copies, remote signals or barrier semaphores. Data moves between devices by JAX's collectives and lax.ppermute only.
A program may use at most 64 MiB of HBM per device.

v0:
```python
import jax
import jax.numpy as jnp
from jax import lax
from jax.sharding import PartitionSpec as P


def padded_2(cells, sides, width):
    for axis, dim in sides:
        count = lax.axis_size(axis)
        ends = count - 1
        head = lax.slice_in_dim(cells, 0, width, axis=dim)
        tail = lax.slice_in_dim(cells, cells.shape[dim] - width, cells.shape[dim], axis=dim)
        cells = jnp.concatenate(
            [
                lax.ppermute(tail, axis, [(i, (i + 1) % count) for i in range(ends)]),
                cells,
                lax.ppermute(head, axis, [((i + 1) % count, i) for i in range(ends)]),
            ],
            axis=dim,
        )
    return cells


def rectify(values):
    return jnp.maximum(values, 0.0)


def pad_faces(values):
    return padded_2(values, (("gx", 1), ("gy", 2), ("gz", 3)), 1)


def convolve(padded, weight):
    channels = padded.shape[0]
    width_out = weight.shape[0]
    size_x = padded.shape[1] - 2
    size_y = padded.shape[2] - 2
    size_z = padded.shape[3] - 2
    volume = size_x * size_y * size_z
    summed = jnp.zeros((width_out, volume), jnp.float32)
    for offset_x in range(3):
        for offset_y in range(3):
            for offset_z in range(3):
                tap_index = (offset_x * 3 + offset_y) * 3 + offset_z
                piece = padded[
                    :,
                    offset_x : offset_x + size_x,
                    offset_y : offset_y + size_y,
                    offset_z : offset_z + size_z,
                ].reshape(channels, volume)
                columns = weight[:, tap_index * channels : (tap_index + 1) * channels]
                summed = summed + jnp.dot(columns, piece, preferred_element_type=jnp.float32)
    return summed.reshape(width_out, size_x, size_y, size_z)


def depthwise(padded, tap_weights):
    size_x = padded.shape[1] - 2
    size_y = padded.shape[2] - 2
    size_z = padded.shape[3] - 2
    summed = jnp.zeros((padded.shape[0], size_x, size_y, size_z), jnp.float32)
    for offset_x in range(3):
        for offset_y in range(3):
            for offset_z in range(3):
                tap_index = (offset_x * 3 + offset_y) * 3 + offset_z
                factor = tap_weights[:, tap_index].astype(jnp.float32)[:, None, None, None]
                window = padded[
                    :,
                    offset_x : offset_x + size_x,
                    offset_y : offset_y + size_y,
                    offset_z : offset_z + size_z,
                ]
                summed = summed + window.astype(jnp.float32) * factor
    return summed.astype(jnp.bfloat16)


def shrink(values):
    channels, size_x, size_y, size_z = values.shape
    return values.reshape(channels, size_x // 2, 2, size_y // 2, 2, size_z // 2, 2).max(
        axis=(2, 4, 6)
    )


def enlarge(values):
    channels, size_x, size_y, size_z = values.shape
    grown = jnp.broadcast_to(
        values[:, :, None, :, None, :, None], (channels, size_x, 2, size_y, 2, size_z, 2)
    )
    return grown.reshape(channels, 2 * size_x, 2 * size_y, 2 * size_z)


def conv_pair(values, weight_a, weight_b):
    middle = rectify(convolve(pad_faces(values), weight_a)).astype(jnp.bfloat16)
    return rectify(convolve(pad_faces(middle), weight_b)).astype(jnp.bfloat16)


def channel_depthwise(values, tap_weights):
    channels, size_x, size_y, size_z = values.shape
    planes = lax.axis_size(("gx", "gy"))
    rows_x = lax.axis_size("gx")
    rows_y = lax.axis_size("gy")
    per_device = channels // planes
    volume = size_x * size_y * size_z
    outgoing = values.reshape(1, channels, volume)
    arrived = lax.all_to_all(outgoing, ("gx", "gy"), split_axis=1, concat_axis=0, tiled=True)
    arranged = arrived.reshape(rows_x, rows_y, per_device, size_x, size_y, size_z).transpose(
        2, 0, 3, 1, 4, 5
    )
    arranged = arranged.reshape(per_device, rows_x * size_x, rows_y * size_y, size_z)
    rimmed = padded_2(arranged, (("gz", 3),), 1)
    padded = jnp.pad(rimmed, ((0, 0), (1, 1), (1, 1), (0, 0)))
    own_taps = lax.dynamic_slice_in_dim(
        tap_weights, lax.axis_index(("gx", "gy")) * per_device, per_device, 0
    )
    spread = depthwise(padded, own_taps)
    outgoing_back = spread.reshape(per_device, rows_x, size_x, rows_y, size_y, size_z).transpose(
        1, 3, 0, 2, 4, 5
    )
    outgoing_back = outgoing_back.reshape(planes, per_device, volume)
    returned = lax.all_to_all(outgoing_back, ("gx", "gy"), split_axis=0, concat_axis=1, tiled=True)
    return returned.reshape(channels, size_x, size_y, size_z)


def quarter_layer(values, tap_weights, mixing):
    channels, size_x, size_y, size_z = values.shape
    spread = channel_depthwise(values, tap_weights)
    flattened = spread.reshape(channels, size_x * size_y * size_z)
    mixed_out = rectify(jnp.dot(mixing, flattened, preferred_element_type=jnp.float32))
    return mixed_out.astype(jnp.bfloat16).reshape(mixing.shape[0], size_x, size_y, size_z)


def decoder_input(coarse, fine_skip):
    return pad_faces(jnp.concatenate([enlarge(coarse), fine_skip], axis=0))


def local(
    features,
    conv_one,
    conv_two,
    conv_three,
    conv_four,
    depth_one,
    point_one,
    depth_two,
    point_two,
    conv_five,
    conv_six,
):
    skip = conv_pair(features, conv_one, conv_two)
    half_in = shrink(skip)
    half_skip = conv_pair(half_in, conv_three, conv_four)
    quarter = shrink(half_skip)
    mixed_one = quarter_layer(quarter, depth_one, point_one)
    mixed_two = quarter_layer(mixed_one, depth_two, point_two)
    half_out = rectify(convolve(decoder_input(mixed_two, half_skip), conv_five)).astype(
        jnp.bfloat16
    )
    return convolve(decoder_input(half_out, skip), conv_six).astype(jnp.bfloat16)


def solution(mesh):
    in_specs = (P(None, "gx", "gy", "gz"), P(), P(), P(), P(), P(), P(), P(), P(), P(), P())
    out_specs = P(None, "gx", "gy", "gz")
    return jax.shard_map(local, mesh=mesh, in_specs=in_specs, out_specs=out_specs, check_vma=False)
```

profile of v0, /device:TPU:72, one launch (start us, length us, event | category | flops | bytes accessed | tf_op | source)
XLA Modules:
  0.0 486.0 jit_solution(7746145017843126168)
XLA Ops:
  2.9 4.5 collective-permute-start.1
  19.6 4.5 collective-permute-done.3
  27.8 6.0 %collective-permute-start.4 = (bf16[32,6,6,1]{3,2,1,0:T(8,128)(2,1)}, bf16[32,6,6,1]{3,2,1,0:T(8,128)(2,1)}, u32[]{:S(2)}, u32[]{:S(2)}) collective-permute-start(bf16[32,6,6,1]{3,2,1,0:T(8,128)(2,1)} %get-tuple-element.112), channel_id=1, source_target_pairs={{0,1},{1,2},{2,3},{4,5},{5,6},{6,7},{8,9},{9,10},{10,11},{12,13},{... | collective-permute-start | bytes 6920 | tf_op jit(solution)/shard_map/ppermute | solution.py:15
  40.0 9.7 %collective-permute-done.5 = bf16[32,6,6,1]{3,2,1,0:T(8,128)(2,1)} collective-permute-done((bf16[32,6,6,1]{3,2,1,0:T(8,128)(2,1)}, bf16[32,6,6,1]{3,2,1,0:T(8,128)(2,1)}, u32[]{:S(2)}, u32[]{:S(2)}) %collective-permute-start.5) | collective-permute-done | bytes 2336 | tf_op jit(solution)/shard_map/ppermute | solution.py:17
  54.0 4.1 fusion.339
  99.3 4.5 collective-permute-start.7
  114.6 4.1 collective-permute-done.9
  120.5 5.6 %collective-permute-start.10 = (bf16[32,6,6,1]{3,2,1,0:T(8,128)(2,1)}, bf16[32,6,6,1]{3,2,1,0:T(8,128)(2,1)}, u32[]{:S(2)}, u32[]{:S(2)}) collective-permute-start(bf16[32,6,6,1]{3,2,1,0:T(8,128)(2,1)} %get-tuple-element.107), channel_id=1, source_target_pairs={{0,1},{1,2},{2,3},{4,5},{5,6},{6,7},{8,9},{9,10},{10,11},{12,13},{... | collective-permute-start | bytes 6920 | tf_op jit(solution)/shard_map/ppermute | solution.py:15
  141.3 6.6 %collective-permute-done.11 = bf16[32,6,6,1]{3,2,1,0:T(8,128)(2,1)} collective-permute-done((bf16[32,6,6,1]{3,2,1,0:T(8,128)(2,1)}, bf16[32,6,6,1]{3,2,1,0:T(8,128)(2,1)}, u32[]{:S(2)}, u32[]{:S(2)}) %collective-permute-start.11) | collective-permute-done | bytes 2336 | tf_op jit(solution)/shard_map/ppermute | solution.py:17
  205.8 4.5 collective-permute-start.13
  217.1 4.2 collective-permute-done.15
  229.3 5.0 %collective-permute-done.17 = bf16[32,4,4,1]{3,0,2,1:T(8,128)(2,1)S(1)} collective-permute-done((bf16[32,4,4,1]{3,0,2,1:T(8,128)(2,1)S(1)}, bf16[32,4,4,1]{3,0,2,1:T(8,128)(2,1)S(1)}, u32[]{:S(2)}, u32[]{:S(2)}) %collective-permute-start.17) | collective-permute-done | bytes 1056 | tf_op jit(solution)/shard_map/ppermute | solution.py:17
  242.2 4.5 collective-permute-start.19
  261.9 5.1 %collective-permute-start.23 = (bf16[64,4,4,1]{3,2,1,0:T(4,128)(2,1)S(1)}, bf16[64,4,4,1]{3,2,1,0:T(4,128)(2,1)S(1)}, u32[]{:S(2)}, u32[]{:S(2)}) collective-permute-start(bf16[64,4,4,1]{3,2,1,0:T(4,128)(2,1)S(1)} %get-tuple-element.170), channel_id=1, source_target_pairs={{1,0},{2,1},{3,2},{5,4},{6,5},{7,6},{9,8},{10,9},{11,10},{13,12},{... | collective-permute-start | bytes 6152 | tf_op jit(solution)/shard_map/ppermute | solution.py:17
  270.8 7.8 %collective-permute-done.23 = bf16[64,4,4,1]{3,2,1,0:T(4,128)(2,1)S(1)} collective-permute-done((bf16[64,4,4,1]{3,2,1,0:T(4,128)(2,1)S(1)}, bf16[64,4,4,1]{3,2,1,0:T(4,128)(2,1)S(1)}, u32[]{:S(2)}, u32[]{:S(2)}) %collective-permute-start.23) | collective-permute-done | bytes 2080 | tf_op jit(solution)/shard_map/ppermute | solution.py:17
  298.9 4.2 all-to-all-start
  323.2 4.8 collective-permute-start.25
  332.2 8.4 %all-to-all-start.1 = ((bf16[64,1,64]{2,1,0:T(2,128)(2,1)}), bf16[64,1,64]{2,1,0:T(2,128)(2,1)S(1)}, u32[]{:S(2)}, u32[]{:S(2)}) async-start(bf16[64,1,64]{2,1,0:T(2,128)(2,1)} %copy.374), calls=%async_computation.1 | async-start | bytes 65536 | tf_op jit(solution)/shard_map/all_to_all | solution.py:118
  340.6 7.0 %all-to-all-done.1 = bf16[64,1,64]{2,1,0:T(2,128)(2,1)S(1)} async-done(((bf16[64,1,64]{2,1,0:T(2,128)(2,1)}), bf16[64,1,64]{2,1,0:T(2,128)(2,1)S(1)}, u32[]{:S(2)}, u32[]{:S(2)}) %all-to-all-start.1) | async-done | bytes 8224 | tf_op jit(solution)/shard_map/all_to_all | solution.py:118
  348.5 5.6 %all-to-all-start.2 = ((bf16[1,128,64]{2,0,1:T(2,128)(2,1)}), bf16[1,128,64]{2,0,1:T(2,128)(2,1)S(1)}, u32[]{:S(2)}, u32[]{:S(2)}) async-start(bf16[1,128,64]{2,0,1:T(2,128)(2,1)} %copy.375), calls=%async_computation.2 | async-start | bytes 131072 | tf_op jit(solution)/shard_map/all_to_all | solution.py:103
  354.3 7.0 %all-to-all-done.2 = bf16[1,128,64]{2,0,1:T(2,128)(2,1)S(1)} async-done(((bf16[1,128,64]{2,0,1:T(2,128)(2,1)}), bf16[1,128,64]{2,0,1:T(2,128)(2,1)S(1)}, u32[]{:S(2)}, u32[]{:S(2)}) %all-to-all-start.2) | async-done | bytes 16416 | tf_op jit(solution)/shard_map/all_to_all | solution.py:103
  363.3 4.8 collective-permute-start.27
  372.2 12.2 %all_to_all.16 = bf16[64,2,64]{2,1,0:T(2,128)(2,1)S(1)} all-to-all(bf16[64,2,64]{2,1,0:T(2,128)(2,1)S(1)} %copy.378), channel_id=1, replica_groups=mesh['gx'=16,'gy'=4,'gz'=4] {'gx','gy'}, dimensions={0} | all-to-all | bytes 32768 | tf_op jit(solution)/shard_map/all_to_all | solution.py:118
  386.6 4.5 collective-permute-start.29
  397.9 4.2 collective-permute-done.30
  402.2 4.1 collective-permute-done.31
  410.0 4.3 collective-permute-start.32
  427.0 4.5 collective-permute-start.35
  441.1 5.6 %collective-permute-done.36 = bf16[96,6,1,256]{0,3,2,1:T(8,128)(2,1)S(1)} collective-permute-done((bf16[96,6,1,256]{0,3,2,1:T(8,128)(2,1)S(1)}, bf16[96,6,1,256]{0,3,2,1:T(8,128)(2,1)S(1)}, u32[]{:S(2)}, u32[]{:S(2)}) %collective-permute-start.36) | collective-permute-done | bytes 294944 | tf_op jit(solution)/shard_map/ppermute | solution.py:15
  446.7 4.3 collective-permute-done.37
  451.1 5.5 %collective-permute-start.38 = (bf16[96,6,6,1]{0,3,2,1:T(2,128)(2,1)S(1)}, bf16[96,6,6,1]{0,3,2,1:T(2,128)(2,1)S(1)}, u32[]{:S(2)}, u32[]{:S(2)}) collective-permute-start(bf16[96,6,6,1]{0,3,2,1:T(2,128)(2,1)S(1)} %get-tuple-element.7), channel_id=1, source_target_pairs={{0,1},{1,2},{2,3},{4,5},{5,6},{6,7},{8,9},{9,10},{10,11},{12,13},{... | collective-permute-start | bytes 20744 | tf_op jit(solution)/shard_map/ppermute | solution.py:15
  464.4 4.2 maximum_maximum_fusion
  (573 shorter events, 289.7 us)
Async XLA Ops:
  11.1 8.5 %collective-permute-start.2 = (bf16[32,6,1,256]{3,2,1,0:T(2,128)(2,1)S(1)}, bf16[32,6,1,256]{3,2,1,0:T(2,128)(2,1)S(1)}, u32[]{:S(2)}, u32[]{:S(2)}) collective-permute-start(bf16[32,6,1,256]{3,2,1,0:T(2,128)(2,1)S(1)} %get-tuple-element.157), channel_id=1, source_target_pairs={{0,4},{4,8},{8,12},{1,5},{5,9},{9,13},{2,6},{6,10},{10,14},{3,7},{... | collective-permute-start | bytes 294920 | tf_op jit(solution)/shard_map/ppermute | solution.py:15
  14.5 9.6 %collective-permute-start.3 = (bf16[32,6,1,256]{3,2,1,0:T(2,128)(2,1)S(1)}, bf16[32,6,1,256]{3,2,1,0:T(2,128)(2,1)S(1)}, u32[]{:S(2)}, u32[]{:S(2)}) collective-permute-start(bf16[32,6,1,256]{3,2,1,0:T(2,128)(2,1)S(1)} %get-tuple-element.158), channel_id=1, source_target_pairs={{4,0},{8,4},{12,8},{5,1},{9,5},{13,9},{6,2},{10,6},{14,10},{7,3},{... | collective-permute-start | bytes 294920 | tf_op jit(solution)/shard_map/ppermute | solution.py:17
  25.9 23.8 %collective-permute-start.5 = (bf16[32,6,6,1]{3,2,1,0:T(8,128)(2,1)}, bf16[32,6,6,1]{3,2,1,0:T(8,128)(2,1)}, u32[]{:S(2)}, u32[]{:S(2)}) collective-permute-start(bf16[32,6,6,1]{3,2,1,0:T(8,128)(2,1)} %get-tuple-element.111), channel_id=1, source_target_pairs={{1,0},{2,1},{3,2},{5,4},{6,5},{7,6},{9,8},{10,9},{11,10},{13,12},{... | collective-permute-start | bytes 6920 | tf_op jit(solution)/shard_map/ppermute | solution.py:17
  27.8 22.5 %collective-permute-start.4 = (bf16[32,6,6,1]{3,2,1,0:T(8,128)(2,1)}, bf16[32,6,6,1]{3,2,1,0:T(8,128)(2,1)}, u32[]{:S(2)}, u32[]{:S(2)}) collective-permute-start(bf16[32,6,6,1]{3,2,1,0:T(8,128)(2,1)} %get-tuple-element.112), channel_id=1, source_target_pairs={{0,1},{1,2},{2,3},{4,5},{5,6},{6,7},{8,9},{9,10},{10,11},{12,13},{... | collective-permute-start | bytes 6920 | tf_op jit(solution)/shard_map/ppermute | solution.py:15
  97.3 6.7 %collective-permute-start.6 = (bf16[32,1,4,256]{3,2,1,0:T(4,128)(2,1)S(1)}, bf16[32,1,4,256]{3,2,1,0:T(4,128)(2,1)S(1)}, u32[]{:S(2)}, u32[]{:S(2)}) collective-permute-start(bf16[32,1,4,256]{3,2,1,0:T(4,128)(2,1)S(1)} %get-tuple-element.193), channel_id=1, source_target_pairs={{0,16},{16,32},{32,48},{48,64},{64,80},{80,96},{96,112},{112,128},... | collective-permute-start | bytes 196616 | tf_op jit(solution)/shard_map/ppermute | solution.py:15
  106.6 8.1 %collective-permute-start.8 = (bf16[32,6,1,256]{3,2,1,0:T(2,128)(2,1)S(1)}, bf16[32,6,1,256]{3,2,1,0:T(2,128)(2,1)S(1)}, u32[]{:S(2)}, u32[]{:S(2)}) collective-permute-start(bf16[32,6,1,256]{3,2,1,0:T(2,128)(2,1)S(1)} %get-tuple-element.152), channel_id=1, source_target_pairs={{0,4},{4,8},{8,12},{1,5},{5,9},{9,13},{2,6},{6,10},{10,14},{3,7},{... | collective-permute-start | bytes 294920 | tf_op jit(solution)/shard_map/ppermute | solution.py:15
  110.0 8.8 %collective-permute-start.9 = (bf16[32,6,1,256]{3,2,1,0:T(2,128)(2,1)S(1)}, bf16[32,6,1,256]{3,2,1,0:T(2,128)(2,1)S(1)}, u32[]{:S(2)}, u32[]{:S(2)}) collective-permute-start(bf16[32,6,1,256]{3,2,1,0:T(2,128)(2,1)S(1)} %get-tuple-element.153), channel_id=1, source_target_pairs={{4,0},{8,4},{12,8},{5,1},{9,5},{13,9},{6,2},{10,6},{14,10},{7,3},{... | collective-permute-start | bytes 294920 | tf_op jit(solution)/shard_map/ppermute | solution.py:17
  120.5 20.8 %collective-permute-start.10 = (bf16[32,6,6,1]{3,2,1,0:T(8,128)(2,1)}, bf16[32,6,6,1]{3,2,1,0:T(8,128)(2,1)}, u32[]{:S(2)}, u32[]{:S(2)}) collective-permute-start(bf16[32,6,6,1]{3,2,1,0:T(8,128)(2,1)} %get-tuple-element.107), channel_id=1, source_target_pairs={{0,1},{1,2},{2,3},{4,5},{5,6},{6,7},{8,9},{9,10},{10,11},{12,13},{... | collective-permute-start | bytes 6920 | tf_op jit(solution)/shard_map/ppermute | solution.py:15
  126.1 21.8 %collective-permute-start.11 = (bf16[32,6,6,1]{3,2,1,0:T(8,128)(2,1)}, bf16[32,6,6,1]{3,2,1,0:T(8,128)(2,1)}, u32[]{:S(2)}, u32[]{:S(2)}) collective-permute-start(bf16[32,6,6,1]{3,2,1,0:T(8,128)(2,1)} %get-tuple-element.108), channel_id=1, source_target_pairs={{1,0},{2,1},{3,2},{5,4},{6,5},{7,6},{9,8},{10,9},{11,10},{13,12},{... | collective-permute-start | bytes 6920 | tf_op jit(solution)/shard_map/ppermute | solution.py:17
  221.4 7.9 %collective-permute-start.16 = (bf16[32,4,4,1]{3,0,2,1:T(8,128)(2,1)S(1)}, bf16[32,4,4,1]{3,0,2,1:T(8,128)(2,1)S(1)}, u32[]{:S(2)}, u32[]{:S(2)}) collective-permute-start(bf16[32,4,4,1]{3,0,2,1:T(8,128)(2,1)S(1)} %get-tuple-element.206), channel_id=1, source_target_pairs={{0,1},{1,2},{2,3},{4,5},{5,6},{6,7},{8,9},{9,10},{10,11},{12,13},{... | collective-permute-start | bytes 3080 | tf_op jit(solution)/shard_map/ppermute | solution.py:15
  224.7 9.6 %collective-permute-start.17 = (bf16[32,4,4,1]{3,0,2,1:T(8,128)(2,1)S(1)}, bf16[32,4,4,1]{3,0,2,1:T(8,128)(2,1)S(1)}, u32[]{:S(2)}, u32[]{:S(2)}) collective-permute-start(bf16[32,4,4,1]{3,0,2,1:T(8,128)(2,1)S(1)} %get-tuple-element.207), channel_id=1, source_target_pairs={{1,0},{2,1},{3,2},{5,4},{6,5},{7,6},{9,8},{10,9},{11,10},{13,12},{... | collective-permute-start | bytes 3080 | tf_op jit(solution)/shard_map/ppermute | solution.py:17
  251.4 7.1 %collective-permute-start.21 = (bf16[64,4,1,128]{3,2,1,0:T(2,128)(2,1)S(1)}, bf16[64,4,1,128]{3,2,1,0:T(2,128)(2,1)S(1)}, u32[]{:S(2)}, u32[]{:S(2)}) collective-permute-start(bf16[64,4,1,128]{3,2,1,0:T(2,128)(2,1)S(1)} %get-tuple-element.203), channel_id=1, source_target_pairs={{4,0},{8,4},{12,8},{5,1},{9,5},{13,9},{6,2},{10,6},{14,10},{7,3},{... | collective-permute-start | bytes 196616 | tf_op jit(solution)/shard_map/ppermute | solution.py:17
  259.8 11.0 %collective-permute-start.22 = (bf16[64,4,4,1]{3,2,1,0:T(4,128)(2,1)}, bf16[64,4,4,1]{3,2,1,0:T(4,128)(2,1)S(1)}, u32[]{:S(2)}, u32[]{:S(2)}) collective-permute-start(bf16[64,4,4,1]{3,2,1,0:T(4,128)(2,1)} %get-tuple-element.169), channel_id=1, source_target_pairs={{0,1},{1,2},{2,3},{4,5},{5,6},{6,7},{8,9},{9,10},{10,11},{12,13},{... | collective-permute-start | bytes 6152 | tf_op jit(solution)/shard_map/ppermute | solution.py:15
  261.9 16.8 %collective-permute-start.23 = (bf16[64,4,4,1]{3,2,1,0:T(4,128)(2,1)S(1)}, bf16[64,4,4,1]{3,2,1,0:T(4,128)(2,1)S(1)}, u32[]{:S(2)}, u32[]{:S(2)}) collective-permute-start(bf16[64,4,4,1]{3,2,1,0:T(4,128)(2,1)S(1)} %get-tuple-element.170), channel_id=1, source_target_pairs={{1,0},{2,1},{3,2},{5,4},{6,5},{7,6},{9,8},{10,9},{11,10},{13,12},{... | collective-permute-start | bytes 6152 | tf_op jit(solution)/shard_map/ppermute | solution.py:17
  298.9 22.3 %all-to-all-start = ((bf16[1,64,64]{2,0,1:T(2,128)(2,1)}), bf16[1,64,64]{2,0,1:T(2,128)(2,1)S(1)}, u32[]{:S(2)}, u32[]{:S(2)}) async-start(bf16[1,64,64]{2,0,1:T(2,128)(2,1)} %copy.373), calls=%async_computation | async-start | bytes 65536 | tf_op jit(solution)/shard_map/all_to_all | solution.py:103
  321.3 7.4 %collective-permute-start.24 = (bf16[1,16,4,1]{3,2,1,0:T(4,128)(2,1)S(1)}, bf16[1,16,4,1]{3,2,1,0:T(4,128)(2,1)S(1)}, u32[]{:S(2)}, u32[]{:S(2)}) collective-permute-start(bf16[1,16,4,1]{3,2,1,0:T(4,128)(2,1)S(1)} %get-tuple-element.229), channel_id=1, source_target_pairs={{0,1},{1,2},{2,3},{4,5},{5,6},{6,7},{8,9},{9,10},{10,11},{12,13},{... | collective-permute-start | bytes 392 | tf_op jit(solution)/shard_map/ppermute | solution.py:15
  323.2 7.8 %collective-permute-start.25 = (bf16[1,16,4,1]{3,2,1,0:T(4,128)(2,1)S(1)}, bf16[1,16,4,1]{3,2,1,0:T(4,128)(2,1)S(1)}, u32[]{:S(2)}, u32[]{:S(2)}) collective-permute-start(bf16[1,16,4,1]{3,2,1,0:T(4,128)(2,1)S(1)} %get-tuple-element.230), channel_id=1, source_target_pairs={{1,0},{2,1},{3,2},{5,4},{6,5},{7,6},{9,8},{10,9},{11,10},{13,12},{... | collective-permute-start | bytes 392 | tf_op jit(solution)/shard_map/ppermute | solution.py:17
  332.2 15.4 %all-to-all-start.1 = ((bf16[64,1,64]{2,1,0:T(2,128)(2,1)}), bf16[64,1,64]{2,1,0:T(2,128)(2,1)S(1)}, u32[]{:S(2)}, u32[]{:S(2)}) async-start(bf16[64,1,64]{2,1,0:T(2,128)(2,1)} %copy.374), calls=%async_computation.1 | async-start | bytes 65536 | tf_op jit(solution)/shard_map/all_to_all | solution.py:118
  348.5 12.7 %all-to-all-start.2 = ((bf16[1,128,64]{2,0,1:T(2,128)(2,1)}), bf16[1,128,64]{2,0,1:T(2,128)(2,1)S(1)}, u32[]{:S(2)}, u32[]{:S(2)}) async-start(bf16[1,128,64]{2,0,1:T(2,128)(2,1)} %copy.375), calls=%async_computation.2 | async-start | bytes 131072 | tf_op jit(solution)/shard_map/all_to_all | solution.py:103
  361.4 6.9 %collective-permute-start.26 = (bf16[2,16,4,1]{3,1,2,0:T(8,128)(2,1)S(1)}, bf16[2,16,4,1]{3,1,2,0:T(8,128)(2,1)S(1)}, u32[]{:S(2)}, u32[]{:S(2)}) collective-permute-start(bf16[2,16,4,1]{3,1,2,0:T(8,128)(2,1)S(1)} %get-tuple-element.225), channel_id=1, source_target_pairs={{0,1},{1,2},{2,3},{4,5},{5,6},{6,7},{8,9},{9,10},{10,11},{12,13},{... | collective-permute-start | bytes 776 | tf_op jit(solution)/shard_map/ppermute | solution.py:15
  363.3 8.3 %collective-permute-start.27 = (bf16[2,16,4,1]{3,1,2,0:T(8,128)(2,1)S(1)}, bf16[2,16,4,1]{3,1,2,0:T(8,128)(2,1)S(1)}, u32[]{:S(2)}, u32[]{:S(2)}) collective-permute-start(bf16[2,16,4,1]{3,1,2,0:T(8,128)(2,1)S(1)} %get-tuple-element.226), channel_id=1, source_target_pairs={{1,0},{2,1},{3,2},{5,4},{6,5},{7,6},{9,8},{10,9},{11,10},{13,12},{... | collective-permute-start | bytes 776 | tf_op jit(solution)/shard_map/ppermute | solution.py:17
  384.7 7.2 %collective-permute-start.28 = (bf16[192,1,2,128]{0,3,2,1:T(8,128)(2,1)S(1)}, bf16[192,1,2,128]{0,3,2,1:T(8,128)(2,1)S(1)}, u32[]{:S(2)}, u32[]{:S(2)}) collective-permute-start(bf16[192,1,2,128]{0,3,2,1:T(8,128)(2,1)S(1)} %get-tuple-element.161), channel_id=1, source_target_pairs={{0,16},{16,32},{32,48},{48,64},{64,80},{80,96},{96,112},{112,128},... | collective-permute-start | bytes 294920 | tf_op jit(solution)/shard_map/ppermute | solution.py:15
  386.6 7.0 %collective-permute-start.29 = (bf16[192,1,2,128]{0,3,2,1:T(8,128)(2,1)S(1)}, bf16[192,1,2,128]{0,3,2,1:T(8,128)(2,1)S(1)}, u32[]{:S(2)}, u32[]{:S(2)}) collective-permute-start(bf16[192,1,2,128]{0,3,2,1:T(8,128)(2,1)S(1)} %get-tuple-element.162), channel_id=1, source_target_pairs={{16,0},{32,16},{48,32},{64,48},{80,64},{96,80},{112,96},{128,112},... | collective-permute-start | bytes 294920 | tf_op jit(solution)/shard_map/ppermute | solution.py:17
  393.8 8.3 %collective-permute-start.30 = (bf16[192,4,1,128]{0,3,2,1:T(8,128)(2,1)S(1)}, bf16[192,4,1,128]{0,3,2,1:T(8,128)(2,1)S(1)}, u32[]{:S(2)}, u32[]{:S(2)}) collective-permute-start(bf16[192,4,1,128]{0,3,2,1:T(8,128)(2,1)S(1)} %get-tuple-element.127), channel_id=1, source_target_pairs={{0,4},{4,8},{8,12},{1,5},{5,9},{9,13},{2,6},{6,10},{10,14},{3,7},{... | collective-permute-start | bytes 589832 | tf_op jit(solution)/shard_map/ppermute | solution.py:15
  396.3 10.0 %collective-permute-start.31 = (bf16[192,4,1,128]{0,3,2,1:T(8,128)(2,1)S(1)}, bf16[192,4,1,128]{0,3,2,1:T(8,128)(2,1)S(1)}, u32[]{:S(2)}, u32[]{:S(2)}) collective-permute-start(bf16[192,4,1,128]{0,3,2,1:T(8,128)(2,1)S(1)} %get-tuple-element.128), channel_id=1, source_target_pairs={{4,0},{8,4},{12,8},{5,1},{9,5},{13,9},{6,2},{10,6},{14,10},{7,3},{... | collective-permute-start | bytes 589832 | tf_op jit(solution)/shard_map/ppermute | solution.py:17
  406.4 8.6 %collective-permute-start.33 = (bf16[192,4,4,1]{0,2,3,1:T(4,128)(2,1)S(1)}, bf16[192,4,4,1]{0,2,3,1:T(4,128)(2,1)S(1)}, u32[]{:S(2)}, u32[]{:S(2)}) collective-permute-start(bf16[192,4,4,1]{0,2,3,1:T(4,128)(2,1)S(1)} %copy.384), channel_id=1, source_target_pairs={{1,0},{2,1},{3,2},{5,4},{6,5},{7,6},{9,8},{10,9},{11,10},{13,12},{... | collective-permute-start | bytes 18440 | tf_op jit(solution)/shard_map/ppermute | solution.py:17
  425.1 9.5 %collective-permute-start.34 = (bf16[96,1,4,256]{0,3,2,1:T(8,128)(2,1)S(1)}, bf16[96,1,4,256]{0,3,2,1:T(8,128)(2,1)S(1)}, u32[]{:S(2)}, u32[]{:S(2)}) collective-permute-start(bf16[96,1,4,256]{0,3,2,1:T(8,128)(2,1)S(1)} %get-tuple-element.33), channel_id=1, source_target_pairs={{0,16},{16,32},{32,48},{48,64},{64,80},{80,96},{96,112},{112,128},... | collective-permute-start | bytes 589832 | tf_op jit(solution)/shard_map/ppermute | solution.py:15
  427.0 8.4 %collective-permute-start.35 = (bf16[96,1,4,256]{0,3,2,1:T(8,128)(2,1)S(1)}, bf16[96,1,4,256]{0,3,2,1:T(8,128)(2,1)S(1)}, u32[]{:S(2)}, u32[]{:S(2)}) collective-permute-start(bf16[96,1,4,256]{0,3,2,1:T(8,128)(2,1)S(1)} %get-tuple-element.34), channel_id=1, source_target_pairs={{16,0},{32,16},{48,32},{64,48},{80,64},{96,80},{112,96},{128,112},... | collective-permute-start | bytes 589832 | tf_op jit(solution)/shard_map/ppermute | solution.py:17
  435.8 10.9 %collective-permute-start.36 = (bf16[96,6,1,256]{0,3,2,1:T(8,128)(2,1)S(1)}, bf16[96,6,1,256]{0,3,2,1:T(8,128)(2,1)S(1)}, u32[]{:S(2)}, u32[]{:S(2)}) collective-permute-start(bf16[96,6,1,256]{0,3,2,1:T(8,128)(2,1)S(1)} %get-tuple-element.11), channel_id=1, source_target_pairs={{0,4},{4,8},{8,12},{1,5},{5,9},{9,13},{2,6},{6,10},{10,14},{3,7},{... | collective-permute-start | bytes 884744 | tf_op jit(solution)/shard_map/ppermute | solution.py:15
  438.3 12.6 %collective-permute-start.37 = (bf16[96,6,1,256]{0,3,2,1:T(8,128)(2,1)S(1)}, bf16[96,6,1,256]{0,3,2,1:T(8,128)(2,1)S(1)}, u32[]{:S(2)}, u32[]{:S(2)}) collective-permute-start(bf16[96,6,1,256]{0,3,2,1:T(8,128)(2,1)S(1)} %get-tuple-element.12), channel_id=1, source_target_pairs={{4,0},{8,4},{12,8},{5,1},{9,5},{13,9},{6,2},{10,6},{14,10},{7,3},{... | collective-permute-start | bytes 884744 | tf_op jit(solution)/shard_map/ppermute | solution.py:17
  451.1 12.3 %collective-permute-start.38 = (bf16[96,6,6,1]{0,3,2,1:T(2,128)(2,1)S(1)}, bf16[96,6,6,1]{0,3,2,1:T(2,128)(2,1)S(1)}, u32[]{:S(2)}, u32[]{:S(2)}) collective-permute-start(bf16[96,6,6,1]{0,3,2,1:T(2,128)(2,1)S(1)} %get-tuple-element.7), channel_id=1, source_target_pairs={{0,1},{1,2},{2,3},{4,5},{5,6},{6,7},{8,9},{9,10},{10,11},{12,13},{... | collective-permute-start | bytes 20744 | tf_op jit(solution)/shard_map/ppermute | solution.py:15
  456.6 7.8 %collective-permute-start.39 = (bf16[96,6,6,1]{0,3,2,1:T(2,128)(2,1)S(1)}, bf16[96,6,6,1]{0,3,2,1:T(2,128)(2,1)S(1)}, u32[]{:S(2)}, u32[]{:S(2)}) collective-permute-start(bf16[96,6,6,1]{0,3,2,1:T(2,128)(2,1)S(1)} %get-tuple-element.8), channel_id=1, source_target_pairs={{1,0},{2,1},{3,2},{5,4},{6,5},{7,6},{9,8},{10,9},{11,10},{13,12},{... | collective-permute-start | bytes 20744 | tf_op jit(solution)/shard_map/ppermute | solution.py:17
  (72 other events, 884.9 us)
where the time goes:
time: 496 us; the launch traced here: 486 us
  starting transfers between devices  141 us (28%)
  waiting for transfers between devices  106 us (21%)
  local copies, waits for them, and re-layouts  104 us (21%)
  matrix products  71.7 us (14%)
  other arithmetic  30.6 us (6%)
  between operations  20 us (4%)
  blocking collectives  12.2 us (2%)
    dot_general x162, matrix products, convolve(): jnp.dot(columns, piece, preferred_element_type=jnp.float32)  71.3 us
    ppermute x20, waiting for transfers between devices, padded_2(): lax.ppermute(head, axis, [((i + 1) % count, i) for i in range(ends)])  70.4 us
    reshape x105, local copies, waits for them, and re-layouts, convolve(): piece = padded[:, offset_x:offset_x + size_x, offset_y:offset_y + size_y,...  69.7 us
    ppermute x20, starting transfers between devices, padded_2(): lax.ppermute(head, axis, [((i + 1) % count, i) for i in range(ends)])  63.2 us
    ppermute x20, starting transfers between devices, padded_2(): lax.ppermute(tail, axis, [(i, (i + 1) % count) for i in range(ends)])  59.5 us
    concatenate x25, other arithmetic, padded_2(): jnp.concatenate([lax.ppermute(tail, axis, [(i, (i + 1) % count) for i in...  25.9 us
    ppermute x20, waiting for transfers between devices, padded_2(): lax.ppermute(tail, axis, [(i, (i + 1) % count) for i in range(ends)])  21.8 us
    slice x43, local copies, waits for them, and re-layouts, convolve(): padded[:, offset_x:offset_x + size_x, offset_y:offset_y + size_y, offset_...  19 us
  transfers between devices with their start and end apart: 43, of which 34 were waited for; matrix products, arithmetic and copies ran while one was open for 7% of the time, Pallas kernels for 0%

commit v1 on v0

v1 whole, which is shorter than its diff:
```python
import jax
import jax.numpy as jnp
from jax import lax
from jax.experimental import pallas as pl
from jax.experimental.pallas import tpu as pltpu
from jax.sharding import PartitionSpec as P

BF = jnp.bfloat16
F32 = jnp.float32
PLANE = ("gx", "gy")
EVERY = ("gx", "gy", "gz")
VMEM_LIMIT = 60 * 1024 * 1024


def device_at(q, r, k):
    return ((q * 4 + r // 4) * 4 + r % 4) * 4 + k


def neighbour_pairs(step_x, step_z):
    pairs = []
    for q in range(4):
        for s in range(64):
            to_q, to_s = q + step_x, s + step_z
            if 0 <= to_q < 4 and 0 <= to_s < 64:
                pairs.append((device_at(q, s % 16, s // 16), device_at(to_q, to_s % 16, to_s // 16)))
    return pairs


GROUPS = [list(range(16 * q, 16 * q + 16)) for q in range(4)]
STEPS = [(-1, 0), (1, 0), (0, -1), (0, 1), (-1, -1), (-1, 1), (1, -1), (1, 1)]


def position():
    gx, gy, gz = lax.axis_index("gx"), lax.axis_index("gy"), lax.axis_index("gz")
    return gx // 4, gz * 16 + (gx % 4) * 4 + gy


def one_hot_order():
    row = lax.broadcasted_iota(jnp.int32, (512, 512), 0)
    lane = lax.broadcasted_iota(jnp.int32, (512, 512), 1)
    target = (row % 16) * 32 + row // 16
    return jnp.where(target == lane, 1.0, 0.0).astype(BF)


def to_rows_kernel(cells_ref, out_ref):
    turned = lax.dot_general(
        cells_ref[...], one_hot_order(), (((0,), (0,)), ((), ())), preferred_element_type=F32
    ).astype(BF)
    for slab in range(16):
        for x in range(4):
            out_ref[slab, x] = turned[16 * slab : 16 * slab + 16, 128 * x : 128 * x + 128]


def from_rows_kernel(rows_ref, out_ref):
    columns = [rows_ref[:, x].reshape(256, 128) for x in range(4)]
    turned = jnp.concatenate(columns, axis=1)
    out_ref[...] = lax.dot_general(
        one_hot_order(), turned, (((1,), (1,)), ((), ())), preferred_element_type=F32
    ).astype(BF)


def band(spread, out_ref, stride, first, used, lanes_in, lanes_out, grown):
    out_pos = lax.broadcasted_iota(jnp.int32, (used, 256), 1) // lanes_out
    base = 128 // lanes_in
    for dx in range(3):
        for dz in range(3):
            parts = []
            for dy in range(3):
                start = ((dx * 3 + dy) * 3 + dz) * stride + first
                parts.append(spread[start : start + used, :])
            for at in range(512 // lanes_in):
                rel = at - base
                if grown:
                    gap = out_pos - 2 * rel
                    block = jnp.where(
                        gap == -1,
                        parts[2],
                        jnp.where(
                            gap == 0,
                            parts[1] + parts[2],
                            jnp.where(
                                gap == 1, parts[0] + parts[1], jnp.where(gap == 2, parts[0], 0.0)
                            ),
                        ),
                    )
                    live = -1 <= rel and 2 * rel <= 256 // lanes_out
                else:
                    gap = rel - out_pos
                    block = jnp.where(
                        gap == -1,
                        parts[0],
                        jnp.where(gap == 0, parts[1], jnp.where(gap == 1, parts[2], 0.0)),
                    )
                    live = -1 <= rel <= 256 // lanes_out
                tap = dx * 3 + dz
                if not live:
                    block = jnp.zeros_like(block)
                out_ref[tap, at * lanes_in : at * lanes_in + used, :] = block.astype(BF)
                if used < lanes_in:
                    out_ref[tap, at * lanes_in + used : (at + 1) * lanes_in, :] = jnp.zeros(
                        (lanes_in - used, 256), BF
                    )


def spread_lanes(weight, lanes_out):
    outs = weight.shape[0]
    row = lax.broadcasted_iota(jnp.int32, (outs, 256), 0)
    lane = lax.broadcasted_iota(jnp.int32, (outs, 256), 1)
    chosen = jnp.where(lane % lanes_out == row, 1.0, 0.0).astype(BF)
    return lax.dot_general(weight, chosen, (((0,), (0,)), ((), ())), preferred_element_type=F32)


def encoder_weights_kernel(w1, w2, w3, w4, o1, o2, o3, o4):
    band(spread_lanes(w1[...], 32), o1, 32, 0, 32, 32, 32, False)
    band(spread_lanes(w2[...], 32), o2, 32, 0, 32, 32, 32, False)
    band(spread_lanes(w3[...], 64), o3, 32, 0, 32, 64, 64, False)
    band(spread_lanes(w4[...], 64), o4, 64, 0, 64, 64, 64, False)


def decoder_weights_kernel(w5, w6, o5u, o5s, o6u, o6s):
    wide = spread_lanes(w5[...], 64)
    band(wide, o5u, 192, 0, 128, 128, 64, True)
    band(wide, o5s, 192, 128, 64, 64, 64, False)
    fine = spread_lanes(w6[...], 32)
    band(fine, o6u, 96, 0, 64, 64, 32, True)
    band(fine, o6s, 96, 64, 32, 32, 32, False)


def convolve(fields, weights, acc_ref, planes, rows):
    taps = [(n, dx, dz) for n in range(len(fields)) for dx in range(3) for dz in range(3)]
    for g in range(2):
        total = None
        for at in range(0, len(taps), 2):
            chunk = taps[at : at + 2]
            left = [
                fields[n][dz, dx : dx + planes, :, 128 * g : 128 * g + 384].reshape(planes * rows, 384)
                for n, dx, dz in chunk
            ]
            right = [
                weights[n][dx * 3 + dz, 128 * (1 - g) : 128 * (1 - g) + 384, :] for n, dx, dz in chunk
            ]
            part = jnp.dot(
                jnp.concatenate(left, axis=1) if len(left) > 1 else left[0],
                jnp.concatenate(right, axis=0) if len(right) > 1 else right[0],
                preferred_element_type=F32,
            )
            total = part if total is None else total + part
        acc_ref[0:planes, 0:rows, 256 * g : 256 * g + 256] = total.reshape(planes, rows, 256)


def row_mask(rows, start, limit):
    at = lax.broadcasted_iota(jnp.int32, (rows, 512), 0) + start
    return (at >= 0) & (at < limit)


def store_turned(dest, plane, value, rows):
    dest[0, plane] = pltpu.roll(value, 1, 0).astype(BF)
    dest[1, plane] = value.astype(BF)
    dest[2, plane] = pltpu.roll(value, rows - 1, 0).astype(BF)


def encoder_kernel(
    own, xd, xu, zd, zu, dd, du, ud, uu, w1, w2, w3, w4,
    skip_out, half_out, field, turned, first, acc, half, mid, pooled,
):
    q, s = position()
    x0, z0 = 16 * q, 16 * s
    for i in range(4):
        for j in range(4):
            lanes = slice(128 * j, 128 * j + 128)
            field[8 + 4 * i : 12 + 4 * i, 8:24, lanes] = own[i, j].astype(F32)
            field[8 + 4 * i : 12 + 4 * i, 0:8, lanes] = zd[i, j].astype(F32)
            field[8 + 4 * i : 12 + 4 * i, 24:32, lanes] = zu[i, j].astype(F32)
    for i in range(2):
        for j in range(4):
            lanes = slice(128 * j, 128 * j + 128)
            low, high = slice(4 * i, 4 * i + 4), slice(24 + 4 * i, 28 + 4 * i)
            field[low, 8:24, lanes] = xd[i, j].astype(F32)
            field[high, 8:24, lanes] = xu[i, j].astype(F32)
            field[low, 0:8, lanes] = dd[i, j].astype(F32)
            field[low, 24:32, lanes] = du[i, j].astype(F32)
            field[high, 0:8, lanes] = ud[i, j].astype(F32)
            field[high, 24:32, lanes] = uu[i, j].astype(F32)

    @pl.loop(0, 28)
    def _(p):
        store_turned(turned, p, field[p + 2], 32)

    convolve([turned], [w1], acc, 26, 32)

    @pl.loop(0, 26)
    def _(p):
        x = x0 - 5 + p
        inside = row_mask(32, z0 - 8, 1024) & (x >= 0) & (x < 64)
        store_turned(first, p, jnp.where(inside, jnp.maximum(acc[p], 0.0), 0.0), 32)

    convolve([first], [w2], acc, 24, 32)

    @pl.loop(0, 12)
    def _(h):
        best = None
        for b in range(2):
            p = 2 * h + b
            x = x0 - 4 + p
            inside = row_mask(32, z0 - 8, 1024) & (x >= 0) & (x < 64)
            value = jnp.where(inside, jnp.maximum(acc[p], 0.0), 0.0)

            @pl.when((p >= 3) & (p < 21))
            def _():
                skip_out[0, p - 3] = pltpu.roll(value, 1, 0)[8:24].astype(BF)
                skip_out[1, p - 3] = value[8:24].astype(BF)
                skip_out[2, p - 3] = pltpu.roll(value, 31, 0)[8:24].astype(BF)

            best = value if best is None else jnp.maximum(best, value)
        best = jnp.maximum(best, pltpu.roll(best, 480, 1))
        for t in range(4):
            pooled[:, :] = best[:, 128 * t : 128 * t + 128]
            piece = jnp.maximum(pooled[pl.ds(0, 16, stride=2), :], pooled[pl.ds(1, 16, stride=2), :])
            half[0, h, :, 128 * t : 128 * t + 128] = pltpu.roll(piece, 1, 0).astype(BF)
            half[1, h, :, 128 * t : 128 * t + 128] = piece.astype(BF)
            half[2, h, :, 128 * t : 128 * t + 128] = pltpu.roll(piece, 15, 0).astype(BF)

    convolve([half], [w3], acc, 10, 16)

    @pl.loop(0, 10)
    def _(p):
        x = 8 * q - 1 + p
        inside = row_mask(16, 8 * s - 4, 512) & (x >= 0) & (x < 32)
        store_turned(mid, p, jnp.where(inside, jnp.maximum(acc[p, 0:16], 0.0), 0.0), 16)

    convolve([mid], [w4], acc, 8, 16)
    half_out[...] = jnp.maximum(acc[0:8, 4:12, :], 0.0).astype(BF)


def depthwise(source, taps, planes, offset):
    sums = []
    for t in range(4):
        total = jnp.zeros((planes, 8, 128), F32)
        for dx in range(3):
            for dy in range(3):
                at = t + dy - 1
                if not 0 <= at < 4:
                    continue
                for dz in range(3):
                    tap = (dx * 3 + dy) * 3 + dz
                    factor = taps[tap : tap + 1, :].reshape(1, 1, 128)
                    total += (
                        source[dx : dx + planes, pl.ds(offset + dz, 8), 128 * at : 128 * at + 128]
                        * factor
                    )
        sums.append(total.reshape(planes * 8, 128).astype(BF))
    return sums


def decoder_kernel(
    own, xd, xu, zd, zu, dd, du, ud, uu, skip, d1, p1, d2, p2, w5u, w5s, w6u, w6s,
    out, whole, sides, pooled, quarter, mixed, grown, ups, acc, tall, fine,
):
    q, s = position()
    blocks = [[dd, xd, du], [zd, own, zu], [ud, xu, uu]]
    for a in range(3):
        for b in range(3):
            whole[8 * a : 8 * a + 8, 8 * b : 8 * b + 8, :] = blocks[a][b][...].astype(F32)

    for p in range(12):
        for dz in range(3):
            sides[dz, p] = whole[p + 6, pl.ds(3 + dz, 16), :].astype(BF)

    quarter[...] = jnp.zeros_like(quarter)

    @pl.loop(0, 10)
    def _(p):
        best = jnp.maximum(whole[2 * p + 2], whole[2 * p + 3])
        best = jnp.maximum(best, pltpu.roll(best, 448, 1))
        for t in range(4):
            pooled[0:24, :] = best[:, 128 * t : 128 * t + 128]
            quarter[p, 0:12, 128 * t : 128 * t + 128] = jnp.maximum(
                pooled[pl.ds(0, 12, stride=2), :], pooled[pl.ds(1, 12, stride=2), :]
            )

    mixed[...] = jnp.zeros_like(mixed)
    spread = depthwise(quarter, d1, 8, 1)
    plane = lax.broadcasted_iota(jnp.int32, (8, 8, 128), 0) + (4 * q - 2)
    row = lax.broadcasted_iota(jnp.int32, (8, 8, 128), 1) + (4 * s - 2)
    inside = (plane >= 0) & (plane < 16) & (row >= 0) & (row < 256)
    for t in range(4):
        value = lax.dot_general(
            spread[t], p1[...], (((1,), (1,)), ((), ())), preferred_element_type=F32
        ).reshape(8, 8, 128)
        value = jnp.where(inside, jnp.maximum(value, 0.0), 0.0)
        mixed[:, 0:8, 128 * t : 128 * t + 128] = value.astype(BF).astype(F32)

    spread = depthwise(mixed, d2, 6, 0)
    plane = lax.broadcasted_iota(jnp.int32, (6, 8, 128), 0) + (4 * q - 1)
    row = lax.broadcasted_iota(jnp.int32, (6, 8, 128), 1) + (4 * s - 1)
    inside = (plane >= 0) & (plane < 16) & (row >= 0) & (row < 256)
    grown[...] = jnp.zeros_like(grown)
    for t in range(4):
        value = lax.dot_general(
            spread[t], p2[...], (((1,), (1,)), ((), ())), preferred_element_type=F32
        ).reshape(6, 8, 128)
        value = jnp.where(inside, jnp.maximum(value, 0.0), 0.0)
        for p in range(6):
            grown[pl.ds(8, 8, stride=2), :] = value[p]
            grown[pl.ds(9, 8, stride=2), :] = value[p]
            for dz in range(3):
                rows = grown[pl.ds(5 + dz, 16), :].astype(BF)
                ups[dz, 2 * p, :, 128 * t : 128 * t + 128] = rows
                ups[dz, 2 * p + 1, :, 128 * t : 128 * t + 128] = rows

    convolve([ups, sides], [w5u, w5s], acc, 10, 16)

    @pl.loop(0, 10)
    def _(p):
        x = 8 * q - 1 + p
        inside = row_mask(16, 8 * s - 4, 512) & (x >= 0) & (x < 32)
        value = jnp.where(inside, jnp.maximum(acc[p], 0.0), 0.0)
        for t in range(4):
            tall[pl.ds(0, 16, stride=2), :] = value[:, 128 * t : 128 * t + 128]
            tall[pl.ds(1, 16, stride=2), :] = value[:, 128 * t : 128 * t + 128]
            for dz in range(3):
                rows = tall[pl.ds(7 + dz, 16), :].astype(BF)

                @pl.when(p > 0)
                def _():
                    fine[dz, 2 * p - 1, :, 128 * t : 128 * t + 128] = rows

                @pl.when(p < 9)
                def _():
                    fine[dz, 2 * p, :, 128 * t : 128 * t + 128] = rows

    convolve([fine, skip], [w6u, w6s], acc, 16, 16)
    for i in range(4):
        for j in range(4):
            out[i, j] = acc[4 * i : 4 * i + 4, :, 128 * j : 128 * j + 128].astype(BF)


def call(kernel, outs, scratch=(), flops=0):
    whole = pl.BlockSpec(memory_space=pltpu.VMEM)

    def run(*args):
        return pl.pallas_call(
            kernel,
            out_shape=outs,
            in_specs=[whole] * len(args),
            out_specs=jax.tree.map(lambda _: whole, outs),
            scratch_shapes=list(scratch),
            compiler_params=pltpu.CompilerParams(vmem_limit_bytes=VMEM_LIMIT),
            cost_estimate=pl.CostEstimate(flops=flops, bytes_accessed=4 << 20, transcendentals=0),
        )(*args)

    return run


def shape(*dims):
    return jax.ShapeDtypeStruct(dims, BF)


def local(
    features, conv_one, conv_two, conv_three, conv_four, depth_one, point_one, depth_two, point_two,
    conv_five, conv_six,
):
    taps_one = jnp.pad(depth_one.astype(F32).T, ((0, 5), (0, 64)))
    taps_two = jnp.pad(depth_two.astype(F32).T, ((0, 5), (0, 0)))
    mix_one = jnp.pad(point_one, ((0, 0), (0, 64)))
    bands = shape(9, 512, 256)

    rows = call(to_rows_kernel, shape(16, 4, 16, 128))(features.reshape(512, 256))
    own = lax.all_to_all(rows, PLANE, 0, 0, tiled=True, axis_index_groups=GROUPS)
    own = own.reshape(4, 4, 4, 16, 128)
    cut_x = {-1: slice(0, 2), 0: slice(0, 4), 1: slice(2, 4)}
    cut_z = {-1: slice(0, 8), 0: slice(0, 16), 1: slice(8, 16)}
    got = {}
    for a, b in STEPS:
        piece = own[cut_x[a], :, :, cut_z[b], :]
        got[(-a, -b)] = lax.ppermute(piece, EVERY, neighbour_pairs(a, b))
    w1, w2, w3, w4 = call(encoder_weights_kernel, (bands,) * 4)(
        conv_one, conv_two, conv_three, conv_four
    )
    skip, half_skip = call(
        encoder_kernel,
        (shape(3, 18, 16, 512), shape(8, 8, 512)),
        [
            pltpu.VMEM((32, 32, 512), F32),
            pltpu.VMEM((3, 28, 32, 512), BF),
            pltpu.VMEM((3, 26, 32, 512), BF),
            pltpu.VMEM((26, 32, 512), F32),
            pltpu.VMEM((3, 12, 16, 512), BF),
            pltpu.VMEM((3, 10, 16, 512), BF),
            pltpu.VMEM((32, 128), F32),
        ],
        flops=6 << 30,
    )(own, *[got[step] for step in STEPS], w1, w2, w3, w4)
    around = {}
    for a, b in STEPS:
        around[(-a, -b)] = lax.ppermute(half_skip, EVERY, neighbour_pairs(a, b))
    w5u, w5s, w6u, w6s = call(decoder_weights_kernel, (bands,) * 4)(conv_five, conv_six)
    rows = call(
        decoder_kernel,
        shape(4, 4, 4, 16, 128),
        [
            pltpu.VMEM((24, 24, 512), F32),
            pltpu.VMEM((3, 12, 16, 512), BF),
            pltpu.VMEM((32, 128), F32),
            pltpu.VMEM((10, 16, 512), F32),
            pltpu.VMEM((8, 16, 512), F32),
            pltpu.VMEM((32, 128), F32),
            pltpu.VMEM((3, 12, 16, 512), BF),
            pltpu.VMEM((16, 16, 512), F32),
            pltpu.VMEM((32, 128), F32),
            pltpu.VMEM((3, 18, 16, 512), BF),
        ],
        flops=2 << 30,
    )(
        half_skip, *[around[step] for step in STEPS], skip,
        taps_one, mix_one, taps_two, point_two, w5u, w5s, w6u, w6s,
    )
    back = lax.all_to_all(
        rows.reshape(16, 4, 16, 128), PLANE, 0, 0, tiled=True, axis_index_groups=GROUPS
    )
    return call(from_rows_kernel, shape(512, 256))(back).reshape(32, 4, 4, 256)


def solution(mesh):
    in_specs = (P(None, "gx", "gy", "gz"), P(), P(), P(), P(), P(), P(), P(), P(), P(), P())
    out_specs = P(None, "gx", "gy", "gz")
    return jax.shard_map(local, mesh=mesh, in_specs=in_specs, out_specs=out_specs, check_vma=False)
```

time: 496 us -> 144 us (0.29)
  the two profiles are of different devices: /device:TPU:72 before, /device:TPU:137 now
where the time goes in v1:
time: 144 us
  starting transfers between devices  54.4 us (38%)
  Pallas kernels  44.3 us (31%)
  blocking collectives  35.4 us (25%)
  local copies, waits for them, and re-layouts  5.65 us (4%)
  waiting for transfers between devices  2.74 us (2%)
    pallas_call x6, Pallas kernels, run(): pl.pallas_call(kernel, out_shape=outs, in_specs=[whole] * len(args), out_...  44.3 us
    ppermute x8, starting transfers between devices, local(): around[-a, -b] = lax.ppermute(half_skip, EVERY, neighbour_pairs(a, b))  28.5 us
    ppermute x8, starting transfers between devices, local(): got[-a, -b] = lax.ppermute(piece, EVERY, neighbour_pairs(a, b))  26 us
    all_to_all x1, blocking collectives, local(): lax.all_to_all(rows.reshape(16, 4, 16, 128), PLANE, 0, 0, tiled=True, axi...  22.5 us
    all_to_all x1, blocking collectives, local(): lax.all_to_all(rows, PLANE, 0, 0, tiled=True, axis_index_groups=GROUPS)  12.9 us
  transfers between devices with their start and end apart: 16, of which 1 were waited for; matrix products, arithmetic and copies ran while one was open for 1% of the time, Pallas kernels for 9%

profile of v1, /device:TPU:137, one launch (start us, length us, event | category | flops | bytes accessed | tf_op | source)
XLA Modules:
  0.0 143.6 jit_solution(11155431057741131646)
XLA Ops:
  0.0 1.7 %reshape.14.cells_ref = bf16[512,256]{1,0:T(8,128)(2,1)} reshape(bf16[32,4,4,256]{3,2,1,0:T(4,128)(2,1)} %param.11) | data formatting | bytes 524288 | tf_op jit(solution)/shard_map/reshape | solution.py:368
  1.7 2.0 %shard_map.109 = bf16[16,4,16,128]{3,2,1,0:T(8,128)(2,1)} custom-call(bf16[512,256]{1,0:T(8,128)(2,1)} %reshape.14.cells_ref), custom_call_target="tpu_custom_call" | custom-call | bytes 4194304 | tf_op jit(solution)/shard_map/pallas_call | solution.py:342
  3.7 12.9 %all_to_all.10 = bf16[16,4,16,128]{3,2,1,0:T(8,128)(2,1)S(1)} all-to-all(bf16[16,4,16,128]{3,2,1,0:T(8,128)(2,1)} %shard_map.109), channel_id=1, replica_groups={{0,4,8,12,16,20,24,28,32,36,40,44,48,52,56,60},{64,68,72,76,80,84,88,92..., dimensions={0} | all-to-all | bytes 524288 | tf_op jit(solution)/shard_map/all_to_all | solution.py:369
  16.7 3.0 %collective-permute-start.4 = (bf16[2,4,4,8,128]{4,3,2,1,0:T(8,128)(2,1)S(1)}, bf16[2,4,4,8,128]{4,3,2,1,0:T(8,128)(2,1)S(1)}, u32[]{:S(2)}, u32[]{:S(2)}) collective-permute-start(bf16[2,4,4,8,128]{4,3,2,1,0:T(8,128)(2,1)S(1)} %get-tuple-element.28), channel_id=1, source_target_pairs={{0,68},{4,72},{8,76},{12,80},{16,84},{20,88},{24,92},{28,96},{32,1... | collective-permute-start | bytes 196616 | tf_op jit(solution)/shard_map/ppermute | solution.py:376
  19.7 5.5 %collective-permute-start.5 = (bf16[2,4,4,8,128]{4,3,2,1,0:T(8,128)(2,1)S(1)}, bf16[2,4,4,8,128]{4,3,2,1,0:T(8,128)(2,1)S(1)}, u32[]{:S(2)}, u32[]{:S(2)}) collective-permute-start(bf16[2,4,4,8,128]{4,3,2,1,0:T(8,128)(2,1)S(1)} %get-tuple-element.27), channel_id=1, source_target_pairs={{4,64},{8,68},{12,72},{16,76},{20,80},{24,84},{28,88},{32,92},{36,... | collective-permute-start | bytes 196616 | tf_op jit(solution)/shard_map/ppermute | solution.py:376
  25.2 1.9 %collective-permute-start.6 = (bf16[2,4,4,8,128]{4,3,2,1,0:T(8,128)(2,1)S(1)}, bf16[2,4,4,8,128]{4,3,2,1,0:T(8,128)(2,1)S(1)}, u32[]{:S(2)}, u32[]{:S(2)}) collective-permute-start(bf16[2,4,4,8,128]{4,3,2,1,0:T(8,128)(2,1)S(1)} %get-tuple-element.26), channel_id=1, source_target_pairs={{64,4},{68,8},{72,12},{76,16},{80,20},{84,24},{88,28},{92,32},{96,... | collective-permute-start | bytes 196616 | tf_op jit(solution)/shard_map/ppermute | solution.py:376
  27.1 1.9 %collective-permute-start.2 = (bf16[4,4,4,8,128]{4,3,2,1,0:T(8,128)(2,1)S(1)}, bf16[4,4,4,8,128]{4,3,2,1,0:T(8,128)(2,1)S(1)}, u32[]{:S(2)}, u32[]{:S(2)}) collective-permute-start(bf16[4,4,4,8,128]{4,3,2,1,0:T(8,128)(2,1)S(1)} %get-tuple-element.30), channel_id=1, source_target_pairs={{0,4},{4,8},{8,12},{12,16},{16,20},{20,24},{24,28},{28,32},{32,36}... | collective-permute-start | bytes 393224 | tf_op jit(solution)/shard_map/ppermute | solution.py:376
  29.1 5.0 %collective-permute-start.3 = (bf16[4,4,4,8,128]{4,3,2,1,0:T(8,128)(2,1)S(1)}, bf16[4,4,4,8,128]{4,3,2,1,0:T(8,128)(2,1)S(1)}, u32[]{:S(2)}, u32[]{:S(2)}) collective-permute-start(bf16[4,4,4,8,128]{4,3,2,1,0:T(8,128)(2,1)S(1)} %get-tuple-element.29), channel_id=1, source_target_pairs={{4,0},{8,4},{12,8},{16,12},{20,16},{24,20},{28,24},{32,28},{36,32}... | collective-permute-start | bytes 393224 | tf_op jit(solution)/shard_map/ppermute | solution.py:376
  34.1 2.9 %collective-permute-start = (bf16[2,4,4,16,128]{4,3,2,1,0:T(8,128)(2,1)S(1)}, bf16[2,4,4,16,128]{4,3,2,1,0:T(8,128)(2,1)S(1)}, u32[]{:S(2)}, u32[]{:S(2)}) collective-permute-start(bf16[2,4,4,16,128]{4,3,2,1,0:T(8,128)(2,1)S(1)} %bitcast.11), channel_id=1, source_target_pairs={{0,64},{4,68},{8,72},{12,76},{16,80},{20,84},{24,88},{28,92},{32,9... | collective-permute-start | bytes 393224 | tf_op jit(solution)/shard_map/ppermute | solution.py:376
  37.1 2.4 %collective-permute-start.1 = (bf16[2,4,4,16,128]{4,3,2,1,0:T(8,128)(2,1)S(1)}, bf16[2,4,4,16,128]{4,3,2,1,0:T(8,128)(2,1)S(1)}, u32[]{:S(2)}, u32[]{:S(2)}) collective-permute-start(bf16[2,4,4,16,128]{4,3,2,1,0:T(8,128)(2,1)S(1)} %bitcast.10), channel_id=1, source_target_pairs={{64,0},{68,4},{72,8},{76,12},{80,16},{84,20},{88,24},{92,28},{96,3... | collective-permute-start | bytes 393224 | tf_op jit(solution)/shard_map/ppermute | solution.py:376
  39.5 3.3 %collective-permute-start.7 = (bf16[2,4,4,8,128]{4,3,2,1,0:T(8,128)(2,1)S(1)}, bf16[2,4,4,8,128]{4,3,2,1,0:T(8,128)(2,1)S(1)}, u32[]{:S(2)}, u32[]{:S(2)}) collective-permute-start(bf16[2,4,4,8,128]{4,3,2,1,0:T(8,128)(2,1)S(1)} %get-tuple-element.25), channel_id=1, source_target_pairs={{68,0},{72,4},{76,8},{80,12},{84,16},{88,20},{92,24},{96,28},{100,... | collective-permute-start | bytes 196616 | tf_op jit(solution)/shard_map/ppermute | solution.py:376
  42.8 5.8 %shard_map.110 = (bf16[9,512,256]{2,1,0:T(8,128)(2,1)}, bf16[9,512,256]{2,1,0:T(8,128)(2,1)}, bf16[9,512,256]{2,1,0:T(8,128)(2,1)}, bf16[9,512,256]{2,1,0:T(8,128)(2,1)}) custom-call(bf16[32,864]{1,0:T(8,128)(2,1)} %w1.1, bf16[32,864]{1,0:T(8,128)(2,1)} %w2.1, bf16[64,864]{1,0:T(8,128)(2,1)} %w3.1, bf16[64,1728]{1,0:T(8,128)(2,1)} %w4.1), custom_call_target="tpu_custom_call" | custom-call | bytes 4194304 | tf_op jit(solution)/shard_map/pallas_call | solution.py:342
  48.7 0.5 copy-done.19
  49.4 15.5 %shard_map.111 = (bf16[3,18,16,512]{3,2,1,0:T(8,128)(2,1)}, bf16[8,8,512]{2,1,0:T(8,128)(2,1)}) custom-call(bf16[4,4,4,16,128]{4,3,2,1,0:T(8,128)(2,1)} %bitcast.8, bf16[2,4,4,16,128]{4,3,2,1,0:T(8,128)(2,1)} %copy-done.14, bf16[2,4,4,16,128]{4,3,2,1,0:T(8,128)(2,1)} %copy-done.15, bf16[4,4,4,8,128]{4,3,2,1,0:T(8,128)(2,1)} %copy-done.12, ...), custom_call_target="tpu_custom_call" | custom-call | flops 6442450944 | bytes 4194304 | tf_op jit(solution)/shard_map/pallas_call | solution.py:342
  64.9 1.9 %collective-permute-start.10 = (bf16[8,8,512]{2,1,0:T(8,128)(2,1)}, bf16[8,8,512]{2,1,0:T(8,128)(2,1)S(1)}, u32[]{:S(2)}, u32[]{:S(2)}) collective-permute-start(bf16[8,8,512]{2,1,0:T(8,128)(2,1)} %get-tuple-element.19.own), channel_id=1, source_target_pairs={{0,4},{4,8},{8,12},{12,16},{16,20},{20,24},{24,28},{28,32},{32,36}... | collective-permute-start | bytes 196616 | tf_op jit(solution)/shard_map/ppermute | solution.py:396
  66.9 4.9 %collective-permute-start.11 = (bf16[8,8,512]{2,1,0:T(8,128)(2,1)}, bf16[8,8,512]{2,1,0:T(8,128)(2,1)S(1)}, u32[]{:S(2)}, u32[]{:S(2)}) collective-permute-start(bf16[8,8,512]{2,1,0:T(8,128)(2,1)} %get-tuple-element.19.own), channel_id=1, source_target_pairs={{4,0},{8,4},{12,8},{16,12},{20,16},{24,20},{28,24},{32,28},{36,32}... | collective-permute-start | bytes 196616 | tf_op jit(solution)/shard_map/ppermute | solution.py:396
  71.7 2.5 %collective-permute-start.12 = (bf16[8,8,512]{2,1,0:T(8,128)(2,1)}, bf16[8,8,512]{2,1,0:T(8,128)(2,1)S(1)}, u32[]{:S(2)}, u32[]{:S(2)}) collective-permute-start(bf16[8,8,512]{2,1,0:T(8,128)(2,1)} %get-tuple-element.19.own), channel_id=1, source_target_pairs={{0,68},{4,72},{8,76},{12,80},{16,84},{20,88},{24,92},{28,96},{32,1... | collective-permute-start | bytes 196616 | tf_op jit(solution)/shard_map/ppermute | solution.py:396
  74.3 0.1 copy.12
  74.4 7.5 %shard_map.112 = (bf16[9,512,256]{2,1,0:T(8,128)(2,1)}, bf16[9,512,256]{2,1,0:T(8,128)(2,1)}, bf16[9,512,256]{2,1,0:T(8,128)(2,1)}, bf16[9,512,256]{2,1,0:T(8,128)(2,1)}) custom-call(bf16[64,5184]{1,0:T(8,128)(2,1)} %w5.1, bf16[32,2592]{1,0:T(8,128)(2,1)} %w6.1), custom_call_target="tpu_custom_call" | custom-call | bytes 4194304 | tf_op jit(solution)/shard_map/pallas_call | solution.py:342
  81.9 0.6 pad.18.p1
  82.5 7.0 %collective-permute-start.13 = (bf16[8,8,512]{2,1,0:T(8,128)(2,1)}, bf16[8,8,512]{2,1,0:T(8,128)(2,1)S(1)}, u32[]{:S(2)}, u32[]{:S(2)}) collective-permute-start(bf16[8,8,512]{2,1,0:T(8,128)(2,1)} %get-tuple-element.19.own), channel_id=1, source_target_pairs={{4,64},{8,68},{12,72},{16,76},{20,80},{24,84},{28,88},{32,92},{36,... | collective-permute-start | bytes 196616 | tf_op jit(solution)/shard_map/ppermute | solution.py:396
  89.5 1.9 %collective-permute-start.14 = (bf16[8,8,512]{2,1,0:T(8,128)(2,1)}, bf16[8,8,512]{2,1,0:T(8,128)(2,1)S(1)}, u32[]{:S(2)}, u32[]{:S(2)}) collective-permute-start(bf16[8,8,512]{2,1,0:T(8,128)(2,1)} %get-tuple-element.19.own), channel_id=1, source_target_pairs={{64,4},{68,8},{72,12},{76,16},{80,20},{84,24},{88,28},{92,32},{96,... | collective-permute-start | bytes 196616 | tf_op jit(solution)/shard_map/ppermute | solution.py:396
  91.5 1.9 %collective-permute-start.15 = (bf16[8,8,512]{2,1,0:T(8,128)(2,1)}, bf16[8,8,512]{2,1,0:T(8,128)(2,1)S(1)}, u32[]{:S(2)}, u32[]{:S(2)}) collective-permute-start(bf16[8,8,512]{2,1,0:T(8,128)(2,1)} %get-tuple-element.19.own), channel_id=1, source_target_pairs={{68,0},{72,4},{76,8},{80,12},{84,16},{88,20},{92,24},{96,28},{100,... | collective-permute-start | bytes 196616 | tf_op jit(solution)/shard_map/ppermute | solution.py:396
  93.4 6.2 %collective-permute-start.8 = (bf16[8,8,512]{2,1,0:T(8,128)(2,1)}, bf16[8,8,512]{2,1,0:T(8,128)(2,1)S(1)}, u32[]{:S(2)}, u32[]{:S(2)}) collective-permute-start(bf16[8,8,512]{2,1,0:T(8,128)(2,1)} %get-tuple-element.19.own), channel_id=1, source_target_pairs={{0,64},{4,68},{8,72},{12,76},{16,80},{20,84},{24,88},{28,92},{32,9... | collective-permute-start | bytes 196616 | tf_op jit(solution)/shard_map/ppermute | solution.py:396
  99.7 2.1 %collective-permute-start.9 = (bf16[8,8,512]{2,1,0:T(8,128)(2,1)}, bf16[8,8,512]{2,1,0:T(8,128)(2,1)S(1)}, u32[]{:S(2)}, u32[]{:S(2)}) collective-permute-start(bf16[8,8,512]{2,1,0:T(8,128)(2,1)} %get-tuple-element.19.own), channel_id=1, source_target_pairs={{64,0},{68,4},{72,8},{76,12},{80,16},{84,20},{88,24},{92,28},{96,3... | collective-permute-start | bytes 196616 | tf_op jit(solution)/shard_map/ppermute | solution.py:396
  101.8 0.6 pad_convert_fusion
  102.5 2.7 %collective-permute-done.9.xu = bf16[8,8,512]{2,1,0:T(8,128)(2,1)S(1)} collective-permute-done((bf16[8,8,512]{2,1,0:T(8,128)(2,1)}, bf16[8,8,512]{2,1,0:T(8,128)(2,1)S(1)}, u32[]{:S(2)}, u32[]{:S(2)}) %collective-permute-start.9) | collective-permute-done | bytes 65568 | tf_op jit(solution)/shard_map/ppermute | solution.py:396
  105.2 0.6 copy-done.8
  105.8 11.5 %shard_map.113 = bf16[4,4,4,16,128]{4,3,2,1,0:T(8,128)(2,1)} custom-call(bf16[8,8,512]{2,1,0:T(8,128)(2,1)} %get-tuple-element.19.own, bf16[8,8,512]{2,1,0:T(8,128)(2,1)} %copy-done.7, bf16[8,8,512]{2,1,0:T(8,128)(2,1)} %copy-done.8, bf16[8,8,512]{2,1,0:T(8,128)(2,1)} %copy-done.1, bf16[8,8,512]{2,1,0:T(8,128)(2,1)} %copy-done.2, ...), custom_call_target="tpu_custom_call" | custom-call | flops 2147483648 | bytes 4194304 | tf_op jit(solution)/shard_map/pallas_call | solution.py:342
  117.4 22.5 %all_to_all.11.rows_ref = bf16[16,4,16,128]{3,2,1,0:T(8,128)(2,1)} all-to-all(bf16[16,4,16,128]{3,2,1,0:T(8,128)(2,1)} %bitcast.9), channel_id=1, replica_groups={{0,4,8,12,16,20,24,28,32,36,40,44,48,52,56,60},{64,68,72,76,80,84,88,92..., dimensions={0} | all-to-all | bytes 524288 | tf_op jit(solution)/shard_map/all_to_all | solution.py:418
  139.9 2.0 %shard_map.114 = bf16[512,256]{1,0:T(8,128)(2,1)} custom-call(bf16[16,4,16,128]{3,2,1,0:T(8,128)(2,1)} %all_to_all.11.rows_ref), custom_call_target="tpu_custom_call" | custom-call | bytes 4194304 | tf_op jit(solution)/shard_map/pallas_call | solution.py:342
  141.9 1.7 %reshape.17 = bf16[32,4,4,256]{3,2,1,0:T(4,128)(2,1)} reshape(bf16[512,256]{1,0:T(8,128)(2,1)} %shard_map.114) | data formatting | bytes 524288 | tf_op jit(solution)/shard_map/reshape | solution.py:421
  (56 shorter events, 0.4 us)
Async XLA Ops:
  16.6 32.1 %copy-start = (bf16[16,4,16,128]{3,2,1,0:T(8,128)(2,1)}, bf16[16,4,16,128]{3,2,1,0:T(8,128)(2,1)S(1)}, u32[]{:S(2)}) copy-start(bf16[16,4,16,128]{3,2,1,0:T(8,128)(2,1)S(1)} %all_to_all.10) | copy-start | bytes 786436
  16.7 17.4 %collective-permute-start.4 = (bf16[2,4,4,8,128]{4,3,2,1,0:T(8,128)(2,1)S(1)}, bf16[2,4,4,8,128]{4,3,2,1,0:T(8,128)(2,1)S(1)}, u32[]{:S(2)}, u32[]{:S(2)}) collective-permute-start(bf16[2,4,4,8,128]{4,3,2,1,0:T(8,128)(2,1)S(1)} %get-tuple-element.28), channel_id=1, source_target_pairs={{0,68},{4,72},{8,76},{12,80},{16,84},{20,88},{24,92},{28,96},{32,1... | collective-permute-start | bytes 196616 | tf_op jit(solution)/shard_map/ppermute | solution.py:376
  19.7 17.4 %collective-permute-start.5 = (bf16[2,4,4,8,128]{4,3,2,1,0:T(8,128)(2,1)S(1)}, bf16[2,4,4,8,128]{4,3,2,1,0:T(8,128)(2,1)S(1)}, u32[]{:S(2)}, u32[]{:S(2)}) collective-permute-start(bf16[2,4,4,8,128]{4,3,2,1,0:T(8,128)(2,1)S(1)} %get-tuple-element.27), channel_id=1, source_target_pairs={{4,64},{8,68},{12,72},{16,76},{20,80},{24,84},{28,88},{32,92},{36,... | collective-permute-start | bytes 196616 | tf_op jit(solution)/shard_map/ppermute | solution.py:376
  25.2 14.3 %collective-permute-start.6 = (bf16[2,4,4,8,128]{4,3,2,1,0:T(8,128)(2,1)S(1)}, bf16[2,4,4,8,128]{4,3,2,1,0:T(8,128)(2,1)S(1)}, u32[]{:S(2)}, u32[]{:S(2)}) collective-permute-start(bf16[2,4,4,8,128]{4,3,2,1,0:T(8,128)(2,1)S(1)} %get-tuple-element.26), channel_id=1, source_target_pairs={{64,4},{68,8},{72,12},{76,16},{80,20},{84,24},{88,28},{92,32},{96,... | collective-permute-start | bytes 196616 | tf_op jit(solution)/shard_map/ppermute | solution.py:376
  27.1 21.4 %collective-permute-start.2 = (bf16[4,4,4,8,128]{4,3,2,1,0:T(8,128)(2,1)S(1)}, bf16[4,4,4,8,128]{4,3,2,1,0:T(8,128)(2,1)S(1)}, u32[]{:S(2)}, u32[]{:S(2)}) collective-permute-start(bf16[4,4,4,8,128]{4,3,2,1,0:T(8,128)(2,1)S(1)} %get-tuple-element.30), channel_id=1, source_target_pairs={{0,4},{4,8},{8,12},{12,16},{16,20},{20,24},{24,28},{28,32},{32,36}... | collective-permute-start | bytes 393224 | tf_op jit(solution)/shard_map/ppermute | solution.py:376
  29.1 19.5 %collective-permute-start.3 = (bf16[4,4,4,8,128]{4,3,2,1,0:T(8,128)(2,1)S(1)}, bf16[4,4,4,8,128]{4,3,2,1,0:T(8,128)(2,1)S(1)}, u32[]{:S(2)}, u32[]{:S(2)}) collective-permute-start(bf16[4,4,4,8,128]{4,3,2,1,0:T(8,128)(2,1)S(1)} %get-tuple-element.29), channel_id=1, source_target_pairs={{4,0},{8,4},{12,8},{16,12},{20,16},{24,20},{28,24},{32,28},{36,32}... | collective-permute-start | bytes 393224 | tf_op jit(solution)/shard_map/ppermute | solution.py:376
  34.1 14.5 %copy-start.16 = (bf16[2,4,4,8,128]{4,3,2,1,0:T(8,128)(2,1)}, bf16[2,4,4,8,128]{4,3,2,1,0:T(8,128)(2,1)S(1)}, u32[]{:S(2)}) copy-start(bf16[2,4,4,8,128]{4,3,2,1,0:T(8,128)(2,1)S(1)} %collective-permute-done.4.dd) | copy-start | bytes 196612
  34.1 14.4 %collective-permute-start = (bf16[2,4,4,16,128]{4,3,2,1,0:T(8,128)(2,1)S(1)}, bf16[2,4,4,16,128]{4,3,2,1,0:T(8,128)(2,1)S(1)}, u32[]{:S(2)}, u32[]{:S(2)}) collective-permute-start(bf16[2,4,4,16,128]{4,3,2,1,0:T(8,128)(2,1)S(1)} %bitcast.11), channel_id=1, source_target_pairs={{0,64},{4,68},{8,72},{12,76},{16,80},{20,84},{24,88},{28,92},{32,9... | collective-permute-start | bytes 393224 | tf_op jit(solution)/shard_map/ppermute | solution.py:376
  37.1 11.6 %copy-start.17 = (bf16[2,4,4,8,128]{4,3,2,1,0:T(8,128)(2,1)}, bf16[2,4,4,8,128]{4,3,2,1,0:T(8,128)(2,1)S(1)}, u32[]{:S(2)}) copy-start(bf16[2,4,4,8,128]{4,3,2,1,0:T(8,128)(2,1)S(1)} %collective-permute-done.5.du) | copy-start | bytes 196612
  37.1 11.5 %collective-permute-start.1 = (bf16[2,4,4,16,128]{4,3,2,1,0:T(8,128)(2,1)S(1)}, bf16[2,4,4,16,128]{4,3,2,1,0:T(8,128)(2,1)S(1)}, u32[]{:S(2)}, u32[]{:S(2)}) collective-permute-start(bf16[2,4,4,16,128]{4,3,2,1,0:T(8,128)(2,1)S(1)} %bitcast.10), channel_id=1, source_target_pairs={{64,0},{68,4},{72,8},{76,12},{80,16},{84,20},{88,24},{92,28},{96,3... | collective-permute-start | bytes 393224 | tf_op jit(solution)/shard_map/ppermute | solution.py:376
  39.5 9.2 %copy-start.18 = (bf16[2,4,4,8,128]{4,3,2,1,0:T(8,128)(2,1)}, bf16[2,4,4,8,128]{4,3,2,1,0:T(8,128)(2,1)S(1)}, u32[]{:S(2)}) copy-start(bf16[2,4,4,8,128]{4,3,2,1,0:T(8,128)(2,1)S(1)} %collective-permute-done.6.ud) | copy-start | bytes 196612
  39.5 9.1 %collective-permute-start.7 = (bf16[2,4,4,8,128]{4,3,2,1,0:T(8,128)(2,1)S(1)}, bf16[2,4,4,8,128]{4,3,2,1,0:T(8,128)(2,1)S(1)}, u32[]{:S(2)}, u32[]{:S(2)}) collective-permute-start(bf16[2,4,4,8,128]{4,3,2,1,0:T(8,128)(2,1)S(1)} %get-tuple-element.25), channel_id=1, source_target_pairs={{68,0},{72,4},{76,8},{80,12},{84,16},{88,20},{92,24},{96,28},{100,... | collective-permute-start | bytes 196616 | tf_op jit(solution)/shard_map/ppermute | solution.py:376
  48.6 0.7 copy-start.14
  48.6 0.8 copy-start.15
  49.4 24.8 %copy-start.9 = (bf16[128,64]{0,1:T(8,128)(2,1)S(1)}, bf16[128,64]{0,1:T(8,128)(2,1)}, u32[]{:S(2)}) copy-start(bf16[128,64]{0,1:T(8,128)(2,1)} %param.17) | copy-start | bytes 49156
  49.4 52.4 %copy-start.10 = (bf16[128,27]{0,1:T(8,128)(2,1)S(1)}, bf16[128,27]{0,1:T(8,128)(2,1)}, u32[]{:S(2)}) copy-start(bf16[128,27]{0,1:T(8,128)(2,1)} %param.18) | copy-start | bytes 20740
  49.4 52.4 %copy-start.11 = (bf16[64,27]{0,1:T(8,128)(2,1)S(1)}, bf16[64,27]{0,1:T(8,128)(2,1)}, u32[]{:S(2)}) copy-start(bf16[64,27]{0,1:T(8,128)(2,1)} %param.16) | copy-start | bytes 10372
  64.9 26.5 %collective-permute-start.10 = (bf16[8,8,512]{2,1,0:T(8,128)(2,1)}, bf16[8,8,512]{2,1,0:T(8,128)(2,1)S(1)}, u32[]{:S(2)}, u32[]{:S(2)}) collective-permute-start(bf16[8,8,512]{2,1,0:T(8,128)(2,1)} %get-tuple-element.19.own), channel_id=1, source_target_pairs={{0,4},{4,8},{8,12},{12,16},{16,20},{20,24},{24,28},{28,32},{32,36}... | collective-permute-start | bytes 196616 | tf_op jit(solution)/shard_map/ppermute | solution.py:396
  66.9 26.6 %collective-permute-start.11 = (bf16[8,8,512]{2,1,0:T(8,128)(2,1)}, bf16[8,8,512]{2,1,0:T(8,128)(2,1)S(1)}, u32[]{:S(2)}, u32[]{:S(2)}) collective-permute-start(bf16[8,8,512]{2,1,0:T(8,128)(2,1)} %get-tuple-element.19.own), channel_id=1, source_target_pairs={{4,0},{8,4},{12,8},{16,12},{20,16},{24,20},{28,24},{32,28},{36,32}... | collective-permute-start | bytes 196616 | tf_op jit(solution)/shard_map/ppermute | solution.py:396
  71.7 27.9 %collective-permute-start.12 = (bf16[8,8,512]{2,1,0:T(8,128)(2,1)}, bf16[8,8,512]{2,1,0:T(8,128)(2,1)S(1)}, u32[]{:S(2)}, u32[]{:S(2)}) collective-permute-start(bf16[8,8,512]{2,1,0:T(8,128)(2,1)} %get-tuple-element.19.own), channel_id=1, source_target_pairs={{0,68},{4,72},{8,76},{12,80},{16,84},{20,88},{24,92},{28,96},{32,1... | collective-permute-start | bytes 196616 | tf_op jit(solution)/shard_map/ppermute | solution.py:396
  82.5 19.9 %collective-permute-start.13 = (bf16[8,8,512]{2,1,0:T(8,128)(2,1)}, bf16[8,8,512]{2,1,0:T(8,128)(2,1)S(1)}, u32[]{:S(2)}, u32[]{:S(2)}) collective-permute-start(bf16[8,8,512]{2,1,0:T(8,128)(2,1)} %get-tuple-element.19.own), channel_id=1, source_target_pairs={{4,64},{8,68},{12,72},{16,76},{20,80},{24,84},{28,88},{32,92},{36,... | collective-permute-start | bytes 196616 | tf_op jit(solution)/shard_map/ppermute | solution.py:396
  89.5 12.9 %collective-permute-start.14 = (bf16[8,8,512]{2,1,0:T(8,128)(2,1)}, bf16[8,8,512]{2,1,0:T(8,128)(2,1)S(1)}, u32[]{:S(2)}, u32[]{:S(2)}) collective-permute-start(bf16[8,8,512]{2,1,0:T(8,128)(2,1)} %get-tuple-element.19.own), channel_id=1, source_target_pairs={{64,4},{68,8},{72,12},{76,16},{80,20},{84,24},{88,28},{92,32},{96,... | collective-permute-start | bytes 196616 | tf_op jit(solution)/shard_map/ppermute | solution.py:396
  91.5 13.7 %copy-start.1 = (bf16[8,8,512]{2,1,0:T(8,128)(2,1)}, bf16[8,8,512]{2,1,0:T(8,128)(2,1)S(1)}, u32[]{:S(2)}) copy-start(bf16[8,8,512]{2,1,0:T(8,128)(2,1)S(1)} %collective-permute-done.10.zd) | copy-start | bytes 196612
  91.5 11.0 %collective-permute-start.15 = (bf16[8,8,512]{2,1,0:T(8,128)(2,1)}, bf16[8,8,512]{2,1,0:T(8,128)(2,1)S(1)}, u32[]{:S(2)}, u32[]{:S(2)}) collective-permute-start(bf16[8,8,512]{2,1,0:T(8,128)(2,1)} %get-tuple-element.19.own), channel_id=1, source_target_pairs={{68,0},{72,4},{76,8},{80,12},{84,16},{88,20},{92,24},{96,28},{100,... | collective-permute-start | bytes 196616 | tf_op jit(solution)/shard_map/ppermute | solution.py:396
  93.4 11.8 %copy-start.2 = (bf16[8,8,512]{2,1,0:T(8,128)(2,1)}, bf16[8,8,512]{2,1,0:T(8,128)(2,1)S(1)}, u32[]{:S(2)}) copy-start(bf16[8,8,512]{2,1,0:T(8,128)(2,1)S(1)} %collective-permute-done.11.zu) | copy-start | bytes 196612
  93.4 9.0 %collective-permute-start.8 = (bf16[8,8,512]{2,1,0:T(8,128)(2,1)}, bf16[8,8,512]{2,1,0:T(8,128)(2,1)S(1)}, u32[]{:S(2)}, u32[]{:S(2)}) collective-permute-start(bf16[8,8,512]{2,1,0:T(8,128)(2,1)} %get-tuple-element.19.own), channel_id=1, source_target_pairs={{0,64},{4,68},{8,72},{12,76},{16,80},{20,84},{24,88},{28,92},{32,9... | collective-permute-start | bytes 196616 | tf_op jit(solution)/shard_map/ppermute | solution.py:396
  99.7 5.5 %copy-start.3 = (bf16[8,8,512]{2,1,0:T(8,128)(2,1)}, bf16[8,8,512]{2,1,0:T(8,128)(2,1)S(1)}, u32[]{:S(2)}) copy-start(bf16[8,8,512]{2,1,0:T(8,128)(2,1)S(1)} %collective-permute-done.12.dd) | copy-start | bytes 196612
  99.7 5.5 %collective-permute-start.9 = (bf16[8,8,512]{2,1,0:T(8,128)(2,1)}, bf16[8,8,512]{2,1,0:T(8,128)(2,1)S(1)}, u32[]{:S(2)}, u32[]{:S(2)}) collective-permute-start(bf16[8,8,512]{2,1,0:T(8,128)(2,1)} %get-tuple-element.19.own), channel_id=1, source_target_pairs={{64,0},{68,4},{72,8},{76,12},{80,16},{84,20},{88,24},{92,28},{96,3... | collective-permute-start | bytes 196616 | tf_op jit(solution)/shard_map/ppermute | solution.py:396
  102.4 2.8 %copy-start.4 = (bf16[8,8,512]{2,1,0:T(8,128)(2,1)}, bf16[8,8,512]{2,1,0:T(8,128)(2,1)S(1)}, u32[]{:S(2)}) copy-start(bf16[8,8,512]{2,1,0:T(8,128)(2,1)S(1)} %collective-permute-done.13.du) | copy-start | bytes 196612
  102.4 2.8 %copy-start.5 = (bf16[8,8,512]{2,1,0:T(8,128)(2,1)}, bf16[8,8,512]{2,1,0:T(8,128)(2,1)S(1)}, u32[]{:S(2)}) copy-start(bf16[8,8,512]{2,1,0:T(8,128)(2,1)S(1)} %collective-permute-done.14.ud) | copy-start | bytes 196612
  102.5 2.8 %copy-start.6 = (bf16[8,8,512]{2,1,0:T(8,128)(2,1)}, bf16[8,8,512]{2,1,0:T(8,128)(2,1)S(1)}, u32[]{:S(2)}) copy-start(bf16[8,8,512]{2,1,0:T(8,128)(2,1)S(1)} %collective-permute-done.15.uu) | copy-start | bytes 196612
  102.5 2.8 %copy-start.7 = (bf16[8,8,512]{2,1,0:T(8,128)(2,1)}, bf16[8,8,512]{2,1,0:T(8,128)(2,1)S(1)}, u32[]{:S(2)}) copy-start(bf16[8,8,512]{2,1,0:T(8,128)(2,1)S(1)} %collective-permute-done.8.xd) | copy-start | bytes 196612
  (4 other events, 2.6 us)

commit v2 on v1

--- a/solution.py
+++ b/solution.py
@@ -9,30 +9,40 @@
 F32 = jnp.float32
 PLANE = ("gx", "gy")
 EVERY = ("gx", "gy", "gz")
-VMEM_LIMIT = 60 * 1024 * 1024
-
-
-def device_at(q, r, k):
-    return ((q * 4 + r // 4) * 4 + r % 4) * 4 + k
-
-
-def neighbour_pairs(step_x, step_z):
+LIMITS = (24, 24, 32, 32)
+
+
+def slab_at(z_low, across, core):
+    step = across + z_low * (3 - 2 * across)
+    return 8 * z_low + 2 * step + (core + step) % 2
+
+
+SLABS = [slab_at(rank // 8, rank % 4, rank // 4 % 2) for rank in range(16)]
+
+
+def device_at(q, slab, k):
+    rank = SLABS.index(slab)
+    return ((q * 4 + rank // 4) * 4 + rank % 4) * 4 + k
+
+
+def swap_pairs(step_x, step_z, parity):
     pairs = []
     for q in range(4):
         for s in range(64):
             to_q, to_s = q + step_x, s + step_z
-            if 0 <= to_q < 4 and 0 <= to_s < 64:
-                pairs.append((device_at(q, s % 16, s // 16), device_at(to_q, to_s % 16, to_s // 16)))
+            if (q * step_x + s * step_z) % 2 == parity and to_q < 4 and to_s < 64:
+                here = device_at(q, s % 16, s // 16)
+                there = device_at(to_q, to_s % 16, to_s // 16)
+                pairs += [(here, there), (there, here)]
     return pairs
 
 
 GROUPS = [list(range(16 * q, 16 * q + 16)) for q in range(4)]
-STEPS = [(-1, 0), (1, 0), (0, -1), (0, 1), (-1, -1), (-1, 1), (1, -1), (1, 1)]
 
 
 def position():
     gx, gy, gz = lax.axis_index("gx"), lax.axis_index("gy"), lax.axis_index("gz")
-    return gx // 4, gz * 16 + (gx % 4) * 4 + gy
+    return gx // 4, gz * 16 + slab_at(gx // 2 % 2, gy, gx % 2)
 
 
 def one_hot_order():
@@ -46,13 +56,15 @@
     turned = lax.dot_general(
         cells_ref[...], one_hot_order(), (((0,), (0,)), ((), ())), preferred_element_type=F32
     ).astype(BF)
-    for slab in range(16):
+    for rank, slab in enumerate(SLABS):
         for x in range(4):
-            out_ref[slab, x] = turned[16 * slab : 16 * slab + 16, 128 * x : 128 * x + 128]
+            out_ref[rank, x] = turned[16 * slab : 16 * slab + 16, 128 * x : 128 * x + 128]
 
 
 def from_rows_kernel(rows_ref, out_ref):
-    columns = [rows_ref[:, x].reshape(256, 128) for x in range(4)]
+    columns = [
+        jnp.concatenate([rows_ref[SLABS.index(slab), x] for slab in range(16)], axis=0) for x in range(4)
+    ]
     turned = jnp.concatenate(columns, axis=1)
     out_ref[...] = lax.dot_general(
         one_hot_order(), turned, (((1,), (1,)), ((), ())), preferred_element_type=F32
@@ -60,52 +72,50 @@
 
 
 def band(spread, out_ref, stride, first, used, lanes_in, lanes_out, grown):
-    out_pos = lax.broadcasted_iota(jnp.int32, (used, 256), 1) // lanes_out
+    per_tile = 128 // lanes_out
     base = 128 // lanes_in
+    group = lax.broadcasted_iota(jnp.int32, (used, 128), 1) // lanes_out
+    chosen = [jnp.where(group == j, 1.0, 0.0).astype(BF) for j in range(per_tile)]
+    empty = jnp.zeros((lanes_in, 128), BF)
     for dx in range(3):
         for dz in range(3):
+            tap = dx * 3 + dz
             parts = []
             for dy in range(3):
                 start = ((dx * 3 + dy) * 3 + dz) * stride + first
                 parts.append(spread[start : start + used, :])
+            if grown:
+                pieces = {-1: parts[2], 0: parts[1] + parts[2], 1: parts[0] + parts[1], 2: parts[0]}
+            else:
+                pieces = {1: parts[0], 0: parts[1], -1: parts[2]}
+            pieces = {gap: piece.astype(BF) for gap, piece in pieces.items()}
+            made = {}
             for at in range(512 // lanes_in):
-                rel = at - base
-                if grown:
-                    gap = out_pos - 2 * rel
-                    block = jnp.where(
-                        gap == -1,
-                        parts[2],
-                        jnp.where(
-                            gap == 0,
-                            parts[1] + parts[2],
-                            jnp.where(
-                                gap == 1, parts[0] + parts[1], jnp.where(gap == 2, parts[0], 0.0)
-                            ),
-                        ),
-                    )
-                    live = -1 <= rel and 2 * rel <= 256 // lanes_out
-                else:
-                    gap = rel - out_pos
-                    block = jnp.where(
-                        gap == -1,
-                        parts[0],
-                        jnp.where(gap == 0, parts[1], jnp.where(gap == 1, parts[2], 0.0)),
-                    )
-                    live = -1 <= rel <= 256 // lanes_out
-                tap = dx * 3 + dz
-                if not live:
-                    block = jnp.zeros_like(block)
-                out_ref[tap, at * lanes_in : at * lanes_in + used, :] = block.astype(BF)
-                if used < lanes_in:
-                    out_ref[tap, at * lanes_in + used : (at + 1) * lanes_in, :] = jnp.zeros(
-                        (lanes_in - used, 256), BF
-                    )
+                for tile in range(2):
+                    key = (2 if grown else 1) * (at - base) - per_tile * tile
+                    if key not in made:
+                        block = None
+                        for gap, piece in pieces.items():
+                            if 0 <= key + gap < per_tile:
+                                term = piece * chosen[key + gap]
+                                block = term if block is None else block + term
+                        made[key] = block
+                    block = made[key]
+                    lanes = slice(128 * tile, 128 * tile + 128)
+                    if block is None:
+                        out_ref[tap, at * lanes_in : (at + 1) * lanes_in, lanes] = empty
+                    else:
+                        out_ref[tap, at * lanes_in : at * lanes_in + used, lanes] = block
+                        if used < lanes_in:
+                            out_ref[tap, at * lanes_in + used : (at + 1) * lanes_in, lanes] = empty[
+                                : lanes_in - used
+                            ]
 
 
 def spread_lanes(weight, lanes_out):
     outs = weight.shape[0]
-    row = lax.broadcasted_iota(jnp.int32, (outs, 256), 0)
-    lane = lax.broadcasted_iota(jnp.int32, (outs, 256), 1)
+    row = lax.broadcasted_iota(jnp.int32, (outs, 128), 0)
+    lane = lax.broadcasted_iota(jnp.int32, (outs, 128), 1)
     chosen = jnp.where(lane % lanes_out == row, 1.0, 0.0).astype(BF)
     return lax.dot_general(weight, chosen, (((0,), (0,)), ((), ())), preferred_element_type=F32)
 
@@ -160,27 +170,24 @@
 
 
 def encoder_kernel(
-    own, xd, xu, zd, zu, dd, du, ud, uu, w1, w2, w3, w4,
+    own, x1, x2, z1, z2, w1, w2, w3, w4,
     skip_out, half_out, field, turned, first, acc, half, mid, pooled,
 ):
     q, s = position()
     x0, z0 = 16 * q, 16 * s
-    for i in range(4):
+    plane_1 = 24 * (1 - q % 2)
+    plane_2 = 24 - plane_1
+    row_1 = pl.multiple_of(24 * (1 - s % 2), 8)
+    row_2 = pl.multiple_of(24 * (s % 2), 8)
+    starts = [plane_1, plane_1 + 4, 8, 12, 16, 20, plane_2, plane_2 + 4]
+    for i in range(8):
+        planes = pl.ds(starts[i], 4)
+        source, at = (x1, i) if i < 2 else ((own, i - 2) if i < 6 else (x2, i - 6))
         for j in range(4):
             lanes = slice(128 * j, 128 * j + 128)
-            field[8 + 4 * i : 12 + 4 * i, 8:24, lanes] = own[i, j].astype(F32)
-            field[8 + 4 * i : 12 + 4 * i, 0:8, lanes] = zd[i, j].astype(F32)
-            field[8 + 4 * i : 12 + 4 * i, 24:32, lanes] = zu[i, j].astype(F32)
-    for i in range(2):
-        for j in range(4):
-            lanes = slice(128 * j, 128 * j + 128)
-            low, high = slice(4 * i, 4 * i + 4), slice(24 + 4 * i, 28 + 4 * i)
-            field[low, 8:24, lanes] = xd[i, j].astype(F32)
-            field[high, 8:24, lanes] = xu[i, j].astype(F32)
-            field[low, 0:8, lanes] = dd[i, j].astype(F32)
-            field[low, 24:32, lanes] = du[i, j].astype(F32)
-            field[high, 0:8, lanes] = ud[i, j].astype(F32)
-            field[high, 24:32, lanes] = uu[i, j].astype(F32)
+            field[planes, 8:24, lanes] = source[at, j].astype(F32)
+            field[planes, pl.ds(row_1, 8), lanes] = z1[i, j].astype(F32)
+            field[planes, pl.ds(row_2, 8), lanes] = z2[i, j].astype(F32)
 
     @pl.loop(0, 28)
     def _(p):
@@ -253,24 +260,28 @@
 
 
 def decoder_kernel(
-    own, xd, xu, zd, zu, dd, du, ud, uu, skip, d1, p1, d2, p2, w5u, w5s, w6u, w6s,
+    own, x1, x2, z1, z2, skip, d1, p1, d2, p2, w5u, w5s, w6u, w6s,
     out, whole, sides, pooled, quarter, mixed, grown, ups, acc, tall, fine,
 ):
     q, s = position()
-    blocks = [[dd, xd, du], [zd, own, zu], [ud, xu, uu]]
-    for a in range(3):
-        for b in range(3):
-            whole[8 * a : 8 * a + 8, 8 * b : 8 * b + 8, :] = blocks[a][b][...].astype(F32)
+    plane_1 = 14 * (1 - q % 2)
+    plane_2 = 14 - plane_1
+    row_1 = pl.multiple_of(16 * (1 - s % 2), 8)
+    row_2 = pl.multiple_of(16 * (s % 2), 8)
+    for start, size, source, at in ((plane_1, 6, x1, 0), (6, 8, own, 6), (plane_2, 6, x2, 14)):
+        whole[pl.ds(start, size), 8:16, :] = source[...].astype(F32)
+        whole[pl.ds(start, size), pl.ds(row_1, 8), :] = z1[at : at + size].astype(F32)
+        whole[pl.ds(start, size), pl.ds(row_2, 8), :] = z2[at : at + size].astype(F32)
 
     for p in range(12):
         for dz in range(3):
-            sides[dz, p] = whole[p + 6, pl.ds(3 + dz, 16), :].astype(BF)
+            sides[dz, p] = whole[p + 4, pl.ds(3 + dz, 16), :].astype(BF)
 
     quarter[...] = jnp.zeros_like(quarter)
 
     @pl.loop(0, 10)
     def _(p):
-        best = jnp.maximum(whole[2 * p + 2], whole[2 * p + 3])
+        best = jnp.maximum(whole[2 * p], whole[2 * p + 1])
         best = jnp.maximum(best, pltpu.roll(best, 448, 1))
         for t in range(4):
             pooled[0:24, :] = best[:, 128 * t : 128 * t + 128]
@@ -335,7 +346,7 @@
             out[i, j] = acc[4 * i : 4 * i + 4, :, 128 * j : 128 * j + 128].astype(BF)
 
 
-def call(kernel, outs, scratch=(), flops=0):
+def call(kernel, outs, scratch=(), flops=0, limit=8):
     whole = pl.BlockSpec(memory_space=pltpu.VMEM)
 
     def run(*args):
@@ -345,7 +356,7 @@
             in_specs=[whole] * len(args),
             out_specs=jax.tree.map(lambda _: whole, outs),
             scratch_shapes=list(scratch),
-            compiler_params=pltpu.CompilerParams(vmem_limit_bytes=VMEM_LIMIT),
+            compiler_params=pltpu.CompilerParams(vmem_limit_bytes=limit << 20),
             cost_estimate=pl.CostEstimate(flops=flops, bytes_accessed=4 << 20, transcendentals=0),
         )(*args)
 
@@ -368,13 +379,20 @@
     rows = call(to_rows_kernel, shape(16, 4, 16, 128))(features.reshape(512, 256))
     own = lax.all_to_all(rows, PLANE, 0, 0, tiled=True, axis_index_groups=GROUPS)
     own = own.reshape(4, 4, 4, 16, 128)
-    cut_x = {-1: slice(0, 2), 0: slice(0, 4), 1: slice(2, 4)}
-    cut_z = {-1: slice(0, 8), 0: slice(0, 16), 1: slice(8, 16)}
-    got = {}
-    for a, b in STEPS:
-        piece = own[cut_x[a], :, :, cut_z[b], :]
-        got[(-a, -b)] = lax.ppermute(piece, EVERY, neighbour_pairs(a, b))
-    w1, w2, w3, w4 = call(encoder_weights_kernel, (bands,) * 4)(
+    q, s = position()
+    x_swaps = [swap_pairs(1, 0, parity) for parity in range(2)]
+    z_swaps = [swap_pairs(0, 1, parity) for parity in range(2)]
+    x_got = []
+    for turn in range(2):
+        start = jnp.where((q + turn) % 2 == 0, 2, 0)
+        piece = lax.dynamic_slice_in_dim(own, start, 2, 0)
+        x_got.append(lax.ppermute(piece, EVERY, x_swaps[turn]))
+    broad = jnp.concatenate([x_got[0], own, x_got[1]], axis=0)
+    z_got = []
+    for turn in range(2):
+        piece = jnp.where((s + turn) % 2 == 0, broad[..., 8:16, :], broad[..., 0:8, :])
+        z_got.append(lax.ppermute(piece, EVERY, z_swaps[turn]))
+    w1, w2, w3, w4 = call(encoder_weights_kernel, (bands,) * 4, limit=LIMITS[0])(
         conv_one, conv_two, conv_three, conv_four
     )
     skip, half_skip = call(
@@ -390,16 +408,21 @@
             pltpu.VMEM((32, 128), F32),
         ],
         flops=6 << 30,
-    )(own, *[got[step] for step in STEPS], w1, w2, w3, w4)
-    around = {}
-    for a, b in STEPS:
-        around[(-a, -b)] = lax.ppermute(half_skip, EVERY, neighbour_pairs(a, b))
-    w5u, w5s, w6u, w6s = call(decoder_weights_kernel, (bands,) * 4)(conv_five, conv_six)
+        limit=LIMITS[2],
+    )(own, *x_got, *z_got, w1, w2, w3, w4)
+    x_got = []
+    for turn in range(2):
+        start = jnp.where((q + turn) % 2 == 0, 2, 0)
+        piece = lax.dynamic_slice_in_dim(half_skip, start, 6, 0)
+        x_got.append(lax.ppermute(piece, EVERY, x_swaps[turn]))
+    broad = jnp.concatenate([x_got[0], half_skip, x_got[1]], axis=0)
+    z_got = [lax.ppermute(broad, EVERY, z_swaps[turn]) for turn in range(2)]
+    w5u, w5s, w6u, w6s = call(decoder_weights_kernel, (bands,) * 4, limit=LIMITS[1])(conv_five, conv_six)
     rows = call(
         decoder_kernel,
         shape(4, 4, 4, 16, 128),
         [
-            pltpu.VMEM((24, 24, 512), F32),
+            pltpu.VMEM((20, 24, 512), F32),
             pltpu.VMEM((3, 12, 16, 512), BF),
             pltpu.VMEM((32, 128), F32),
             pltpu.VMEM((10, 16, 512), F32),
@@ -411,8 +434,9 @@
             pltpu.VMEM((3, 18, 16, 512), BF),
         ],
         flops=2 << 30,
+        limit=LIMITS[3],
     )(
-        half_skip, *[around[step] for step in STEPS], skip,
+        half_skip, *x_got, *z_got, skip,
         taps_one, mix_one, taps_two, point_two, w5u, w5s, w6u, w6s,
     )
     back = lax.all_to_all(

time: 144 us -> 77.2 us (0.54)
  the two profiles are of different devices: /device:TPU:137 before, /device:TPU:72 now
where the time goes in v2:
time: 77.2 us; the launch traced here: 76.5 us
  Pallas kernels  21.6 us (28%)
  waiting for transfers between devices  21.6 us (28%)
  starting transfers between devices  18.4 us (24%)
  blocking collectives  12.3 us (16%)
  local copies, waits for them, and re-layouts  2.05 us (3%)
    pallas_call x6, Pallas kernels, run(): pl.pallas_call(kernel, out_shape=outs, in_specs=[whole] * len(args), out_...  21.6 us
    all_to_all x1, blocking collectives, local(): lax.all_to_all(rows.reshape(16, 4, 16, 128), PLANE, 0, 0, tiled=True, axi...  12.3 us
    ppermute x4, starting transfers between devices, local(): x_got.append(lax.ppermute(piece, EVERY, x_swaps[turn]))  8.57 us
    all_to_all x1, waiting for transfers between devices, local(): lax.all_to_all(rows, PLANE, 0, 0, tiled=True, axis_index_groups=GROUPS)  7.71 us
    all_to_all x1, starting transfers between devices, local(): lax.all_to_all(rows, PLANE, 0, 0, tiled=True, axis_index_groups=GROUPS)  5.76 us
    ppermute x4, waiting for transfers between devices, local(): x_got.append(lax.ppermute(piece, EVERY, x_swaps[turn]))  5.68 us
    ppermute x2, waiting for transfers between devices, local(): z_got.append(lax.ppermute(piece, EVERY, z_swaps[turn]))  4.89 us
    ppermute x2, waiting for transfers between devices, local(): z_got = [lax.ppermute(broad, EVERY, z_swaps[turn]) for turn in range(2)]  3.31 us
  transfers between devices with their start and end apart: 9, of which 7 were waited for; matrix products, arithmetic and copies ran while one was open for 0% of the time, Pallas kernels for 4%

profile of v2, /device:TPU:72, one launch (start us, length us, event | category | flops | bytes accessed | tf_op | source)
XLA Modules:
  0.0 76.5 jit_solution(9807296459113266962)
XLA Ops:
  0.0 0.0 copy-start.1
  0.0 1.1 %reshape.12.cells_ref = bf16[512,256]{1,0:T(8,128)(2,1)S(1)} reshape(bf16[32,4,4,256]{3,2,1,0:T(4,128)(2,1)} %param.11) | data formatting | bytes 524288 | tf_op jit(solution)/shard_map/reshape | solution.py:379
  1.1 1.0 %shard_map.109 = bf16[16,4,16,128]{3,2,1,0:T(8,128)(2,1)} custom-call(bf16[512,256]{1,0:T(8,128)(2,1)S(1)} %reshape.12.cells_ref), custom_call_target="tpu_custom_call" | custom-call | bytes 4194304 | tf_op jit(solution)/shard_map/pallas_call | solution.py:353
  2.1 5.8 %all-to-all-start = ((bf16[16,4,16,128]{3,2,1,0:T(8,128)(2,1)}), bf16[16,4,16,128]{3,2,1,0:T(8,128)(2,1)S(1)}, u32[]{:S(2)}, u32[]{:S(2)}) async-start(bf16[16,4,16,128]{3,2,1,0:T(8,128)(2,1)} %shard_map.109), calls=%async_computation | async-start | bytes 524288 | tf_op jit(solution)/shard_map/all_to_all | solution.py:380
  8.0 7.7 %all-to-all-done = bf16[16,4,16,128]{3,2,1,0:T(8,128)(2,1)S(1)} async-done(((bf16[16,4,16,128]{3,2,1,0:T(8,128)(2,1)}), bf16[16,4,16,128]{3,2,1,0:T(8,128)(2,1)S(1)}, u32[]{:S(2)}, u32[]{:S(2)}) %all-to-all-start) | async-done | bytes 262176 | tf_op jit(solution)/shard_map/all_to_all | solution.py:380
  15.7 0.5 collective-permute-start
  16.2 4.3 %collective-permute-start.1 = (bf16[2,4,4,16,128]{4,3,2,1,0:T(8,128)(2,1)S(1)}, bf16[2,4,4,16,128]{4,3,2,1,0:T(8,128)(2,1)S(1)}, u32[]{:S(2)}, u32[]{:S(2)}) collective-permute-start(bf16[2,4,4,16,128]{4,3,2,1,0:T(8,128)(2,1)S(1)} %get-tuple-element.27), channel_id=1, source_target_pairs={{64,128},{128,64},{80,144},{144,80},{84,148},{148,84},{68,132},{13... | collective-permute-start | bytes 393224 | tf_op jit(solution)/shard_map/ppermute | solution.py:389
  20.6 0.6 collective-permute-done.x1
  21.3 2.7 %collective-permute-done.1.x2 = bf16[2,4,4,16,128]{4,3,2,1,0:T(8,128)(2,1)S(1)} collective-permute-done((bf16[2,4,4,16,128]{4,3,2,1,0:T(8,128)(2,1)S(1)}, bf16[2,4,4,16,128]{4,3,2,1,0:T(8,128)(2,1)S(1)}, u32[]{:S(2)}, u32[]{:S(2)}) %collective-permute-start.1) | collective-permute-done | bytes 131104 | tf_op jit(solution)/shard_map/ppermute | solution.py:389
  24.0 0.1 pad_maximum_fusion
  24.1 0.1 collective-permute-start.2
  24.2 1.9 %collective-permute-start.3 = (bf16[8,4,4,8,128]{4,3,2,1,0:T(8,128)(2,1)S(1)}, bf16[8,4,4,8,128]{4,3,2,1,0:T(8,128)(2,1)S(1)}, u32[]{:S(2)}, u32[]{:S(2)}) collective-permute-start(bf16[8,4,4,8,128]{4,3,2,1,0:T(8,128)(2,1)S(1)} %get-tuple-element.25), channel_id=1, source_target_pairs={{16,20},{20,16},{4,8},{8,4},{24,28},{28,24},{12,44},{44,12},{60,56... | collective-permute-start | bytes 786440 | tf_op jit(solution)/shard_map/ppermute | solution.py:394
  26.2 1.4 %shard_map.110 = (bf16[9,512,256]{2,1,0:T(8,128)(2,1)S(1)}, bf16[9,512,256]{2,1,0:T(8,128)(2,1)S(1)}, bf16[9,512,256]{2,1,0:T(8,128)(2,1)S(1)}, bf16[9,512,256]{2,1,0:T(8,128)(2,1)S(1)}) custom-call(bf16[32,864]{1,0:T(8,128)(2,1)S(1)} %copy-done.4, bf16[32,864]{1,0:T(8,128)(2,1)S(1)} %copy-done.5, bf16[64,864]{1,0:T(8,128)(2,1)S(1)} %copy-done.3, ...), custom_call_target="tpu_custom_call" | custom-call | bytes 4194304 | tf_op jit(solution)/shard_map/pallas_call | solution.py:353
  27.6 0.0 collective-permute-done.2.z1
  27.6 4.9 %collective-permute-done.3.z2 = bf16[8,4,4,8,128]{4,3,2,1,0:T(8,128)(2,1)S(1)} collective-permute-done((bf16[8,4,4,8,128]{4,3,2,1,0:T(8,128)(2,1)S(1)}, bf16[8,4,4,8,128]{4,3,2,1,0:T(8,128)(2,1)S(1)}, u32[]{:S(2)}, u32[]{:S(2)}) %collective-permute-start.3) | collective-permute-done | bytes 262176 | tf_op jit(solution)/shard_map/ppermute | solution.py:394
  32.5 0.0 copy-start.9
  32.5 0.0 copy-start.6
  32.5 10.6 %shard_map.111 = (bf16[3,18,16,512]{3,2,1,0:T(8,128)(2,1)S(1)}, bf16[8,8,512]{2,1,0:T(8,128)(2,1)S(1)}) custom-call(bf16[4,4,4,16,128]{4,3,2,1,0:T(8,128)(2,1)S(1)} %bitcast.6, bf16[2,4,4,16,128]{4,3,2,1,0:T(8,128)(2,1)S(1)} %collective-permute-done.x1, bf16[2,4,4,16,128]{4,3,2,1,0:T(8,128)(2,1)S(1)} %collective-permute-done.1.x2, ...), custom_call_target="tpu_custom_call" | custom-call | flops 6442450944 | bytes 4194304 | tf_op jit(solution)/shard_map/pallas_call | solution.py:353
  43.2 0.1 collective-permute-start.4
  43.3 3.6 %collective-permute-start.5 = (bf16[6,8,512]{2,1,0:T(8,128)(2,1)S(1)}, bf16[6,8,512]{2,1,0:T(8,128)(2,1)S(1)}, u32[]{:S(2)}, u32[]{:S(2)}) collective-permute-start(bf16[6,8,512]{2,1,0:T(8,128)(2,1)S(1)} %get-tuple-element.29), channel_id=1, source_target_pairs={{64,128},{128,64},{80,144},{144,80},{84,148},{148,84},{68,132},{13... | collective-permute-start | bytes 147464 | tf_op jit(solution)/shard_map/ppermute | solution.py:417
  46.9 0.4 collective-permute-done.4.x1
  47.4 1.9 %collective-permute-done.5.x2 = bf16[6,8,512]{2,1,0:T(8,128)(2,1)S(1)} collective-permute-done((bf16[6,8,512]{2,1,0:T(8,128)(2,1)S(1)}, bf16[6,8,512]{2,1,0:T(8,128)(2,1)S(1)}, u32[]{:S(2)}, u32[]{:S(2)}) %collective-permute-start.5) | collective-permute-done | bytes 49184 | tf_op jit(solution)/shard_map/ppermute | solution.py:417
  49.3 0.0 collective-permute-start.6
  49.3 2.1 %collective-permute-start.7 = (bf16[20,8,512]{2,1,0:T(8,128)(2,1)S(1)}, bf16[20,8,512]{2,1,0:T(8,128)(2,1)S(1)}, u32[]{:S(2)}, u32[]{:S(2)}) collective-permute-start(bf16[20,8,512]{2,1,0:T(8,128)(2,1)S(1)} %constant_dynamic-update-slice_fusion), channel_id=1, source_target_pairs={{16,20},{20,16},{4,8},{8,4},{24,28},{28,24},{12,44},{44,12},{60,56... | collective-permute-start | bytes 491528 | tf_op jit(solution)/shard_map/ppermute | solution.py:419
  51.4 0.1 copy.12
  51.5 1.6 %shard_map.112 = (bf16[9,512,256]{2,1,0:T(8,128)(2,1)S(1)}, bf16[9,512,256]{2,1,0:T(8,128)(2,1)S(1)}, bf16[9,512,256]{2,1,0:T(8,128)(2,1)S(1)}, bf16[9,512,256]{2,1,0:T(8,128)(2,1)S(1)}) custom-call(bf16[64,5184]{1,0:T(8,128)(2,1)S(1)} %copy-done, bf16[32,2592]{1,0:T(8,128)(2,1)S(1)} %copy-done.2), custom_call_target="tpu_custom_call" | custom-call | bytes 4194304 | tf_op jit(solution)/shard_map/pallas_call | solution.py:353
  53.2 0.0 collective-permute-done.6.z1
  53.2 3.3 %collective-permute-done.7.z2 = bf16[20,8,512]{2,1,0:T(8,128)(2,1)S(1)} collective-permute-done((bf16[20,8,512]{2,1,0:T(8,128)(2,1)S(1)}, bf16[20,8,512]{2,1,0:T(8,128)(2,1)S(1)}, u32[]{:S(2)}, u32[]{:S(2)}) %collective-permute-start.7) | collective-permute-done | bytes 163872 | tf_op jit(solution)/shard_map/ppermute | solution.py:419
  56.5 6.6 %shard_map.113 = bf16[4,4,4,16,128]{4,3,2,1,0:T(8,128)(2,1)S(1)} custom-call(bf16[8,8,512]{2,1,0:T(8,128)(2,1)S(1)} %get-tuple-element.19.own, bf16[6,8,512]{2,1,0:T(8,128)(2,1)S(1)} %collective-permute-done.4.x1, bf16[6,8,512]{2,1,0:T(8,128)(2,1)S(1)} %collective-permute-done.5.x2, bf16[20,8,512]{2,1,0:T(8,128)(2,1)S(1)} %collective-permute-done.6.z1, ...), custom_call_target="tpu_custom_call" | custom-call | flops 2147483648 | bytes 4194304 | tf_op jit(solution)/shard_map/pallas_call | solution.py:353
  63.1 12.3 %all_to_all.10.rows_ref = bf16[16,4,16,128]{3,2,1,0:T(8,128)(2,1)S(1)} all-to-all(bf16[16,4,16,128]{3,2,1,0:T(8,128)(2,1)S(1)} %bitcast.7), channel_id=1, replica_groups={{0,4,8,12,16,20,24,28,32,36,40,44,48,52,56,60},{64,68,72,76,80,84,88,92..., dimensions={0} | all-to-all | bytes 524288 | tf_op jit(solution)/shard_map/all_to_all | solution.py:442
  75.4 0.3 shard_map.114
  75.7 0.8 %reshape.15 = bf16[32,4,4,256]{3,2,1,0:T(4,128)(2,1)} reshape(bf16[512,256]{1,0:T(8,128)(2,1)S(1)} %shard_map.114) | data formatting | bytes 524288 | tf_op jit(solution)/shard_map/reshape | solution.py:445
  (25 shorter events, 0.1 us)
Async XLA Ops:
  0.0 26.1 %copy-start.4 = (bf16[32,864]{1,0:T(8,128)(2,1)S(1)}, bf16[32,864]{1,0:T(8,128)(2,1)}, u32[]{:S(2)}) copy-start(bf16[32,864]{1,0:T(8,128)(2,1)} %w1.1) | copy-start | bytes 165892
  0.0 26.1 %copy-start.5 = (bf16[32,864]{1,0:T(8,128)(2,1)S(1)}, bf16[32,864]{1,0:T(8,128)(2,1)}, u32[]{:S(2)}) copy-start(bf16[32,864]{1,0:T(8,128)(2,1)} %w2.1) | copy-start | bytes 165892
  0.0 26.1 %copy-start.3 = (bf16[64,864]{1,0:T(8,128)(2,1)S(1)}, bf16[64,864]{1,0:T(8,128)(2,1)}, u32[]{:S(2)}) copy-start(bf16[64,864]{1,0:T(8,128)(2,1)} %w3.1) | copy-start | bytes 331780
  0.0 26.2 %copy-start.1 = (bf16[64,1728]{1,0:T(8,128)(2,1)S(1)}, bf16[64,1728]{1,0:T(8,128)(2,1)}, u32[]{:S(2)}) copy-start(bf16[64,1728]{1,0:T(8,128)(2,1)} %w4.1) | copy-start | bytes 663556
  2.1 13.5 %all-to-all-start = ((bf16[16,4,16,128]{3,2,1,0:T(8,128)(2,1)}), bf16[16,4,16,128]{3,2,1,0:T(8,128)(2,1)S(1)}, u32[]{:S(2)}, u32[]{:S(2)}) async-start(bf16[16,4,16,128]{3,2,1,0:T(8,128)(2,1)} %shard_map.109), calls=%async_computation | async-start | bytes 524288 | tf_op jit(solution)/shard_map/all_to_all | solution.py:380
  15.7 5.6 %collective-permute-start = (bf16[2,4,4,16,128]{4,3,2,1,0:T(8,128)(2,1)S(1)}, bf16[2,4,4,16,128]{4,3,2,1,0:T(8,128)(2,1)S(1)}, u32[]{:S(2)}, u32[]{:S(2)}) collective-permute-start(bf16[2,4,4,16,128]{4,3,2,1,0:T(8,128)(2,1)S(1)} %get-tuple-element.28), channel_id=1, source_target_pairs={{0,64},{64,0},{16,80},{80,16},{20,84},{84,20},{4,68},{68,4},{8,72}... | collective-permute-start | bytes 393224 | tf_op jit(solution)/shard_map/ppermute | solution.py:389
  16.2 7.8 %collective-permute-start.1 = (bf16[2,4,4,16,128]{4,3,2,1,0:T(8,128)(2,1)S(1)}, bf16[2,4,4,16,128]{4,3,2,1,0:T(8,128)(2,1)S(1)}, u32[]{:S(2)}, u32[]{:S(2)}) collective-permute-start(bf16[2,4,4,16,128]{4,3,2,1,0:T(8,128)(2,1)S(1)} %get-tuple-element.27), channel_id=1, source_target_pairs={{64,128},{128,64},{80,144},{144,80},{84,148},{148,84},{68,132},{13... | collective-permute-start | bytes 393224 | tf_op jit(solution)/shard_map/ppermute | solution.py:389
  24.1 3.5 %collective-permute-start.2 = (bf16[8,4,4,8,128]{4,3,2,1,0:T(8,128)(2,1)S(1)}, bf16[8,4,4,8,128]{4,3,2,1,0:T(8,128)(2,1)S(1)}, u32[]{:S(2)}, u32[]{:S(2)}) collective-permute-start(bf16[8,4,4,8,128]{4,3,2,1,0:T(8,128)(2,1)S(1)} %get-tuple-element.26), channel_id=1, source_target_pairs={{0,16},{16,0},{20,4},{4,20},{8,24},{24,8},{28,12},{12,28},{44,60},... | collective-permute-start | bytes 786440 | tf_op jit(solution)/shard_map/ppermute | solution.py:394
  24.2 8.3 %collective-permute-start.3 = (bf16[8,4,4,8,128]{4,3,2,1,0:T(8,128)(2,1)S(1)}, bf16[8,4,4,8,128]{4,3,2,1,0:T(8,128)(2,1)S(1)}, u32[]{:S(2)}, u32[]{:S(2)}) collective-permute-start(bf16[8,4,4,8,128]{4,3,2,1,0:T(8,128)(2,1)S(1)} %get-tuple-element.25), channel_id=1, source_target_pairs={{16,20},{20,16},{4,8},{8,4},{24,28},{28,24},{12,44},{44,12},{60,56... | collective-permute-start | bytes 786440 | tf_op jit(solution)/shard_map/ppermute | solution.py:394
  32.5 18.9 %copy-start.7 = (bf16[128,64]{0,1:T(8,128)(2,1)S(1)}, bf16[128,64]{0,1:T(8,128)(2,1)}, u32[]{:S(2)}) copy-start(bf16[128,64]{0,1:T(8,128)(2,1)} %param.17) | copy-start | bytes 49156
  32.5 19.0 %copy-start = (bf16[64,5184]{1,0:T(8,128)(2,1)S(1)}, bf16[64,5184]{1,0:T(8,128)(2,1)}, u32[]{:S(2)}) copy-start(bf16[64,5184]{1,0:T(8,128)(2,1)} %w5.1) | copy-start | bytes 1990660
  32.5 19.1 %copy-start.2 = (bf16[32,2592]{1,0:T(8,128)(2,1)S(1)}, bf16[32,2592]{1,0:T(8,128)(2,1)}, u32[]{:S(2)}) copy-start(bf16[32,2592]{1,0:T(8,128)(2,1)} %w6.1) | copy-start | bytes 497668
  32.5 20.7 %copy-start.8 = (bf16[128,27]{0,1:T(8,128)(2,1)S(1)}, bf16[128,27]{0,1:T(8,128)(2,1)}, u32[]{:S(2)}) copy-start(bf16[128,27]{0,1:T(8,128)(2,1)} %param.18) | copy-start | bytes 20740
  32.5 20.7 %copy-start.9 = (bf16[64,27]{0,1:T(8,128)(2,1)S(1)}, bf16[64,27]{0,1:T(8,128)(2,1)}, u32[]{:S(2)}) copy-start(bf16[64,27]{0,1:T(8,128)(2,1)} %param.16) | copy-start | bytes 10372
  32.5 24.0 %copy-start.6 = (bf16[128,128]{1,0:T(8,128)(2,1)S(1)}, bf16[128,128]{1,0:T(8,128)(2,1)}, u32[]{:S(2)}) copy-start(bf16[128,128]{1,0:T(8,128)(2,1)} %p2.1) | copy-start | bytes 98308
  43.2 4.2 %collective-permute-start.4 = (bf16[6,8,512]{2,1,0:T(8,128)(2,1)S(1)}, bf16[6,8,512]{2,1,0:T(8,128)(2,1)S(1)}, u32[]{:S(2)}, u32[]{:S(2)}) collective-permute-start(bf16[6,8,512]{2,1,0:T(8,128)(2,1)S(1)} %get-tuple-element.30), channel_id=1, source_target_pairs={{0,64},{64,0},{16,80},{80,16},{20,84},{84,20},{4,68},{68,4},{8,72}... | collective-permute-start | bytes 147464 | tf_op jit(solution)/shard_map/ppermute | solution.py:417
  43.3 6.0 %collective-permute-start.5 = (bf16[6,8,512]{2,1,0:T(8,128)(2,1)S(1)}, bf16[6,8,512]{2,1,0:T(8,128)(2,1)S(1)}, u32[]{:S(2)}, u32[]{:S(2)}) collective-permute-start(bf16[6,8,512]{2,1,0:T(8,128)(2,1)S(1)} %get-tuple-element.29), channel_id=1, source_target_pairs={{64,128},{128,64},{80,144},{144,80},{84,148},{148,84},{68,132},{13... | collective-permute-start | bytes 147464 | tf_op jit(solution)/shard_map/ppermute | solution.py:417
  49.3 3.9 %collective-permute-start.6 = (bf16[20,8,512]{2,1,0:T(8,128)(2,1)S(1)}, bf16[20,8,512]{2,1,0:T(8,128)(2,1)S(1)}, u32[]{:S(2)}, u32[]{:S(2)}) collective-permute-start(bf16[20,8,512]{2,1,0:T(8,128)(2,1)S(1)} %constant_dynamic-update-slice_fusion), channel_id=1, source_target_pairs={{0,16},{16,0},{20,4},{4,20},{8,24},{24,8},{28,12},{12,28},{44,60},... | collective-permute-start | bytes 491528 | tf_op jit(solution)/shard_map/ppermute | solution.py:419
  49.3 7.2 %collective-permute-start.7 = (bf16[20,8,512]{2,1,0:T(8,128)(2,1)S(1)}, bf16[20,8,512]{2,1,0:T(8,128)(2,1)S(1)}, u32[]{:S(2)}, u32[]{:S(2)}) collective-permute-start(bf16[20,8,512]{2,1,0:T(8,128)(2,1)S(1)} %constant_dynamic-update-slice_fusion), channel_id=1, source_target_pairs={{16,20},{20,16},{4,8},{8,4},{24,28},{28,24},{12,44},{44,12},{60,56... | collective-permute-start | bytes 491528 | tf_op jit(solution)/shard_map/ppermute | solution.py:419

commit v3 on v2

--- a/solution.py
+++ b/solution.py
@@ -71,9 +71,9 @@
     ).astype(BF)
 
 
-def band(spread, out_ref, stride, first, used, lanes_in, lanes_out, grown):
+def band(spread, out_ref, stride, first, used, lanes_in, lanes_out, grown=False):
     per_tile = 128 // lanes_out
-    base = 128 // lanes_in
+    lead = 128 // lanes_in
     group = lax.broadcasted_iota(jnp.int32, (used, 128), 1) // lanes_out
     chosen = [jnp.where(group == j, 1.0, 0.0).astype(BF) for j in range(per_tile)]
     empty = jnp.zeros((lanes_in, 128), BF)
@@ -90,9 +90,9 @@
                 pieces = {1: parts[0], 0: parts[1], -1: parts[2]}
             pieces = {gap: piece.astype(BF) for gap, piece in pieces.items()}
             made = {}
-            for at in range(512 // lanes_in):
+            for at in range(out_ref.shape[1] // lanes_in):
                 for tile in range(2):
-                    key = (2 if grown else 1) * (at - base) - per_tile * tile
+                    key = (2 if grown else 1) * (at - lead) - per_tile * tile
                     if key not in made:
                         block = None
                         for gap, piece in pieces.items():
@@ -121,41 +121,38 @@
 
 
 def encoder_weights_kernel(w1, w2, w3, w4, o1, o2, o3, o4):
-    band(spread_lanes(w1[...], 32), o1, 32, 0, 32, 32, 32, False)
-    band(spread_lanes(w2[...], 32), o2, 32, 0, 32, 32, 32, False)
-    band(spread_lanes(w3[...], 64), o3, 32, 0, 32, 64, 64, False)
-    band(spread_lanes(w4[...], 64), o4, 64, 0, 64, 64, 64, False)
+    band(spread_lanes(w1[...], 32), o1, 32, 0, 32, 32, 32)
+    band(spread_lanes(w2[...], 32), o2, 32, 0, 32, 32, 32)
+    band(spread_lanes(w3[...], 64), o3, 32, 0, 32, 64, 64)
+    band(spread_lanes(w4[...], 64), o4, 64, 0, 64, 64, 64)
 
 
 def decoder_weights_kernel(w5, w6, o5u, o5s, o6u, o6s):
     wide = spread_lanes(w5[...], 64)
-    band(wide, o5u, 192, 0, 128, 128, 64, True)
-    band(wide, o5s, 192, 128, 64, 64, 64, False)
+    band(wide, o5u, 192, 0, 128, 128, 64, grown=True)
+    band(wide, o5s, 192, 128, 64, 64, 64)
     fine = spread_lanes(w6[...], 32)
-    band(fine, o6u, 96, 0, 64, 64, 32, True)
-    band(fine, o6s, 96, 64, 32, 32, 32, False)
-
-
-def convolve(fields, weights, acc_ref, planes, rows):
-    taps = [(n, dx, dz) for n in range(len(fields)) for dx in range(3) for dz in range(3)]
-    for g in range(2):
-        total = None
-        for at in range(0, len(taps), 2):
-            chunk = taps[at : at + 2]
-            left = [
-                fields[n][dz, dx : dx + planes, :, 128 * g : 128 * g + 384].reshape(planes * rows, 384)
-                for n, dx, dz in chunk
-            ]
-            right = [
-                weights[n][dx * 3 + dz, 128 * (1 - g) : 128 * (1 - g) + 384, :] for n, dx, dz in chunk
-            ]
-            part = jnp.dot(
-                jnp.concatenate(left, axis=1) if len(left) > 1 else left[0],
-                jnp.concatenate(right, axis=0) if len(right) > 1 else right[0],
-                preferred_element_type=F32,
-            )
-            total = part if total is None else total + part
-        acc_ref[0:planes, 0:rows, 256 * g : 256 * g + 256] = total.reshape(planes, rows, 256)
+    band(fine, o6u, 96, 0, 64, 64, 32, grown=True)
+    band(fine, o6s, 96, 64, 32, 32, 32)
+
+
+def convolve(terms, planes, rows, g):
+    taps = [
+        (field[dz, dx : dx + planes, :, 128 * g : 128 * g + 384].reshape(planes * rows, 384),
+         weights[dx * 3 + dz, 128 * (1 - g) : 128 * (1 - g) + 384, :])
+        for field, weights in terms
+        for dx in range(3)
+        for dz in range(3)
+    ]
+    total = None
+    for at in range(0, len(taps), 2):
+        left = [left for left, _ in taps[at : at + 2]]
+        right = [right for _, right in taps[at : at + 2]]
+        part = jnp.dot(
+            jnp.concatenate(left, axis=1), jnp.concatenate(right, axis=0), preferred_element_type=F32
+        )
+        total = part if total is None else total + part
+    return total.reshape(planes, rows, 256)
 
 
 def row_mask(rows, start, limit):
@@ -163,47 +160,85 @@
     return (at >= 0) & (at < limit)
 
 
-def store_turned(dest, plane, value, rows):
-    dest[0, plane] = pltpu.roll(value, 1, 0).astype(BF)
-    dest[1, plane] = value.astype(BF)
-    dest[2, plane] = pltpu.roll(value, rows - 1, 0).astype(BF)
+def store_turned(dest, plane, value, keep=slice(None)):
+    dest[0, plane] = pltpu.roll(value, 1, 0)[keep].astype(BF)
+    dest[1, plane] = value[keep].astype(BF)
+    dest[2, plane] = pltpu.roll(value, value.shape[0] - 1, 0)[keep].astype(BF)
+
+
+def x_blocks(own, x1, x2, q):
+    plane_1 = 24 * (1 - q % 2)
+    plane_2 = 24 - plane_1
+    starts = [plane_1, plane_1 + 4, 8, 12, 16, 20, plane_2, plane_2 + 4]
+    sources = [(x1, 0), (x1, 1), (own, 0), (own, 1), (own, 2), (own, 3), (x2, 0), (x2, 1)]
+    return [(pl.ds(start, 4), source, i) for start, (source, i) in zip(starts, sources)]
+
+
+def own_rows_kernel(own, x1, x2, w1, out, field, turned, acc):
+    q, _ = position()
+    for planes, source, i in x_blocks(own, x1, x2, q):
+        for j in range(4):
+            field[planes, :, 128 * j : 128 * j + 128] = source[i, j].astype(F32)
+
+    @pl.loop(0, 28, unroll=4)
+    def _(p):
+        store_turned(turned, p, field[p + 2])
+
+    for g in range(2):
+        acc[:, :, 256 * g : 256 * g + 256] = convolve([(turned, w1)], 26, 16, g)
+
+    @pl.loop(0, 26, unroll=2)
+    def _(p):
+        x = 16 * q - 5 + p
+        out[p] = jnp.where((x >= 0) & (x < 64), jnp.maximum(acc[p], 0.0), 0.0).astype(BF)
 
 
 def encoder_kernel(
-    own, x1, x2, z1, z2, w1, w2, w3, w4,
-    skip_out, half_out, field, turned, first, acc, half, mid, pooled,
+    own, x1, x2, z1, z2, own_first, w1, w2, w3, w4,
+    skip_out, half_out, field, turned, full, first, acc, half, mid, pooled,
 ):
     q, s = position()
     x0, z0 = 16 * q, 16 * s
-    plane_1 = 24 * (1 - q % 2)
-    plane_2 = 24 - plane_1
     row_1 = pl.multiple_of(24 * (1 - s % 2), 8)
     row_2 = pl.multiple_of(24 * (s % 2), 8)
-    starts = [plane_1, plane_1 + 4, 8, 12, 16, 20, plane_2, plane_2 + 4]
-    for i in range(8):
-        planes = pl.ds(starts[i], 4)
-        source, at = (x1, i) if i < 2 else ((own, i - 2) if i < 6 else (x2, i - 6))
+    for at, (planes, source, i) in enumerate(x_blocks(own, x1, x2, q)):
         for j in range(4):
             lanes = slice(128 * j, 128 * j + 128)
-            field[planes, 8:24, lanes] = source[at, j].astype(F32)
-            field[planes, pl.ds(row_1, 8), lanes] = z1[i, j].astype(F32)
-            field[planes, pl.ds(row_2, 8), lanes] = z2[i, j].astype(F32)
-
-    @pl.loop(0, 28)
-    def _(p):
-        store_turned(turned, p, field[p + 2], 32)
-
-    convolve([turned], [w1], acc, 26, 32)
-
-    @pl.loop(0, 26)
+            field[planes, 8:24, lanes] = source[i, j].astype(F32)
+            field[planes, pl.ds(row_1, 8), lanes] = z1[at, j].astype(F32)
+            field[planes, pl.ds(row_2, 8), lanes] = z2[at, j].astype(F32)
+
+    @pl.loop(0, 28, unroll=4)
+    def _(p):
+        for dz in range(3):
+            turned[dz, p] = jnp.concatenate(
+                [field[p + 2, pl.ds(dz, 8), :], field[p + 2, pl.ds(22 + dz, 8), :]], axis=0
+            ).astype(BF)
+
+    for g in range(2):
+        acc[0:26, 0:16, 256 * g : 256 * g + 256] = convolve([(turned, w1)], 26, 16, g)
+
+    for slot in range(2):
+        full[slot, 0:8] = jnp.zeros((8, 512), F32)
+        full[slot, 24:32] = jnp.zeros((8, 512), F32)
+    row = lax.broadcasted_iota(jnp.int32, (16, 512), 0)
+    row = jnp.where(row < 8, row + (z0 - 7), row + (z0 + 7))
+    row_inside = (row >= 0) & (row < 1024)
+
+    @pl.loop(0, 26, unroll=2)
     def _(p):
         x = x0 - 5 + p
-        inside = row_mask(32, z0 - 8, 1024) & (x >= 0) & (x < 64)
-        store_turned(first, p, jnp.where(inside, jnp.maximum(acc[p], 0.0), 0.0), 32)
-
-    convolve([first], [w2], acc, 24, 32)
-
-    @pl.loop(0, 12)
+        value = jnp.where(row_inside & (x >= 0) & (x < 64), jnp.maximum(acc[p, 0:16], 0.0), 0.0)
+        slot = p % 2
+        full[slot, 8:24] = own_first[p].astype(F32)
+        full[slot, 1:9] = value[0:8]
+        full[slot, 23:31] = value[8:16]
+        store_turned(first, p, full[slot])
+
+    for g in range(2):
+        acc[0:24, :, 256 * g : 256 * g + 256] = convolve([(first, w2)], 24, 32, g)
+
+    @pl.loop(0, 12, unroll=4)
     def _(h):
         best = None
         for b in range(2):
@@ -211,32 +246,36 @@
             x = x0 - 4 + p
             inside = row_mask(32, z0 - 8, 1024) & (x >= 0) & (x < 64)
             value = jnp.where(inside, jnp.maximum(acc[p], 0.0), 0.0)
-
-            @pl.when((p >= 3) & (p < 21))
-            def _():
-                skip_out[0, p - 3] = pltpu.roll(value, 1, 0)[8:24].astype(BF)
-                skip_out[1, p - 3] = value[8:24].astype(BF)
-                skip_out[2, p - 3] = pltpu.roll(value, 31, 0)[8:24].astype(BF)
-
+            store_turned(skip_out, jnp.where((p >= 3) & (p < 21), p - 3, 18), value, slice(8, 24))
             best = value if best is None else jnp.maximum(best, value)
         best = jnp.maximum(best, pltpu.roll(best, 480, 1))
+        pieces = []
         for t in range(4):
-            pooled[:, :] = best[:, 128 * t : 128 * t + 128]
-            piece = jnp.maximum(pooled[pl.ds(0, 16, stride=2), :], pooled[pl.ds(1, 16, stride=2), :])
-            half[0, h, :, 128 * t : 128 * t + 128] = pltpu.roll(piece, 1, 0).astype(BF)
-            half[1, h, :, 128 * t : 128 * t + 128] = piece.astype(BF)
-            half[2, h, :, 128 * t : 128 * t + 128] = pltpu.roll(piece, 15, 0).astype(BF)
-
-    convolve([half], [w3], acc, 10, 16)
-
-    @pl.loop(0, 10)
+            pooled[h % 4, t] = best[:, 128 * t : 128 * t + 128]
+            pieces.append(
+                jnp.maximum(
+                    pooled[h % 4, t, pl.ds(0, 16, stride=2), :], pooled[h % 4, t, pl.ds(1, 16, stride=2), :]
+                )
+            )
+        store_turned(half, h, jnp.concatenate(pieces, axis=1))
+
+    for g in range(2):
+        acc[0:10, 0:16, 256 * g : 256 * g + 256] = convolve([(half, w3)], 10, 16, g)
+
+    @pl.loop(0, 10, unroll=5)
     def _(p):
         x = 8 * q - 1 + p
         inside = row_mask(16, 8 * s - 4, 512) & (x >= 0) & (x < 32)
-        store_turned(mid, p, jnp.where(inside, jnp.maximum(acc[p, 0:16], 0.0), 0.0), 16)
-
-    convolve([mid], [w4], acc, 8, 16)
+        store_turned(mid, p, jnp.where(inside, jnp.maximum(acc[p, 0:16], 0.0), 0.0))
+
+    for g in range(2):
+        acc[0:8, 0:16, 256 * g : 256 * g + 256] = convolve([(mid, w4)], 8, 16, g)
     half_out[...] = jnp.maximum(acc[0:8, 4:12, :], 0.0).astype(BF)
+
+
+def skip_kernel(skip, w6s, out):
+    for g in range(2):
+        out[:, :, 256 * g : 256 * g + 256] = convolve([(skip.at[:, 0:18], w6s)], 16, 16, g)
 
 
 def depthwise(source, taps, planes, offset):
@@ -260,7 +299,7 @@
 
 
 def decoder_kernel(
-    own, x1, x2, z1, z2, skip, d1, p1, d2, p2, w5u, w5s, w6u, w6s,
+    own, x1, x2, z1, z2, skip_part, d1, p1, d2, p2, w5u, w5s, w6u,
     out, whole, sides, pooled, quarter, mixed, grown, ups, acc, tall, fine,
 ):
     q, s = position()
@@ -273,13 +312,14 @@
         whole[pl.ds(start, size), pl.ds(row_1, 8), :] = z1[at : at + size].astype(F32)
         whole[pl.ds(start, size), pl.ds(row_2, 8), :] = z2[at : at + size].astype(F32)
 
-    for p in range(12):
+    @pl.loop(0, 12, unroll=4)
+    def _(p):
         for dz in range(3):
             sides[dz, p] = whole[p + 4, pl.ds(3 + dz, 16), :].astype(BF)
 
     quarter[...] = jnp.zeros_like(quarter)
 
-    @pl.loop(0, 10)
+    @pl.loop(0, 10, unroll=5)
     def _(p):
         best = jnp.maximum(whole[2 * p], whole[2 * p + 1])
         best = jnp.maximum(best, pltpu.roll(best, 448, 1))
@@ -319,31 +359,30 @@
                 ups[dz, 2 * p, :, 128 * t : 128 * t + 128] = rows
                 ups[dz, 2 * p + 1, :, 128 * t : 128 * t + 128] = rows
 
-    convolve([ups, sides], [w5u, w5s], acc, 10, 16)
-
-    @pl.loop(0, 10)
+    for g in range(2):
+        acc[0:10, :, 256 * g : 256 * g + 256] = convolve(
+            [(ups, w5u), (sides, w5s)], 10, 16, g
+        )
+
+    @pl.loop(0, 10, unroll=5)
     def _(p):
         x = 8 * q - 1 + p
         inside = row_mask(16, 8 * s - 4, 512) & (x >= 0) & (x < 32)
         value = jnp.where(inside, jnp.maximum(acc[p], 0.0), 0.0)
         for t in range(4):
-            tall[pl.ds(0, 16, stride=2), :] = value[:, 128 * t : 128 * t + 128]
-            tall[pl.ds(1, 16, stride=2), :] = value[:, 128 * t : 128 * t + 128]
-            for dz in range(3):
-                rows = tall[pl.ds(7 + dz, 16), :].astype(BF)
-
-                @pl.when(p > 0)
-                def _():
-                    fine[dz, 2 * p - 1, :, 128 * t : 128 * t + 128] = rows
-
-                @pl.when(p < 9)
-                def _():
-                    fine[dz, 2 * p, :, 128 * t : 128 * t + 128] = rows
-
-    convolve([fine, skip], [w6u, w6s], acc, 16, 16)
-    for i in range(4):
-        for j in range(4):
-            out[i, j] = acc[4 * i : 4 * i + 4, :, 128 * j : 128 * j + 128].astype(BF)
+            tall[t, pl.ds(0, 16, stride=2), :] = value[:, 128 * t : 128 * t + 128]
+            tall[t, pl.ds(1, 16, stride=2), :] = value[:, 128 * t : 128 * t + 128]
+        for dz in range(3):
+            rows = jnp.concatenate([tall[t, pl.ds(7 + dz, 16), :] for t in range(4)], axis=1).astype(BF)
+            fine[dz, 2 * p] = rows
+            fine[dz, 2 * p + 1] = rows
+
+    for g in range(2):
+        total = convolve([(fine.at[:, 1:19], w6u)], 16, 16, g)
+        total = (total + skip_part[:, :, 256 * g : 256 * g + 256]).astype(BF)
+        for i in range(4):
+            for j in range(2):
+                out[i, 2 * g + j] = total[4 * i : 4 * i + 4, :, 128 * j : 128 * j + 128]
 
 
 def call(kernel, outs, scratch=(), flops=0, limit=8):
@@ -379,6 +418,10 @@
     rows = call(to_rows_kernel, shape(16, 4, 16, 128))(features.reshape(512, 256))
     own = lax.all_to_all(rows, PLANE, 0, 0, tiled=True, axis_index_groups=GROUPS)
     own = own.reshape(4, 4, 4, 16, 128)
+    w1, w2, w3, w4 = call(encoder_weights_kernel, (bands,) * 4, limit=LIMITS[0])(
+        conv_one, conv_two, conv_three, conv_four
+    )
+    w5u, w5s, w6u, w6s = call(decoder_weights_kernel, (bands,) * 4, limit=LIMITS[1])(conv_five, conv_six)
     q, s = position()
     x_swaps = [swap_pairs(1, 0, parity) for parity in range(2)]
     z_swaps = [swap_pairs(0, 1, parity) for parity in range(2)]
@@ -392,24 +435,33 @@
     for turn in range(2):
         piece = jnp.where((s + turn) % 2 == 0, broad[..., 8:16, :], broad[..., 0:8, :])
         z_got.append(lax.ppermute(piece, EVERY, z_swaps[turn]))
-    w1, w2, w3, w4 = call(encoder_weights_kernel, (bands,) * 4, limit=LIMITS[0])(
-        conv_one, conv_two, conv_three, conv_four
-    )
+    own_first = call(
+        own_rows_kernel,
+        shape(26, 16, 512),
+        [
+            pltpu.VMEM((32, 16, 512), F32),
+            pltpu.VMEM((3, 28, 16, 512), BF),
+            pltpu.VMEM((26, 16, 512), F32),
+        ],
+        flops=3 << 30,
+        limit=16,
+    )(own, *x_got, w1)
     skip, half_skip = call(
         encoder_kernel,
-        (shape(3, 18, 16, 512), shape(8, 8, 512)),
+        (shape(3, 19, 16, 512), shape(8, 8, 512)),
         [
             pltpu.VMEM((32, 32, 512), F32),
-            pltpu.VMEM((3, 28, 32, 512), BF),
+            pltpu.VMEM((3, 28, 16, 512), BF),
+            pltpu.VMEM((2, 32, 512), F32),
             pltpu.VMEM((3, 26, 32, 512), BF),
             pltpu.VMEM((26, 32, 512), F32),
             pltpu.VMEM((3, 12, 16, 512), BF),
             pltpu.VMEM((3, 10, 16, 512), BF),
-            pltpu.VMEM((32, 128), F32),
+            pltpu.VMEM((4, 4, 32, 128), F32),
         ],
         flops=6 << 30,
         limit=LIMITS[2],
-    )(own, *x_got, *z_got, w1, w2, w3, w4)
+    )(own, *x_got, *z_got, own_first, w1, w2, w3, w4)
     x_got = []
     for turn in range(2):
         start = jnp.where((q + turn) % 2 == 0, 2, 0)
@@ -417,7 +469,9 @@
         x_got.append(lax.ppermute(piece, EVERY, x_swaps[turn]))
     broad = jnp.concatenate([x_got[0], half_skip, x_got[1]], axis=0)
     z_got = [lax.ppermute(broad, EVERY, z_swaps[turn]) for turn in range(2)]
-    w5u, w5s, w6u, w6s = call(decoder_weights_kernel, (bands,) * 4, limit=LIMITS[1])(conv_five, conv_six)
+    skip_part = call(
+        skip_kernel, jax.ShapeDtypeStruct((16, 16, 512), F32), flops=2 << 30, limit=12
+    )(skip, w6s)
     rows = call(
         decoder_kernel,
         shape(4, 4, 4, 16, 128),
@@ -430,14 +484,14 @@
             pltpu.VMEM((32, 128), F32),
             pltpu.VMEM((3, 12, 16, 512), BF),
             pltpu.VMEM((16, 16, 512), F32),
-            pltpu.VMEM((32, 128), F32),
-            pltpu.VMEM((3, 18, 16, 512), BF),
+            pltpu.VMEM((4, 32, 128), F32),
+            pltpu.VMEM((3, 20, 16, 512), BF),
         ],
         flops=2 << 30,
         limit=LIMITS[3],
     )(
-        half_skip, *x_got, *z_got, skip,
-        taps_one, mix_one, taps_two, point_two, w5u, w5s, w6u, w6s,
+        half_skip, *x_got, *z_got, skip_part,
+        taps_one, mix_one, taps_two, point_two, w5u, w5s, w6u,
     )
     back = lax.all_to_all(
         rows.reshape(16, 4, 16, 128), PLANE, 0, 0, tiled=True, axis_index_groups=GROUPS

time: 77.2 us -> 74.2 us (0.961)
  Pallas kernels: 21.6 us -> 20 us
  waiting for transfers between devices: 21.6 us -> 20.1 us
    pallas_call x6 -> x8, Pallas kernels: 21.6 us -> 20 us  [run(): pl.pallas_call(kernel, out_shape=outs, in_specs=[whole] * len(args), out_...]
    ppermute x4, waiting for transfers between devices: 5.68 us -> 4.22 us  [local(): x_got.append(lax.ppermute(piece, EVERY, x_swaps[turn]))]
  transfers between devices with their start and end apart: 9 -> 9, of which waited for: 7 -> 5; matrix products, arithmetic and copies ran while one was open for 0% -> 0% of each run, Pallas kernels for 4% -> 8%
where the time goes in v3:
time: 74.2 us; the launch traced here: 73.5 us
  waiting for transfers between devices  20.1 us (27%)
  Pallas kernels  20 us (27%)
  starting transfers between devices  18.4 us (25%)
  blocking collectives  12.3 us (17%)
  local copies, waits for them, and re-layouts  2.05 us (3%)
    pallas_call x8, Pallas kernels, run(): pl.pallas_call(kernel, out_shape=outs, in_specs=[whole] * len(args), out_...  20 us
    all_to_all x1, blocking collectives, local(): lax.all_to_all(rows.reshape(16, 4, 16, 128), PLANE, 0, 0, tiled=True, axi...  12.3 us
    ppermute x4, starting transfers between devices, local(): x_got.append(lax.ppermute(piece, EVERY, x_swaps[turn]))  8.56 us
    all_to_all x1, waiting for transfers between devices, local(): lax.all_to_all(rows, PLANE, 0, 0, tiled=True, axis_index_groups=GROUPS)  7.71 us
    all_to_all x1, starting transfers between devices, local(): lax.all_to_all(rows, PLANE, 0, 0, tiled=True, axis_index_groups=GROUPS)  5.76 us
    ppermute x4, waiting for transfers between devices, local(): x_got.append(lax.ppermute(piece, EVERY, x_swaps[turn]))  4.22 us
    ppermute x2, waiting for transfers between devices, local(): z_got.append(lax.ppermute(piece, EVERY, z_swaps[turn]))  4.19 us
    ppermute x2, waiting for transfers between devices, local(): z_got = [lax.ppermute(broad, EVERY, z_swaps[turn]) for turn in range(2)]  3.97 us
  transfers between devices with their start and end apart: 9, of which 5 were waited for; matrix products, arithmetic and copies ran while one was open for 0% of the time, Pallas kernels for 8%

profile of v3, /device:TPU:72, one launch (start us, length us, event | category | flops | bytes accessed | tf_op | source)
XLA Modules:
  0.0 73.5 jit_solution(6860186405958538216)
XLA Ops:
  0.0 1.1 %reshape.12.cells_ref = bf16[512,256]{1,0:T(8,128)(2,1)S(1)} reshape(bf16[32,4,4,256]{3,2,1,0:T(4,128)(2,1)} %param.11) | data formatting | bytes 524288 | tf_op jit(solution)/shard_map/reshape | solution.py:418
  1.1 1.0 %shard_map.109 = bf16[16,4,16,128]{3,2,1,0:T(8,128)(2,1)} custom-call(bf16[512,256]{1,0:T(8,128)(2,1)S(1)} %reshape.12.cells_ref), custom_call_target="tpu_custom_call" | custom-call | bytes 4194304 | tf_op jit(solution)/shard_map/pallas_call | solution.py:392
  2.1 5.8 %all-to-all-start = ((bf16[16,4,16,128]{3,2,1,0:T(8,128)(2,1)}), bf16[16,4,16,128]{3,2,1,0:T(8,128)(2,1)S(1)}, u32[]{:S(2)}, u32[]{:S(2)}) async-start(bf16[16,4,16,128]{3,2,1,0:T(8,128)(2,1)} %shard_map.109), calls=%async_computation | async-start | bytes 524288 | tf_op jit(solution)/shard_map/all_to_all | solution.py:419
  8.0 7.7 %all-to-all-done = bf16[16,4,16,128]{3,2,1,0:T(8,128)(2,1)S(1)} async-done(((bf16[16,4,16,128]{3,2,1,0:T(8,128)(2,1)}), bf16[16,4,16,128]{3,2,1,0:T(8,128)(2,1)S(1)}, u32[]{:S(2)}, u32[]{:S(2)}) %all-to-all-start) | async-done | bytes 262176 | tf_op jit(solution)/shard_map/all_to_all | solution.py:419
  15.7 0.5 collective-permute-start
  16.2 4.3 %collective-permute-start.1 = (bf16[2,4,4,16,128]{4,3,2,1,0:T(8,128)(2,1)S(1)}, bf16[2,4,4,16,128]{4,3,2,1,0:T(8,128)(2,1)S(1)}, u32[]{:S(2)}, u32[]{:S(2)}) collective-permute-start(bf16[2,4,4,16,128]{4,3,2,1,0:T(8,128)(2,1)S(1)} %get-tuple-element.27), channel_id=1, source_target_pairs={{64,128},{128,64},{80,144},{144,80},{84,148},{148,84},{68,132},{13... | collective-permute-start | bytes 393224 | tf_op jit(solution)/shard_map/ppermute | solution.py:432
  20.7 1.4 %shard_map.110 = (bf16[9,512,256]{2,1,0:T(8,128)(2,1)S(1)}, bf16[9,512,256]{2,1,0:T(8,128)(2,1)S(1)}, bf16[9,512,256]{2,1,0:T(8,128)(2,1)S(1)}, bf16[9,512,256]{2,1,0:T(8,128)(2,1)S(1)}) custom-call(bf16[32,864]{1,0:T(8,128)(2,1)S(1)} %copy-done.4, bf16[32,864]{1,0:T(8,128)(2,1)S(1)} %copy-done.5, bf16[64,864]{1,0:T(8,128)(2,1)S(1)} %copy-done.3, ...), custom_call_target="tpu_custom_call" | custom-call | bytes 4194304 | tf_op jit(solution)/shard_map/pallas_call | solution.py:392
  22.1 0.0 collective-permute-done.x1
  22.1 1.9 %collective-permute-done.1.x2 = bf16[2,4,4,16,128]{4,3,2,1,0:T(8,128)(2,1)S(1)} collective-permute-done((bf16[2,4,4,16,128]{4,3,2,1,0:T(8,128)(2,1)S(1)}, bf16[2,4,4,16,128]{4,3,2,1,0:T(8,128)(2,1)S(1)}, u32[]{:S(2)}, u32[]{:S(2)}) %collective-permute-start.1) | collective-permute-done | bytes 131104 | tf_op jit(solution)/shard_map/ppermute | solution.py:432
  24.0 0.1 pad_maximum_fusion
  24.1 0.1 collective-permute-start.2
  24.2 1.9 %collective-permute-start.3 = (bf16[8,4,4,8,128]{4,3,2,1,0:T(8,128)(2,1)S(1)}, bf16[8,4,4,8,128]{4,3,2,1,0:T(8,128)(2,1)S(1)}, u32[]{:S(2)}, u32[]{:S(2)}) collective-permute-start(bf16[8,4,4,8,128]{4,3,2,1,0:T(8,128)(2,1)S(1)} %get-tuple-element.25), channel_id=1, source_target_pairs={{16,20},{20,16},{4,8},{8,4},{24,28},{28,24},{12,44},{44,12},{60,56... | collective-permute-start | bytes 786440 | tf_op jit(solution)/shard_map/ppermute | solution.py:437
  26.1 2.1 %shard_map.111.own_first = bf16[26,16,512]{2,1,0:T(8,128)(2,1)S(1)} custom-call(bf16[4,4,4,16,128]{4,3,2,1,0:T(8,128)(2,1)S(1)} %bitcast.6, bf16[2,4,4,16,128]{4,3,2,1,0:T(8,128)(2,1)S(1)} %collective-permute-done.x1, bf16[2,4,4,16,128]{4,3,2,1,0:T(8,128)(2,1)S(1)} %collective-permute-done.1.x2, bf16[9,512,256]{2,1,0:T(8,128)(2,1)S(1)} %get-tuple-element.15.w1), custom_call_target="tpu_custom_call" | custom-call | flops 3221225472 | bytes 4194304 | tf_op jit(solution)/shard_map/pallas_call | solution.py:392
  28.3 0.0 collective-permute-done.2.z1
  28.3 4.2 %collective-permute-done.3.z2 = bf16[8,4,4,8,128]{4,3,2,1,0:T(8,128)(2,1)S(1)} collective-permute-done((bf16[8,4,4,8,128]{4,3,2,1,0:T(8,128)(2,1)S(1)}, bf16[8,4,4,8,128]{4,3,2,1,0:T(8,128)(2,1)S(1)}, u32[]{:S(2)}, u32[]{:S(2)}) %collective-permute-start.3) | collective-permute-done | bytes 262176 | tf_op jit(solution)/shard_map/ppermute | solution.py:437
  32.5 0.0 copy-start.2
  32.5 8.1 %shard_map.112 = (bf16[3,19,16,512]{3,2,1,0:T(8,128)(2,1)S(1)}, bf16[8,8,512]{2,1,0:T(8,128)(2,1)S(1)}) custom-call(bf16[4,4,4,16,128]{4,3,2,1,0:T(8,128)(2,1)S(1)} %bitcast.7, bf16[2,4,4,16,128]{4,3,2,1,0:T(8,128)(2,1)S(1)} %collective-permute-done.x1, bf16[2,4,4,16,128]{4,3,2,1,0:T(8,128)(2,1)S(1)} %collective-permute-done.1.x2, ...), custom_call_target="tpu_custom_call" | custom-call | flops 6442450944 | bytes 4194304 | tf_op jit(solution)/shard_map/pallas_call | solution.py:392
  40.6 0.1 collective-permute-start.4
  40.8 0.1 copy.12
  40.9 1.6 %shard_map.113 = (bf16[9,512,256]{2,1,0:T(8,128)(2,1)S(1)}, bf16[9,512,256]{2,1,0:T(8,128)(2,1)S(1)}, bf16[9,512,256]{2,1,0:T(8,128)(2,1)S(1)}, bf16[9,512,256]{2,1,0:T(8,128)(2,1)S(1)}) custom-call(bf16[64,5184]{1,0:T(8,128)(2,1)S(1)} %copy-done, bf16[32,2592]{1,0:T(8,128)(2,1)S(1)} %copy-done.2), custom_call_target="tpu_custom_call" | custom-call | bytes 4194304 | tf_op jit(solution)/shard_map/pallas_call | solution.py:392
  42.5 3.6 %collective-permute-start.5 = (bf16[6,8,512]{2,1,0:T(8,128)(2,1)S(1)}, bf16[6,8,512]{2,1,0:T(8,128)(2,1)S(1)}, u32[]{:S(2)}, u32[]{:S(2)}) collective-permute-start(bf16[6,8,512]{2,1,0:T(8,128)(2,1)S(1)} %get-tuple-element.29), channel_id=1, source_target_pairs={{64,128},{128,64},{80,144},{144,80},{84,148},{148,84},{68,132},{13... | collective-permute-start | bytes 147464 | tf_op jit(solution)/shard_map/ppermute | solution.py:469
  46.1 0.0 collective-permute-done.4.x1
  46.2 2.3 %collective-permute-done.5.x2 = bf16[6,8,512]{2,1,0:T(8,128)(2,1)S(1)} collective-permute-done((bf16[6,8,512]{2,1,0:T(8,128)(2,1)S(1)}, bf16[6,8,512]{2,1,0:T(8,128)(2,1)S(1)}, u32[]{:S(2)}, u32[]{:S(2)}) %collective-permute-start.5) | collective-permute-done | bytes 49184 | tf_op jit(solution)/shard_map/ppermute | solution.py:469
  48.5 2.1 %collective-permute-start.7 = (bf16[20,8,512]{2,1,0:T(8,128)(2,1)S(1)}, bf16[20,8,512]{2,1,0:T(8,128)(2,1)S(1)}, u32[]{:S(2)}, u32[]{:S(2)}) collective-permute-start(bf16[20,8,512]{2,1,0:T(8,128)(2,1)S(1)} %constant_dynamic-update-slice_fusion), channel_id=1, source_target_pairs={{16,20},{20,16},{4,8},{8,4},{24,28},{28,24},{12,44},{44,12},{60,56... | collective-permute-start | bytes 491528 | tf_op jit(solution)/shard_map/ppermute | solution.py:471
  50.6 0.0 copy-start.6
  50.6 1.1 %shard_map.114.skip_part = f32[16,16,512]{2,1,0:T(8,128)S(1)} custom-call(bf16[3,19,16,512]{3,2,1,0:T(8,128)(2,1)S(1)} %get-tuple-element.20.skip, bf16[9,512,256]{2,1,0:T(8,128)(2,1)S(1)} %get-tuple-element.21.w6s), custom_call_target="tpu_custom_call" | custom-call | flops 2147483648 | bytes 4194304 | tf_op jit(solution)/shard_map/pallas_call | solution.py:392
  51.7 0.0 collective-permute-done.6.z1
  51.7 4.0 %collective-permute-done.7.z2 = bf16[20,8,512]{2,1,0:T(8,128)(2,1)S(1)} collective-permute-done((bf16[20,8,512]{2,1,0:T(8,128)(2,1)S(1)}, bf16[20,8,512]{2,1,0:T(8,128)(2,1)S(1)}, u32[]{:S(2)}, u32[]{:S(2)}) %collective-permute-start.7) | collective-permute-done | bytes 163872 | tf_op jit(solution)/shard_map/ppermute | solution.py:471
  55.7 4.4 %shard_map.115 = bf16[4,4,4,16,128]{4,3,2,1,0:T(8,128)(2,1)S(1)} custom-call(bf16[8,8,512]{2,1,0:T(8,128)(2,1)S(1)} %get-tuple-element.19.own, bf16[6,8,512]{2,1,0:T(8,128)(2,1)S(1)} %collective-permute-done.4.x1, bf16[6,8,512]{2,1,0:T(8,128)(2,1)S(1)} %collective-permute-done.5.x2, bf16[20,8,512]{2,1,0:T(8,128)(2,1)S(1)} %collective-permute-done.6.z1, ...), custom_call_target="tpu_custom_call" | custom-call | flops 2147483648 | bytes 4194304 | tf_op jit(solution)/shard_map/pallas_call | solution.py:392
  60.1 12.3 %all_to_all.10.rows_ref = bf16[16,4,16,128]{3,2,1,0:T(8,128)(2,1)S(1)} all-to-all(bf16[16,4,16,128]{3,2,1,0:T(8,128)(2,1)S(1)} %bitcast.8), channel_id=1, replica_groups={{0,4,8,12,16,20,24,28,32,36,40,44,48,52,56,60},{64,68,72,76,80,84,88,92..., dimensions={0} | all-to-all | bytes 524288 | tf_op jit(solution)/shard_map/all_to_all | solution.py:496
  72.4 0.3 shard_map.116
  72.7 0.8 %reshape.15 = bf16[32,4,4,256]{3,2,1,0:T(4,128)(2,1)} reshape(bf16[512,256]{1,0:T(8,128)(2,1)S(1)} %shard_map.116) | data formatting | bytes 524288 | tf_op jit(solution)/shard_map/reshape | solution.py:499
  (27 shorter events, 0.1 us)
Async XLA Ops:
  0.0 20.6 %copy-start.4 = (bf16[32,864]{1,0:T(8,128)(2,1)S(1)}, bf16[32,864]{1,0:T(8,128)(2,1)}, u32[]{:S(2)}) copy-start(bf16[32,864]{1,0:T(8,128)(2,1)} %w1.1) | copy-start | bytes 165892
  0.0 20.6 %copy-start.5 = (bf16[32,864]{1,0:T(8,128)(2,1)S(1)}, bf16[32,864]{1,0:T(8,128)(2,1)}, u32[]{:S(2)}) copy-start(bf16[32,864]{1,0:T(8,128)(2,1)} %w2.1) | copy-start | bytes 165892
  0.0 20.6 %copy-start.3 = (bf16[64,864]{1,0:T(8,128)(2,1)S(1)}, bf16[64,864]{1,0:T(8,128)(2,1)}, u32[]{:S(2)}) copy-start(bf16[64,864]{1,0:T(8,128)(2,1)} %w3.1) | copy-start | bytes 331780
  0.0 20.7 %copy-start.1 = (bf16[64,1728]{1,0:T(8,128)(2,1)S(1)}, bf16[64,1728]{1,0:T(8,128)(2,1)}, u32[]{:S(2)}) copy-start(bf16[64,1728]{1,0:T(8,128)(2,1)} %w4.1) | copy-start | bytes 663556
  2.1 13.5 %all-to-all-start = ((bf16[16,4,16,128]{3,2,1,0:T(8,128)(2,1)}), bf16[16,4,16,128]{3,2,1,0:T(8,128)(2,1)S(1)}, u32[]{:S(2)}, u32[]{:S(2)}) async-start(bf16[16,4,16,128]{3,2,1,0:T(8,128)(2,1)} %shard_map.109), calls=%async_computation | async-start | bytes 524288 | tf_op jit(solution)/shard_map/all_to_all | solution.py:419
  15.7 6.4 %collective-permute-start = (bf16[2,4,4,16,128]{4,3,2,1,0:T(8,128)(2,1)S(1)}, bf16[2,4,4,16,128]{4,3,2,1,0:T(8,128)(2,1)S(1)}, u32[]{:S(2)}, u32[]{:S(2)}) collective-permute-start(bf16[2,4,4,16,128]{4,3,2,1,0:T(8,128)(2,1)S(1)} %get-tuple-element.28), channel_id=1, source_target_pairs={{0,64},{64,0},{16,80},{80,16},{20,84},{84,20},{4,68},{68,4},{8,72}... | collective-permute-start | bytes 393224 | tf_op jit(solution)/shard_map/ppermute | solution.py:432
  16.2 7.8 %collective-permute-start.1 = (bf16[2,4,4,16,128]{4,3,2,1,0:T(8,128)(2,1)S(1)}, bf16[2,4,4,16,128]{4,3,2,1,0:T(8,128)(2,1)S(1)}, u32[]{:S(2)}, u32[]{:S(2)}) collective-permute-start(bf16[2,4,4,16,128]{4,3,2,1,0:T(8,128)(2,1)S(1)} %get-tuple-element.27), channel_id=1, source_target_pairs={{64,128},{128,64},{80,144},{144,80},{84,148},{148,84},{68,132},{13... | collective-permute-start | bytes 393224 | tf_op jit(solution)/shard_map/ppermute | solution.py:432
  24.1 4.2 %collective-permute-start.2 = (bf16[8,4,4,8,128]{4,3,2,1,0:T(8,128)(2,1)S(1)}, bf16[8,4,4,8,128]{4,3,2,1,0:T(8,128)(2,1)S(1)}, u32[]{:S(2)}, u32[]{:S(2)}) collective-permute-start(bf16[8,4,4,8,128]{4,3,2,1,0:T(8,128)(2,1)S(1)} %get-tuple-element.26), channel_id=1, source_target_pairs={{0,16},{16,0},{20,4},{4,20},{8,24},{24,8},{28,12},{12,28},{44,60},... | collective-permute-start | bytes 786440 | tf_op jit(solution)/shard_map/ppermute | solution.py:437
  24.2 8.3 %collective-permute-start.3 = (bf16[8,4,4,8,128]{4,3,2,1,0:T(8,128)(2,1)S(1)}, bf16[8,4,4,8,128]{4,3,2,1,0:T(8,128)(2,1)S(1)}, u32[]{:S(2)}, u32[]{:S(2)}) collective-permute-start(bf16[8,4,4,8,128]{4,3,2,1,0:T(8,128)(2,1)S(1)} %get-tuple-element.25), channel_id=1, source_target_pairs={{16,20},{20,16},{4,8},{8,4},{24,28},{28,24},{12,44},{44,12},{60,56... | collective-permute-start | bytes 786440 | tf_op jit(solution)/shard_map/ppermute | solution.py:437
  32.5 8.2 %copy-start.8 = (bf16[128,27]{0,1:T(8,128)(2,1)S(1)}, bf16[128,27]{0,1:T(8,128)(2,1)}, u32[]{:S(2)}) copy-start(bf16[128,27]{0,1:T(8,128)(2,1)} %param.18) | copy-start | bytes 20740
  32.5 8.3 %copy-start.9 = (bf16[64,27]{0,1:T(8,128)(2,1)S(1)}, bf16[64,27]{0,1:T(8,128)(2,1)}, u32[]{:S(2)}) copy-start(bf16[64,27]{0,1:T(8,128)(2,1)} %param.16) | copy-start | bytes 10372
  32.5 8.3 %copy-start.7 = (bf16[128,64]{0,1:T(8,128)(2,1)S(1)}, bf16[128,64]{0,1:T(8,128)(2,1)}, u32[]{:S(2)}) copy-start(bf16[128,64]{0,1:T(8,128)(2,1)} %param.17) | copy-start | bytes 49156
  32.5 8.4 %copy-start = (bf16[64,5184]{1,0:T(8,128)(2,1)S(1)}, bf16[64,5184]{1,0:T(8,128)(2,1)}, u32[]{:S(2)}) copy-start(bf16[64,5184]{1,0:T(8,128)(2,1)} %w5.1) | copy-start | bytes 1990660
  32.5 8.4 %copy-start.2 = (bf16[32,2592]{1,0:T(8,128)(2,1)S(1)}, bf16[32,2592]{1,0:T(8,128)(2,1)}, u32[]{:S(2)}) copy-start(bf16[32,2592]{1,0:T(8,128)(2,1)} %w6.1) | copy-start | bytes 497668
  40.6 5.5 %collective-permute-start.4 = (bf16[6,8,512]{2,1,0:T(8,128)(2,1)S(1)}, bf16[6,8,512]{2,1,0:T(8,128)(2,1)S(1)}, u32[]{:S(2)}, u32[]{:S(2)}) collective-permute-start(bf16[6,8,512]{2,1,0:T(8,128)(2,1)S(1)} %get-tuple-element.30), channel_id=1, source_target_pairs={{0,64},{64,0},{16,80},{80,16},{20,84},{84,20},{4,68},{68,4},{8,72}... | collective-permute-start | bytes 147464 | tf_op jit(solution)/shard_map/ppermute | solution.py:469
  42.5 6.0 %collective-permute-start.5 = (bf16[6,8,512]{2,1,0:T(8,128)(2,1)S(1)}, bf16[6,8,512]{2,1,0:T(8,128)(2,1)S(1)}, u32[]{:S(2)}, u32[]{:S(2)}) collective-permute-start(bf16[6,8,512]{2,1,0:T(8,128)(2,1)S(1)} %get-tuple-element.29), channel_id=1, source_target_pairs={{64,128},{128,64},{80,144},{144,80},{84,148},{148,84},{68,132},{13... | collective-permute-start | bytes 147464 | tf_op jit(solution)/shard_map/ppermute | solution.py:469
  48.5 3.2 %collective-permute-start.6 = (bf16[20,8,512]{2,1,0:T(8,128)(2,1)S(1)}, bf16[20,8,512]{2,1,0:T(8,128)(2,1)S(1)}, u32[]{:S(2)}, u32[]{:S(2)}) collective-permute-start(bf16[20,8,512]{2,1,0:T(8,128)(2,1)S(1)} %constant_dynamic-update-slice_fusion), channel_id=1, source_target_pairs={{0,16},{16,0},{20,4},{4,20},{8,24},{24,8},{28,12},{12,28},{44,60},... | collective-permute-start | bytes 491528 | tf_op jit(solution)/shard_map/ppermute | solution.py:471
  48.5 7.2 %collective-permute-start.7 = (bf16[20,8,512]{2,1,0:T(8,128)(2,1)S(1)}, bf16[20,8,512]{2,1,0:T(8,128)(2,1)S(1)}, u32[]{:S(2)}, u32[]{:S(2)}) collective-permute-start(bf16[20,8,512]{2,1,0:T(8,128)(2,1)S(1)} %constant_dynamic-update-slice_fusion), channel_id=1, source_target_pairs={{16,20},{20,16},{4,8},{8,4},{24,28},{28,24},{12,44},{44,12},{60,56... | collective-permute-start | bytes 491528 | tf_op jit(solution)/shard_map/ppermute | solution.py:471
  50.6 5.1 %copy-start.6 = (bf16[128,128]{1,0:T(8,128)(2,1)S(1)}, bf16[128,128]{1,0:T(8,128)(2,1)}, u32[]{:S(2)}) copy-start(bf16[128,128]{1,0:T(8,128)(2,1)} %p2.1) | copy-start | bytes 98308

commit v4 on v3

--- a/solution.py
+++ b/solution.py
@@ -4,6 +4,7 @@
 from jax.experimental import pallas as pl
 from jax.experimental.pallas import tpu as pltpu
 from jax.sharding import PartitionSpec as P
+
 
 BF = jnp.bfloat16
 F32 = jnp.float32
@@ -45,30 +46,32 @@
     return gx // 4, gz * 16 + slab_at(gx // 2 % 2, gy, gx % 2)
 
 
-def one_hot_order():
-    row = lax.broadcasted_iota(jnp.int32, (512, 512), 0)
-    lane = lax.broadcasted_iota(jnp.int32, (512, 512), 1)
-    target = (row % 16) * 32 + row // 16
-    return jnp.where(target == lane, 1.0, 0.0).astype(BF)
+def identity():
+    row = lax.broadcasted_iota(jnp.int32, (128, 128), 0)
+    lane = lax.broadcasted_iota(jnp.int32, (128, 128), 1)
+    return jnp.where(row == lane, 1.0, 0.0).astype(BF)
 
 
 def to_rows_kernel(cells_ref, out_ref):
-    turned = lax.dot_general(
-        cells_ref[...], one_hot_order(), (((0,), (0,)), ((), ())), preferred_element_type=F32
-    ).astype(BF)
-    for rank, slab in enumerate(SLABS):
-        for x in range(4):
-            out_ref[rank, x] = turned[16 * slab : 16 * slab + 16, 128 * x : 128 * x + 128]
+    same = identity()
+    for x in range(4):
+        cells = jnp.concatenate([cells_ref[:, x, y, :] for y in range(4)], axis=0)
+        turned = lax.dot_general(
+            cells, same, (((0,), (0,)), ((), ())), preferred_element_type=F32
+        ).astype(BF)
+        for rank, slab in enumerate(SLABS):
+            out_ref[rank, x] = turned[16 * slab : 16 * slab + 16]
 
 
 def from_rows_kernel(rows_ref, out_ref):
-    columns = [
-        jnp.concatenate([rows_ref[SLABS.index(slab), x] for slab in range(16)], axis=0) for x in range(4)
-    ]
-    turned = jnp.concatenate(columns, axis=1)
-    out_ref[...] = lax.dot_general(
-        one_hot_order(), turned, (((1,), (1,)), ((), ())), preferred_element_type=F32
-    ).astype(BF)
+    same = identity()
+    for x in range(4):
+        rows = jnp.concatenate([rows_ref[SLABS.index(slab), x] for slab in range(16)], axis=0)
+        turned = lax.dot_general(
+            same, rows, (((1,), (1,)), ((), ())), preferred_element_type=F32
+        ).astype(BF)
+        for y in range(4):
+            out_ref[:, x, y, :] = turned[32 * y : 32 * y + 32]
 
 
 def band(spread, out_ref, stride, first, used, lanes_in, lanes_out, grown=False):
@@ -127,13 +130,18 @@
     band(spread_lanes(w4[...], 64), o4, 64, 0, 64, 64, 64)
 
 
-def decoder_weights_kernel(w5, w6, o5u, o5s, o6u, o6s):
+def decoder_weights_kernel(w5, w6, d1, d2, o5u, o5s, o6u, o6s, taps_one, taps_two):
     wide = spread_lanes(w5[...], 64)
     band(wide, o5u, 192, 0, 128, 128, 64, grown=True)
     band(wide, o5s, 192, 128, 64, 64, 64)
     fine = spread_lanes(w6[...], 32)
     band(fine, o6u, 96, 0, 64, 64, 32, grown=True)
     band(fine, o6s, 96, 64, 32, 32, 32)
+    for taps, weight in ((taps_one, d1), (taps_two, d2)):
+        same = identity()[: weight.shape[0]]
+        taps[...] = lax.dot_general(
+            weight[...], same, (((0,), (0,)), ((), ())), preferred_element_type=F32
+        )
 
 
 def convolve(terms, planes, rows, g):
@@ -166,23 +174,67 @@
     dest[2, plane] = pltpu.roll(value, value.shape[0] - 1, 0)[keep].astype(BF)
 
 
+def pick_x_kernel(own, out_1, out_2):
+    q, _ = position()
+
+    def fill(out, start):
+        for p in range(6):
+            out[p] = own[(start + p) // 4, :, (start + p) % 4]
+
+    @pl.when(q % 2 == 0)
+    def _():
+        fill(out_1, 10)
+        fill(out_2, 0)
+
+    @pl.when(q % 2 == 1)
+    def _():
+        fill(out_1, 0)
+        fill(out_2, 10)
+
+
+def pick_z_kernel(own, x1, x2, out_1, out_2):
+    _, s = position()
+
+    def fill(out, rows):
+        out[0:6] = x1[:, :, rows]
+        for x in range(16):
+            out[6 + x] = own[x // 4, :, x % 4, rows]
+        out[22:28] = x2[:, :, rows]
+
+    @pl.when(s % 2 == 0)
+    def _():
+        fill(out_1, slice(8, 16))
+        fill(out_2, slice(0, 8))
+
+    @pl.when(s % 2 == 1)
+    def _():
+        fill(out_1, slice(0, 8))
+        fill(out_2, slice(8, 16))
+
+
+def join_kernel(own, x1, x2, out):
+    out[0:6] = x1[...]
+    out[6:14] = own[...]
+    out[14:20] = x2[...]
+
+
 def x_blocks(own, x1, x2, q):
-    plane_1 = 24 * (1 - q % 2)
-    plane_2 = 24 - plane_1
-    starts = [plane_1, plane_1 + 4, 8, 12, 16, 20, plane_2, plane_2 + 4]
-    sources = [(x1, 0), (x1, 1), (own, 0), (own, 1), (own, 2), (own, 3), (x2, 0), (x2, 1)]
-    return [(pl.ds(start, 4), source, i) for start, (source, i) in zip(starts, sources)]
-
-
-def own_rows_kernel(own, x1, x2, w1, out, field, turned, acc):
+    plane_1 = 22 * (1 - q % 2)
+    blocks = [(pl.ds(plane_1, 6), lambda j: x1[:, j], 0), (pl.ds(22 - plane_1, 6), lambda j: x2[:, j], 22)]
+    for i in range(4):
+        blocks.append((slice(6 + 4 * i, 10 + 4 * i), lambda j, i=i: own[i, j], 6 + 4 * i))
+    return blocks
+
+
+def own_rows_kernel(own, x1, x2, w1, w2, own_first, own_skip, field, turned, acc):
     q, _ = position()
-    for planes, source, i in x_blocks(own, x1, x2, q):
+    for planes, source, _ in x_blocks(own, x1, x2, q):
         for j in range(4):
-            field[planes, :, 128 * j : 128 * j + 128] = source[i, j].astype(F32)
+            field[planes, :, 128 * j : 128 * j + 128] = source(j).astype(F32)
 
     @pl.loop(0, 28, unroll=4)
     def _(p):
-        store_turned(turned, p, field[p + 2])
+        store_turned(turned, p, field[p])
 
     for g in range(2):
         acc[:, :, 256 * g : 256 * g + 256] = convolve([(turned, w1)], 26, 16, g)
@@ -190,53 +242,77 @@
     @pl.loop(0, 26, unroll=2)
     def _(p):
         x = 16 * q - 5 + p
-        out[p] = jnp.where((x >= 0) & (x < 64), jnp.maximum(acc[p], 0.0), 0.0).astype(BF)
+        value = jnp.where((x >= 0) & (x < 64), jnp.maximum(acc[p], 0.0), 0.0)
+        own_first[p] = value.astype(BF)
+        store_turned(turned, p, value)
+
+    for g in range(2):
+        acc[0:24, :, 256 * g : 256 * g + 256] = convolve([(turned, w2)], 24, 16, g)
+
+    @pl.loop(0, 24, unroll=4)
+    def _(p):
+        x = 16 * q - 4 + p
+        own_skip[p] = jnp.where((x >= 0) & (x < 64), jnp.maximum(acc[p], 0.0), 0.0).astype(BF)
+
+
+def rim_rows_inside(low, high):
+    row = lax.broadcasted_iota(jnp.int32, (16, 512), 0)
+    row = jnp.where(row < 8, row + low, row + (high - 8))
+    return (row >= 0) & (row < 1024)
 
 
 def encoder_kernel(
-    own, x1, x2, z1, z2, own_first, w1, w2, w3, w4,
-    skip_out, half_out, field, turned, full, first, acc, half, mid, pooled,
+    own, x1, x2, z1, z2, own_first, own_skip, w1, w2, w3, w4,
+    skip_out, half_out, half_1, half_2, field, turned, full, acc, half, mid, pooled,
 ):
     q, s = position()
     x0, z0 = 16 * q, 16 * s
     row_1 = pl.multiple_of(24 * (1 - s % 2), 8)
     row_2 = pl.multiple_of(24 * (s % 2), 8)
-    for at, (planes, source, i) in enumerate(x_blocks(own, x1, x2, q)):
+    for planes, source, at in x_blocks(own, x1, x2, q):
         for j in range(4):
             lanes = slice(128 * j, 128 * j + 128)
-            field[planes, 8:24, lanes] = source[i, j].astype(F32)
-            field[planes, pl.ds(row_1, 8), lanes] = z1[at, j].astype(F32)
-            field[planes, pl.ds(row_2, 8), lanes] = z2[at, j].astype(F32)
+            cells = source(j)
+            count = cells.shape[0]
+            field[planes, 8:24, lanes] = cells.astype(F32)
+            field[planes, pl.ds(row_1, 8), lanes] = z1[at : at + count, j].astype(F32)
+            field[planes, pl.ds(row_2, 8), lanes] = z2[at : at + count, j].astype(F32)
 
     @pl.loop(0, 28, unroll=4)
     def _(p):
         for dz in range(3):
             turned[dz, p] = jnp.concatenate(
-                [field[p + 2, pl.ds(dz, 8), :], field[p + 2, pl.ds(22 + dz, 8), :]], axis=0
+                [field[p, pl.ds(dz, 8), :], field[p, pl.ds(22 + dz, 8), :]], axis=0
             ).astype(BF)
 
     for g in range(2):
-        acc[0:26, 0:16, 256 * g : 256 * g + 256] = convolve([(turned, w1)], 26, 16, g)
-
-    for slot in range(2):
+        acc[:, :, 256 * g : 256 * g + 256] = convolve([(turned, w1)], 26, 16, g)
+
+    for slot in range(4):
         full[slot, 0:8] = jnp.zeros((8, 512), F32)
         full[slot, 24:32] = jnp.zeros((8, 512), F32)
-    row = lax.broadcasted_iota(jnp.int32, (16, 512), 0)
-    row = jnp.where(row < 8, row + (z0 - 7), row + (z0 + 7))
-    row_inside = (row >= 0) & (row < 1024)
+    inside = rim_rows_inside(z0 - 7, z0 + 15)
 
     @pl.loop(0, 26, unroll=2)
     def _(p):
         x = x0 - 5 + p
-        value = jnp.where(row_inside & (x >= 0) & (x < 64), jnp.maximum(acc[p, 0:16], 0.0), 0.0)
+        value = jnp.where(inside & (x >= 0) & (x < 64), jnp.maximum(acc[p], 0.0), 0.0)
         slot = p % 2
         full[slot, 8:24] = own_first[p].astype(F32)
         full[slot, 1:9] = value[0:8]
         full[slot, 23:31] = value[8:16]
-        store_turned(first, p, full[slot])
-
-    for g in range(2):
-        acc[0:24, :, 256 * g : 256 * g + 256] = convolve([(first, w2)], 24, 32, g)
+        for dz in range(3):
+            turned[dz, p] = jnp.concatenate(
+                [full[slot, pl.ds(1 + dz, 8), :], full[slot, pl.ds(21 + dz, 8), :]], axis=0
+            ).astype(BF)
+
+    for g in range(2):
+        acc[0:24, :, 256 * g : 256 * g + 256] = convolve([(turned, w2)], 24, 16, g)
+
+    for slot in range(4):
+        full[slot, 0:8] = jnp.zeros((8, 512), F32)
+        full[slot, 24:32] = jnp.zeros((8, 512), F32)
+    inside_two = rim_rows_inside(z0 - 6, z0 + 14)
 
     @pl.loop(0, 12, unroll=4)
     def _(h):
@@ -244,8 +320,12 @@
         for b in range(2):
             p = 2 * h + b
             x = x0 - 4 + p
-            inside = row_mask(32, z0 - 8, 1024) & (x >= 0) & (x < 64)
-            value = jnp.where(inside, jnp.maximum(acc[p], 0.0), 0.0)
+            rim = jnp.where(inside_two & (x >= 0) & (x < 64), jnp.maximum(acc[p], 0.0), 0.0)
+            slot = 2 * (h % 2) + b
+            full[slot, 8:24] = own_skip[p].astype(F32)
+            full[slot, 2:10] = rim[0:8]
+            full[slot, 22:30] = rim[8:16]
+            value = full[slot]
             store_turned(skip_out, jnp.where((p >= 3) & (p < 21), p - 3, 18), value, slice(8, 24))
             best = value if best is None else jnp.maximum(best, value)
         best = jnp.maximum(best, pltpu.roll(best, 480, 1))
@@ -271,6 +351,16 @@
     for g in range(2):
         acc[0:8, 0:16, 256 * g : 256 * g + 256] = convolve([(mid, w4)], 8, 16, g)
     half_out[...] = jnp.maximum(acc[0:8, 4:12, :], 0.0).astype(BF)
+
+    @pl.when(q % 2 == 0)
+    def _():
+        half_1[...] = half_out[2:8]
+        half_2[...] = half_out[0:6]
+
+    @pl.when(q % 2 == 1)
+    def _():
+        half_1[...] = half_out[0:6]
+        half_2[...] = half_out[2:8]
 
 
 def skip_kernel(skip, w6s, out):
@@ -336,7 +426,7 @@
     inside = (plane >= 0) & (plane < 16) & (row >= 0) & (row < 256)
     for t in range(4):
         value = lax.dot_general(
-            spread[t], p1[...], (((1,), (1,)), ((), ())), preferred_element_type=F32
+            spread[t][:, :64], p1[...], (((1,), (1,)), ((), ())), preferred_element_type=F32
         ).reshape(8, 8, 128)
         value = jnp.where(inside, jnp.maximum(value, 0.0), 0.0)
         mixed[:, 0:8, 128 * t : 128 * t + 128] = value.astype(BF).astype(F32)
@@ -406,69 +496,59 @@
     return jax.ShapeDtypeStruct(dims, BF)
 
 
-def local(
+def forward(
     features, conv_one, conv_two, conv_three, conv_four, depth_one, point_one, depth_two, point_two,
     conv_five, conv_six,
 ):
-    taps_one = jnp.pad(depth_one.astype(F32).T, ((0, 5), (0, 64)))
-    taps_two = jnp.pad(depth_two.astype(F32).T, ((0, 5), (0, 0)))
-    mix_one = jnp.pad(point_one, ((0, 0), (0, 64)))
     bands = shape(9, 512, 256)
 
-    rows = call(to_rows_kernel, shape(16, 4, 16, 128))(features.reshape(512, 256))
+    rows = call(to_rows_kernel, shape(16, 4, 16, 128))(features)
     own = lax.all_to_all(rows, PLANE, 0, 0, tiled=True, axis_index_groups=GROUPS)
     own = own.reshape(4, 4, 4, 16, 128)
     w1, w2, w3, w4 = call(encoder_weights_kernel, (bands,) * 4, limit=LIMITS[0])(
         conv_one, conv_two, conv_three, conv_four
     )
-    w5u, w5s, w6u, w6s = call(decoder_weights_kernel, (bands,) * 4, limit=LIMITS[1])(conv_five, conv_six)
-    q, s = position()
+    taps = jax.ShapeDtypeStruct((27, 128), F32)
+    w5u, w5s, w6u, w6s, taps_one, taps_two = call(
+        decoder_weights_kernel, (bands,) * 4 + (taps,) * 2, limit=LIMITS[1]
+    )(conv_five, conv_six, depth_one, depth_two)
     x_swaps = [swap_pairs(1, 0, parity) for parity in range(2)]
     z_swaps = [swap_pairs(0, 1, parity) for parity in range(2)]
-    x_got = []
-    for turn in range(2):
-        start = jnp.where((q + turn) % 2 == 0, 2, 0)
-        piece = lax.dynamic_slice_in_dim(own, start, 2, 0)
-        x_got.append(lax.ppermute(piece, EVERY, x_swaps[turn]))
-    broad = jnp.concatenate([x_got[0], own, x_got[1]], axis=0)
-    z_got = []
-    for turn in range(2):
-        piece = jnp.where((s + turn) % 2 == 0, broad[..., 8:16, :], broad[..., 0:8, :])
-        z_got.append(lax.ppermute(piece, EVERY, z_swaps[turn]))
-    own_first = call(
+    pieces = call(pick_x_kernel, (shape(6, 4, 16, 128),) * 2, flops=8 << 30)(own)
+    x_got = [lax.ppermute(piece, EVERY, pairs) for piece, pairs in zip(pieces, x_swaps)]
+    pieces = call(pick_z_kernel, (shape(28, 4, 8, 128),) * 2)(own, *x_got)
+    z_got = [lax.ppermute(piece, EVERY, pairs) for piece, pairs in zip(pieces, z_swaps)]
+    own_first, own_skip = call(
         own_rows_kernel,
-        shape(26, 16, 512),
+        (shape(26, 16, 512), shape(24, 16, 512)),
         [
-            pltpu.VMEM((32, 16, 512), F32),
+            pltpu.VMEM((28, 16, 512), F32),
             pltpu.VMEM((3, 28, 16, 512), BF),
             pltpu.VMEM((26, 16, 512), F32),
         ],
         flops=3 << 30,
         limit=16,
-    )(own, *x_got, w1)
-    skip, half_skip = call(
+    )(own, *x_got, w1, w2)
+    skip, half_skip, *pieces = call(
         encoder_kernel,
-        (shape(3, 19, 16, 512), shape(8, 8, 512)),
+        (shape(3, 19, 16, 512), shape(8, 8, 512), shape(6, 8, 512), shape(6, 8, 512)),
         [
-            pltpu.VMEM((32, 32, 512), F32),
+            pltpu.VMEM((28, 32, 512), F32),
             pltpu.VMEM((3, 28, 16, 512), BF),
-            pltpu.VMEM((2, 32, 512), F32),
-            pltpu.VMEM((3, 26, 32, 512), BF),
-            pltpu.VMEM((26, 32, 512), F32),
+            pltpu.VMEM((4, 32, 512), F32),
+            pltpu.VMEM((26, 16, 512), F32),
             pltpu.VMEM((3, 12, 16, 512), BF),
             pltpu.VMEM((3, 10, 16, 512), BF),
             pltpu.VMEM((4, 4, 32, 128), F32),
         ],
         flops=6 << 30,
         limit=LIMITS[2],
-    )(own, *x_got, *z_got, own_first, w1, w2, w3, w4)
+    )(own, *x_got, *z_got, own_first, own_skip, w1, w2, w3, w4)
     x_got = []
     for turn in range(2):
-        start = jnp.where((q + turn) % 2 == 0, 2, 0)
-        piece = lax.dynamic_slice_in_dim(half_skip, start, 6, 0)
-        x_got.append(lax.ppermute(piece, EVERY, x_swaps[turn]))
-    broad = jnp.concatenate([x_got[0], half_skip, x_got[1]], axis=0)
-    z_got = [lax.ppermute(broad, EVERY, z_swaps[turn]) for turn in range(2)]
+        x_got.append(lax.ppermute(pieces[turn], EVERY, x_swaps[turn]))
+    broad = call(join_kernel, shape(20, 8, 512))(half_skip, *x_got)
+    z_got = [lax.ppermute(broad, EVERY, pairs) for pairs in z_swaps]
     skip_part = call(
         skip_kernel, jax.ShapeDtypeStruct((16, 16, 512), F32), flops=2 << 30, limit=12
     )(skip, w6s)
@@ -491,15 +571,15 @@
         limit=LIMITS[3],
     )(
         half_skip, *x_got, *z_got, skip_part,
-        taps_one, mix_one, taps_two, point_two, w5u, w5s, w6u,
+        taps_one, point_one, taps_two, point_two, w5u, w5s, w6u,
     )
     back = lax.all_to_all(
         rows.reshape(16, 4, 16, 128), PLANE, 0, 0, tiled=True, axis_index_groups=GROUPS
     )
-    return call(from_rows_kernel, shape(512, 256))(back).reshape(32, 4, 4, 256)
+    return call(from_rows_kernel, shape(32, 4, 4, 256))(back)
 
 
 def solution(mesh):
     in_specs = (P(None, "gx", "gy", "gz"), P(), P(), P(), P(), P(), P(), P(), P(), P(), P())
     out_specs = P(None, "gx", "gy", "gz")
-    return jax.shard_map(local, mesh=mesh, in_specs=in_specs, out_specs=out_specs, check_vma=False)
+    return jax.shard_map(forward, mesh=mesh, in_specs=in_specs, out_specs=out_specs, check_vma=False)

time: 74.2 us -> 69.8 us (0.941)
  blocking collectives: 12.3 us -> 25.6 us
  waiting for transfers between devices: 20.1 us -> 7.5 us
  starting transfers between devices: 18.4 us -> 12.9 us
  Pallas kernels: 20 us -> 21.4 us
    all_to_all x1 -> x2, blocking collectives: 12.3 us -> 25.6 us  [the longest x1 13.3 us: forward(): lax.all_to_all(rows, PLANE, 0, 0, tiled=True, axis_index_groups=GROUPS)]
    all_to_all x1 -> x0, waiting for transfers between devices: 7.71 us -> none  [local(): lax.all_to_all(rows, PLANE, 0, 0, tiled=True, axis_index_groups=GROUPS)]
    all_to_all x1 -> x0, starting transfers between devices: 5.76 us -> none  [local(): lax.all_to_all(rows, PLANE, 0, 0, tiled=True, axis_index_groups=GROUPS)]
    ppermute x8, waiting for transfers between devices: 12.4 us -> 7.5 us  [the longest x2 4.12 us: forward(): z_got = [lax.ppermute(broad, EVERY, pairs) for pairs in z_swaps]]
    reshape x2 -> x0, local copies, waits for them, and re-layouts: 1.83 us -> none  [the longest x1 1.06 us: local(): features.reshape(512, 256)]
    pallas_call x8 -> x11, Pallas kernels: 20 us -> 21.4 us  [run(): pl.pallas_call(kernel, out_shape=outs, in_specs=[whole] * len(args), out_...]
    unnamed x23 -> x25, local copies, waits for them, and re-layouts: 0.17 us -> 1.34 us
  transfers between devices with their start and end apart: 9 -> 8, of which waited for: 5 -> 3; matrix products, arithmetic and copies ran while one was open for 0% -> 1% of each run, Pallas kernels for 8% -> 12%
where the time goes in v4:
time: 69.8 us; the launch traced here: 69 us
  blocking collectives  25.6 us (37%)
  Pallas kernels  21.4 us (31%)
  starting transfers between devices  12.9 us (18%)
  waiting for transfers between devices  7.5 us (11%)
  local copies, waits for them, and re-layouts  1.34 us (2%)
    pallas_call x11, Pallas kernels, run(): pl.pallas_call(kernel, out_shape=outs, in_specs=[whole] * len(args), out_...  21.4 us
    all_to_all x1, blocking collectives, forward(): lax.all_to_all(rows, PLANE, 0, 0, tiled=True, axis_index_groups=GROUPS)  13.3 us
    all_to_all x1, blocking collectives, forward(): lax.all_to_all(rows.reshape(16, 4, 16, 128), PLANE, 0, 0, tiled=True, axi...  12.3 us
    ppermute x4, starting transfers between devices, forward(): lax.ppermute(piece, EVERY, pairs)  6.86 us
    ppermute x2, waiting for transfers between devices, forward(): z_got = [lax.ppermute(broad, EVERY, pairs) for pairs in z_swaps]  4.12 us
    ppermute x2, starting transfers between devices, forward(): x_got.append(lax.ppermute(pieces[turn], EVERY, x_swaps[turn]))  4.03 us
    ppermute x4, waiting for transfers between devices, forward(): lax.ppermute(piece, EVERY, pairs)  3.34 us
    ppermute x2, starting transfers between devices, forward(): z_got = [lax.ppermute(broad, EVERY, pairs) for pairs in z_swaps]  2.04 us
  transfers between devices with their start and end apart: 8, of which 3 were waited for; matrix products, arithmetic and copies ran while one was open for 1% of the time, Pallas kernels for 12%

profile of v4, /device:TPU:72, one launch (start us, length us, event | category | flops | bytes accessed | tf_op | source)
XLA Modules:
  0.0 69.0 jit_solution(12268741295787817929)
XLA Ops:
  0.0 0.9 %copy-done.1 = bf16[32,4,4,256]{3,2,1,0:T(4,128)(2,1)S(1)} copy-done((bf16[32,4,4,256]{3,2,1,0:T(4,128)(2,1)S(1)}, bf16[32,4,4,256]{3,2,1,0:T(4,128)(2,1)}, u32[]{:S(2)}) %copy-start.1) | copy-done | bytes 262168
  1.0 0.7 shard_map.109
  1.6 13.3 %all_to_all.10 = bf16[16,4,16,128]{3,2,1,0:T(8,128)(2,1)S(1)} all-to-all(bf16[16,4,16,128]{3,2,1,0:T(8,128)(2,1)S(1)} %shard_map.109), channel_id=1, replica_groups={{0,4,8,12,16,20,24,28,32,36,40,44,48,52,56,60},{64,68,72,76,80,84,88,92..., dimensions={0} | all-to-all | bytes 524288 | tf_op jit(solution)/shard_map/all_to_all | solution.py:506
  15.0 0.5 collective-permute-start
  15.5 4.3 %collective-permute-start.1 = (bf16[6,4,16,128]{3,2,1,0:T(8,128)(2,1)S(1)}, bf16[6,4,16,128]{3,2,1,0:T(8,128)(2,1)S(1)}, u32[]{:S(2)}, u32[]{:S(2)}) collective-permute-start(bf16[6,4,16,128]{3,2,1,0:T(8,128)(2,1)S(1)} %get-tuple-element.26), channel_id=1, source_target_pairs={{64,128},{128,64},{80,144},{144,80},{84,148},{148,84},{68,132},{13... | collective-permute-start | bytes 294920 | tf_op jit(solution)/shard_map/ppermute | solution.py:518
  19.9 1.4 %shard_map.112 = (bf16[9,512,256]{2,1,0:T(8,128)(2,1)S(1)}, bf16[9,512,256]{2,1,0:T(8,128)(2,1)S(1)}, bf16[9,512,256]{2,1,0:T(8,128)(2,1)S(1)}, bf16[9,512,256]{2,1,0:T(8,128)(2,1)S(1)}) custom-call(bf16[32,864]{1,0:T(8,128)(2,1)S(1)} %copy-done.5, bf16[32,864]{1,0:T(8,128)(2,1)S(1)} %copy-done.6, bf16[64,864]{1,0:T(8,128)(2,1)S(1)} %copy-done.4, ...), custom_call_target="tpu_custom_call" | custom-call | bytes 4194304 | tf_op jit(solution)/shard_map/pallas_call | solution.py:482
  21.3 0.0 collective-permute-done.x1
  21.3 1.3 %collective-permute-done.1.x2 = bf16[6,4,16,128]{3,2,1,0:T(8,128)(2,1)S(1)} collective-permute-done((bf16[6,4,16,128]{3,2,1,0:T(8,128)(2,1)S(1)}, bf16[6,4,16,128]{3,2,1,0:T(8,128)(2,1)S(1)}, u32[]{:S(2)}, u32[]{:S(2)}) %collective-permute-start.1) | collective-permute-done | bytes 98336 | tf_op jit(solution)/shard_map/ppermute | solution.py:518
  22.6 0.1 shard_map.111
  22.7 0.1 collective-permute-start.2
  22.8 1.9 %collective-permute-start.3 = (bf16[28,4,8,128]{3,2,1,0:T(8,128)(2,1)S(1)}, bf16[28,4,8,128]{3,2,1,0:T(8,128)(2,1)S(1)}, u32[]{:S(2)}, u32[]{:S(2)}) collective-permute-start(bf16[28,4,8,128]{3,2,1,0:T(8,128)(2,1)S(1)} %get-tuple-element.28), channel_id=1, source_target_pairs={{16,20},{20,16},{4,8},{8,4},{24,28},{28,24},{12,44},{44,12},{60,56... | collective-permute-start | bytes 688136 | tf_op jit(solution)/shard_map/ppermute | solution.py:520
  24.7 3.9 %shard_map.113 = (bf16[26,16,512]{2,1,0:T(8,128)(2,1)S(1)}, bf16[24,16,512]{2,1,0:T(8,128)(2,1)S(1)}) custom-call(bf16[4,4,4,16,128]{4,3,2,1,0:T(8,128)(2,1)S(1)} %bitcast.5, bf16[6,4,16,128]{3,2,1,0:T(8,128)(2,1)S(1)} %collective-permute-done.x1, bf16[6,4,16,128]{3,2,1,0:T(8,128)(2,1)S(1)} %collective-permute-done.1.x2, ...), custom_call_target="tpu_custom_call" | custom-call | flops 3221225472 | bytes 4194304 | tf_op jit(solution)/shard_map/pallas_call | solution.py:482
  28.7 0.0 collective-permute-done.2.z1
  28.7 2.0 %collective-permute-done.3.z2 = bf16[28,4,8,128]{3,2,1,0:T(8,128)(2,1)S(1)} collective-permute-done((bf16[28,4,8,128]{3,2,1,0:T(8,128)(2,1)S(1)}, bf16[28,4,8,128]{3,2,1,0:T(8,128)(2,1)S(1)}, u32[]{:S(2)}, u32[]{:S(2)}) %collective-permute-start.3) | collective-permute-done | bytes 229408 | tf_op jit(solution)/shard_map/ppermute | solution.py:520
  30.7 0.0 copy-start.3
  30.7 7.0 %shard_map.114 = (bf16[3,19,16,512]{3,2,1,0:T(8,128)(2,1)S(1)}, bf16[8,8,512]{2,1,0:T(8,128)(2,1)S(1)}, bf16[6,8,512]{2,1,0:T(8,128)(2,1)S(1)}, bf16[6,8,512]{2,1,0:T(8,128)(2,1)S(1)}) custom-call(bf16[4,4,4,16,128]{4,3,2,1,0:T(8,128)(2,1)S(1)} %bitcast.6, bf16[6,4,16,128]{3,2,1,0:T(8,128)(2,1)S(1)} %collective-permute-done.x1, ...), custom_call_target="tpu_custom_call" | custom-call | flops 6442450944 | bytes 4194304 | tf_op jit(solution)/shard_map/pallas_call | solution.py:482
  37.8 0.1 collective-permute-start.4
  37.9 3.9 %collective-permute-start.5 = (bf16[6,8,512]{2,1,0:T(8,128)(2,1)S(1)}, bf16[6,8,512]{2,1,0:T(8,128)(2,1)S(1)}, u32[]{:S(2)}, u32[]{:S(2)}) collective-permute-start(bf16[6,8,512]{2,1,0:T(8,128)(2,1)S(1)} %get-tuple-element.37), channel_id=1, source_target_pairs={{64,128},{128,64},{80,144},{144,80},{84,148},{148,84},{68,132},{13... | collective-permute-start | bytes 147464 | tf_op jit(solution)/shard_map/ppermute | solution.py:549
  41.8 0.1 copy.13.d2
  41.9 0.1 copy.12.d1
  42.1 0.1 copy.14.p1
  42.2 1.6 %shard_map.116 = (bf16[9,512,256]{2,1,0:T(8,128)(2,1)S(1)}, bf16[9,512,256]{2,1,0:T(8,128)(2,1)S(1)}, bf16[9,512,256]{2,1,0:T(8,128)(2,1)S(1)}, bf16[9,512,256]{...) custom-call(bf16[64,5184]{1,0:T(8,128)(2,1)S(1)} %copy-done, bf16[32,2592]{1,0:T(8,128)(2,1)S(1)} %copy-done.3, ...), custom_call_target="tpu_custom_call" | custom-call | bytes 4194304 | tf_op jit(solution)/shard_map/pallas_call | solution.py:482
  43.8 0.0 collective-permute-done.4.x1
  43.8 0.0 collective-permute-done.5.x2
  43.9 0.1 collective-permute-start.6
  44.0 1.9 %collective-permute-start.7 = (bf16[20,8,512]{2,1,0:T(8,128)(2,1)S(1)}, bf16[20,8,512]{2,1,0:T(8,128)(2,1)S(1)}, u32[]{:S(2)}, u32[]{:S(2)}) collective-permute-start(bf16[20,8,512]{2,1,0:T(8,128)(2,1)S(1)} %shard_map.115), channel_id=1, source_target_pairs={{16,20},{20,16},{4,8},{8,4},{24,28},{28,24},{12,44},{44,12},{60,56... | collective-permute-start | bytes 491528 | tf_op jit(solution)/shard_map/ppermute | solution.py:551
  45.9 0.0 copy-start.7
  45.9 1.1 %shard_map.117.skip_part = f32[16,16,512]{2,1,0:T(8,128)S(1)} custom-call(bf16[3,19,16,512]{3,2,1,0:T(8,128)(2,1)S(1)} %get-tuple-element.38.skip, bf16[9,512,256]{2,1,0:T(8,128)(2,1)S(1)} %get-tuple-element.39.w6s), custom_call_target="tpu_custom_call" | custom-call | flops 2147483648 | bytes 4194304 | tf_op jit(solution)/shard_map/pallas_call | solution.py:482
  47.0 4.1 %collective-permute-done.7.z2 = bf16[20,8,512]{2,1,0:T(8,128)(2,1)S(1)} collective-permute-done((bf16[20,8,512]{2,1,0:T(8,128)(2,1)S(1)}, bf16[20,8,512]{2,1,0:T(8,128)(2,1)S(1)}, u32[]{:S(2)}, u32[]{:S(2)}) %collective-permute-start.7) | collective-permute-done | bytes 163872 | tf_op jit(solution)/shard_map/ppermute | solution.py:551
  51.2 4.4 %shard_map.118 = bf16[4,4,4,16,128]{4,3,2,1,0:T(8,128)(2,1)S(1)} custom-call(bf16[8,8,512]{2,1,0:T(8,128)(2,1)S(1)} %get-tuple-element.35.own, bf16[6,8,512]{2,1,0:T(8,128)(2,1)S(1)} %collective-permute-done.4.x1, bf16[6,8,512]{2,1,0:T(8,128)(2,1)S(1)} %collective-permute-done.5.x2, bf16[20,8,512]{2,1,0:T(8,128)(2,1)S(1)} %collective-permute-done.6.z1, ...), custom_call_target="tpu_custom_call" | custom-call | flops 2147483648 | bytes 4194304 | tf_op jit(solution)/shard_map/pallas_call | solution.py:482
  55.5 12.3 %all_to_all.11.rows_ref = bf16[16,4,16,128]{3,2,1,0:T(8,128)(2,1)S(1)} all-to-all(bf16[16,4,16,128]{3,2,1,0:T(8,128)(2,1)S(1)} %bitcast.2), channel_id=1, replica_groups={{0,4,8,12,16,20,24,28,32,36,40,44,48,52,56,60},{64,68,72,76,80,84,88,92..., dimensions={0} | all-to-all | bytes 524288 | tf_op jit(solution)/shard_map/all_to_all | solution.py:576
  67.9 1.2 %shard_map.119 = bf16[32,4,4,256]{3,2,1,0:T(4,128)(2,1)} custom-call(bf16[16,4,16,128]{3,2,1,0:T(8,128)(2,1)S(1)} %all_to_all.11.rows_ref), custom_call_target="tpu_custom_call" | custom-call | bytes 4194304 | tf_op jit(solution)/shard_map/pallas_call | solution.py:482
  (22 shorter events, 0.1 us)
Async XLA Ops:
  0.0 0.9 %copy-start.1 = (bf16[32,4,4,256]{3,2,1,0:T(4,128)(2,1)S(1)}, bf16[32,4,4,256]{3,2,1,0:T(4,128)(2,1)}, u32[]{:S(2)}) copy-start(bf16[32,4,4,256]{3,2,1,0:T(4,128)(2,1)} %cells_ref.1) | copy-start | bytes 786436
  14.9 4.9 %copy-start.2 = (bf16[64,1728]{1,0:T(8,128)(2,1)S(1)}, bf16[64,1728]{1,0:T(8,128)(2,1)}, u32[]{:S(2)}) copy-start(bf16[64,1728]{1,0:T(8,128)(2,1)} %w4.1) | copy-start | bytes 663556
  14.9 4.9 %copy-start.4 = (bf16[64,864]{1,0:T(8,128)(2,1)S(1)}, bf16[64,864]{1,0:T(8,128)(2,1)}, u32[]{:S(2)}) copy-start(bf16[64,864]{1,0:T(8,128)(2,1)} %w3.1) | copy-start | bytes 331780
  14.9 4.9 %copy-start.5 = (bf16[32,864]{1,0:T(8,128)(2,1)S(1)}, bf16[32,864]{1,0:T(8,128)(2,1)}, u32[]{:S(2)}) copy-start(bf16[32,864]{1,0:T(8,128)(2,1)} %w1.1) | copy-start | bytes 165892
  14.9 4.9 %copy-start.6 = (bf16[32,864]{1,0:T(8,128)(2,1)S(1)}, bf16[32,864]{1,0:T(8,128)(2,1)}, u32[]{:S(2)}) copy-start(bf16[32,864]{1,0:T(8,128)(2,1)} %w2.1) | copy-start | bytes 165892
  15.0 6.3 %collective-permute-start = (bf16[6,4,16,128]{3,2,1,0:T(8,128)(2,1)S(1)}, bf16[6,4,16,128]{3,2,1,0:T(8,128)(2,1)S(1)}, u32[]{:S(2)}, u32[]{:S(2)}) collective-permute-start(bf16[6,4,16,128]{3,2,1,0:T(8,128)(2,1)S(1)} %get-tuple-element.25), channel_id=1, source_target_pairs={{0,64},{64,0},{16,80},{80,16},{20,84},{84,20},{4,68},{68,4},{8,72}... | collective-permute-start | bytes 294920 | tf_op jit(solution)/shard_map/ppermute | solution.py:518
  15.5 7.1 %collective-permute-start.1 = (bf16[6,4,16,128]{3,2,1,0:T(8,128)(2,1)S(1)}, bf16[6,4,16,128]{3,2,1,0:T(8,128)(2,1)S(1)}, u32[]{:S(2)}, u32[]{:S(2)}) collective-permute-start(bf16[6,4,16,128]{3,2,1,0:T(8,128)(2,1)S(1)} %get-tuple-element.26), channel_id=1, source_target_pairs={{64,128},{128,64},{80,144},{144,80},{84,148},{148,84},{68,132},{13... | collective-permute-start | bytes 294920 | tf_op jit(solution)/shard_map/ppermute | solution.py:518
  22.7 6.0 %collective-permute-start.2 = (bf16[28,4,8,128]{3,2,1,0:T(8,128)(2,1)S(1)}, bf16[28,4,8,128]{3,2,1,0:T(8,128)(2,1)S(1)}, u32[]{:S(2)}, u32[]{:S(2)}) collective-permute-start(bf16[28,4,8,128]{3,2,1,0:T(8,128)(2,1)S(1)} %get-tuple-element.27), channel_id=1, source_target_pairs={{0,16},{16,0},{20,4},{4,20},{8,24},{24,8},{28,12},{12,28},{44,60},... | collective-permute-start | bytes 688136 | tf_op jit(solution)/shard_map/ppermute | solution.py:520
  22.8 7.9 %collective-permute-start.3 = (bf16[28,4,8,128]{3,2,1,0:T(8,128)(2,1)S(1)}, bf16[28,4,8,128]{3,2,1,0:T(8,128)(2,1)S(1)}, u32[]{:S(2)}, u32[]{:S(2)}) collective-permute-start(bf16[28,4,8,128]{3,2,1,0:T(8,128)(2,1)S(1)} %get-tuple-element.28), channel_id=1, source_target_pairs={{16,20},{20,16},{4,8},{8,4},{24,28},{28,24},{12,44},{44,12},{60,56... | collective-permute-start | bytes 688136 | tf_op jit(solution)/shard_map/ppermute | solution.py:520
  30.7 11.1 %copy-start.9 = (bf16[128,27]{0,1:T(8,128)(2,1)S(1)}, bf16[128,27]{0,1:T(8,128)(2,1)}, u32[]{:S(2)}) copy-start(bf16[128,27]{0,1:T(8,128)(2,1)} %param.18) | copy-start | bytes 20740
  30.7 11.2 %copy-start.10 = (bf16[64,27]{0,1:T(8,128)(2,1)S(1)}, bf16[64,27]{0,1:T(8,128)(2,1)}, u32[]{:S(2)}) copy-start(bf16[64,27]{0,1:T(8,128)(2,1)} %param.16) | copy-start | bytes 10372
  30.7 11.3 %copy-start.8 = (bf16[128,64]{0,1:T(8,128)(2,1)S(1)}, bf16[128,64]{0,1:T(8,128)(2,1)}, u32[]{:S(2)}) copy-start(bf16[128,64]{0,1:T(8,128)(2,1)} %param.17) | copy-start | bytes 49156
  30.7 11.5 %copy-start = (bf16[64,5184]{1,0:T(8,128)(2,1)S(1)}, bf16[64,5184]{1,0:T(8,128)(2,1)}, u32[]{:S(2)}) copy-start(bf16[64,5184]{1,0:T(8,128)(2,1)} %w5.1) | copy-start | bytes 1990660
  30.7 11.5 %copy-start.3 = (bf16[32,2592]{1,0:T(8,128)(2,1)S(1)}, bf16[32,2592]{1,0:T(8,128)(2,1)}, u32[]{:S(2)}) copy-start(bf16[32,2592]{1,0:T(8,128)(2,1)} %w6.1) | copy-start | bytes 497668
  37.8 6.0 %collective-permute-start.4 = (bf16[6,8,512]{2,1,0:T(8,128)(2,1)S(1)}, bf16[6,8,512]{2,1,0:T(8,128)(2,1)S(1)}, u32[]{:S(2)}, u32[]{:S(2)}) collective-permute-start(bf16[6,8,512]{2,1,0:T(8,128)(2,1)S(1)} %get-tuple-element.36), channel_id=1, source_target_pairs={{0,64},{64,0},{16,80},{80,16},{20,84},{84,20},{4,68},{68,4},{8,72}... | collective-permute-start | bytes 147464 | tf_op jit(solution)/shard_map/ppermute | solution.py:549
  37.9 6.0 %collective-permute-start.5 = (bf16[6,8,512]{2,1,0:T(8,128)(2,1)S(1)}, bf16[6,8,512]{2,1,0:T(8,128)(2,1)S(1)}, u32[]{:S(2)}, u32[]{:S(2)}) collective-permute-start(bf16[6,8,512]{2,1,0:T(8,128)(2,1)S(1)} %get-tuple-element.37), channel_id=1, source_target_pairs={{64,128},{128,64},{80,144},{144,80},{84,148},{148,84},{68,132},{13... | collective-permute-start | bytes 147464 | tf_op jit(solution)/shard_map/ppermute | solution.py:549
  43.9 3.2 %collective-permute-start.6 = (bf16[20,8,512]{2,1,0:T(8,128)(2,1)S(1)}, bf16[20,8,512]{2,1,0:T(8,128)(2,1)S(1)}, u32[]{:S(2)}, u32[]{:S(2)}) collective-permute-start(bf16[20,8,512]{2,1,0:T(8,128)(2,1)S(1)} %shard_map.115), channel_id=1, source_target_pairs={{0,16},{16,0},{20,4},{4,20},{8,24},{24,8},{28,12},{12,28},{44,60},... | collective-permute-start | bytes 491528 | tf_op jit(solution)/shard_map/ppermute | solution.py:551
  44.0 7.2 %collective-permute-start.7 = (bf16[20,8,512]{2,1,0:T(8,128)(2,1)S(1)}, bf16[20,8,512]{2,1,0:T(8,128)(2,1)S(1)}, u32[]{:S(2)}, u32[]{:S(2)}) collective-permute-start(bf16[20,8,512]{2,1,0:T(8,128)(2,1)S(1)} %shard_map.115), channel_id=1, source_target_pairs={{16,20},{20,16},{4,8},{8,4},{24,28},{28,24},{12,44},{44,12},{60,56... | collective-permute-start | bytes 491528 | tf_op jit(solution)/shard_map/ppermute | solution.py:551
  45.9 5.3 %copy-start.7 = (bf16[128,128]{1,0:T(8,128)(2,1)S(1)}, bf16[128,128]{1,0:T(8,128)(2,1)}, u32[]{:S(2)}) copy-start(bf16[128,128]{1,0:T(8,128)(2,1)} %p2.1) | copy-start | bytes 98308

commit v5 on v4

--- a/solution.py
+++ b/solution.py
@@ -368,7 +368,9 @@
         out[:, :, 256 * g : 256 * g + 256] = convolve([(skip.at[:, 0:18], w6s)], 16, 16, g)
 
 
-def depthwise(source, taps, planes, offset):
+def depthwise(source, taps, planes, offset, shifted):
+    for dz in range(3):
+        shifted[dz, 0 : planes + 2] = source[0 : planes + 2, pl.ds(offset + dz, 8), :]
     sums = []
     for t in range(4):
         total = jnp.zeros((planes, 8, 128), F32)
@@ -380,17 +382,14 @@
                 for dz in range(3):
                     tap = (dx * 3 + dy) * 3 + dz
                     factor = taps[tap : tap + 1, :].reshape(1, 1, 128)
-                    total += (
-                        source[dx : dx + planes, pl.ds(offset + dz, 8), 128 * at : 128 * at + 128]
-                        * factor
-                    )
+                    total += shifted[dz, dx : dx + planes, :, 128 * at : 128 * at + 128] * factor
         sums.append(total.reshape(planes * 8, 128).astype(BF))
     return sums
 
 
 def decoder_kernel(
     own, x1, x2, z1, z2, skip_part, d1, p1, d2, p2, w5u, w5s, w6u,
-    out, whole, sides, pooled, quarter, mixed, grown, ups, acc, tall, fine,
+    out, whole, sides, pooled, quarter, mixed, grown, ups, acc, tall, fine, shifted,
 ):
     q, s = position()
     plane_1 = 14 * (1 - q % 2)
@@ -420,7 +419,7 @@
             )
 
     mixed[...] = jnp.zeros_like(mixed)
-    spread = depthwise(quarter, d1, 8, 1)
+    spread = depthwise(quarter, d1, 8, 1, shifted)
     plane = lax.broadcasted_iota(jnp.int32, (8, 8, 128), 0) + (4 * q - 2)
     row = lax.broadcasted_iota(jnp.int32, (8, 8, 128), 1) + (4 * s - 2)
     inside = (plane >= 0) & (plane < 16) & (row >= 0) & (row < 256)
@@ -431,7 +430,7 @@
         value = jnp.where(inside, jnp.maximum(value, 0.0), 0.0)
         mixed[:, 0:8, 128 * t : 128 * t + 128] = value.astype(BF).astype(F32)
 
-    spread = depthwise(mixed, d2, 6, 0)
+    spread = depthwise(mixed, d2, 6, 0, shifted)
     plane = lax.broadcasted_iota(jnp.int32, (6, 8, 128), 0) + (4 * q - 1)
     row = lax.broadcasted_iota(jnp.int32, (6, 8, 128), 1) + (4 * s - 1)
     inside = (plane >= 0) & (plane < 16) & (row >= 0) & (row < 256)
@@ -517,7 +516,9 @@
     pieces = call(pick_x_kernel, (shape(6, 4, 16, 128),) * 2, flops=8 << 30)(own)
     x_got = [lax.ppermute(piece, EVERY, pairs) for piece, pairs in zip(pieces, x_swaps)]
     pieces = call(pick_z_kernel, (shape(28, 4, 8, 128),) * 2)(own, *x_got)
-    z_got = [lax.ppermute(piece, EVERY, pairs) for piece, pairs in zip(pieces, z_swaps)]
+    z_got = []
+    for turn in range(2):
+        z_got.append(lax.ppermute(pieces[turn], EVERY, z_swaps[turn]))
     own_first, own_skip = call(
         own_rows_kernel,
         (shape(26, 16, 512), shape(24, 16, 512)),
@@ -548,7 +549,9 @@
     for turn in range(2):
         x_got.append(lax.ppermute(pieces[turn], EVERY, x_swaps[turn]))
     broad = call(join_kernel, shape(20, 8, 512))(half_skip, *x_got)
-    z_got = [lax.ppermute(broad, EVERY, pairs) for pairs in z_swaps]
+    z_got = []
+    for turn in range(2):
+        z_got.append(lax.ppermute(broad, EVERY, z_swaps[turn]))
     skip_part = call(
         skip_kernel, jax.ShapeDtypeStruct((16, 16, 512), F32), flops=2 << 30, limit=12
     )(skip, w6s)
@@ -566,6 +569,7 @@
             pltpu.VMEM((16, 16, 512), F32),
             pltpu.VMEM((4, 32, 128), F32),
             pltpu.VMEM((3, 20, 16, 512), BF),
+            pltpu.VMEM((3, 10, 8, 512), F32),
         ],
         flops=2 << 30,
         limit=LIMITS[3],

time: 69.8 us -> 69.3 us (level)
    ppermute x2 -> x4, waiting for transfers between devices: 4.12 us -> 6.16 us  [the longest x2 4.12 us: forward(): z_got.append(lax.ppermute(broad, EVERY, z_swaps[turn]))]
    ppermute x4 -> x2, waiting for transfers between devices: 3.34 us -> 1.3 us  [forward(): lax.ppermute(piece, EVERY, pairs)]
    ppermute x2 -> x4, starting transfers between devices: 2.04 us -> 4.05 us  [the longest x2 2.04 us: forward(): z_got.append(lax.ppermute(broad, EVERY, z_swaps[turn]))]
    ppermute x4 -> x2, starting transfers between devices: 6.86 us -> 4.84 us  [forward(): lax.ppermute(piece, EVERY, pairs)]
where the time goes in v5:
time: 69.3 us; the launch traced here: 68.5 us
  blocking collectives  25.6 us (37%)
  Pallas kernels  20.9 us (30%)
  starting transfers between devices  12.9 us (19%)
  waiting for transfers between devices  7.5 us (11%)
  local copies, waits for them, and re-layouts  1.34 us (2%)
    pallas_call x11, Pallas kernels, run(): pl.pallas_call(kernel, out_shape=outs, in_specs=[whole] * len(args), out_...  20.9 us
    all_to_all x1, blocking collectives, forward(): lax.all_to_all(rows, PLANE, 0, 0, tiled=True, axis_index_groups=GROUPS)  13.3 us
    all_to_all x1, blocking collectives, forward(): lax.all_to_all(rows.reshape(16, 4, 16, 128), PLANE, 0, 0, tiled=True, axi...  12.3 us
    ppermute x2, starting transfers between devices, forward(): lax.ppermute(piece, EVERY, pairs)  4.84 us
    ppermute x2, waiting for transfers between devices, forward(): z_got.append(lax.ppermute(broad, EVERY, z_swaps[turn]))  4.12 us
    ppermute x2, starting transfers between devices, forward(): x_got.append(lax.ppermute(pieces[turn], EVERY, x_swaps[turn]))  4.03 us
    ppermute x2, waiting for transfers between devices, forward(): z_got.append(lax.ppermute(pieces[turn], EVERY, z_swaps[turn]))  2.04 us
    ppermute x2, starting transfers between devices, forward(): z_got.append(lax.ppermute(broad, EVERY, z_swaps[turn]))  2.04 us
  transfers between devices with their start and end apart: 8, of which 3 were waited for; matrix products, arithmetic and copies ran while one was open for 1% of the time, Pallas kernels for 12%

profile of v5, /device:TPU:72, one launch (start us, length us, event | category | flops | bytes accessed | tf_op | source)
XLA Modules:
  0.0 68.5 jit_solution(12623775595262898856)
XLA Ops:
  0.0 0.9 %copy-done.1 = bf16[32,4,4,256]{3,2,1,0:T(4,128)(2,1)S(1)} copy-done((bf16[32,4,4,256]{3,2,1,0:T(4,128)(2,1)S(1)}, bf16[32,4,4,256]{3,2,1,0:T(4,128)(2,1)}, u32[]{:S(2)}) %copy-start.1) | copy-done | bytes 262168
  1.0 0.7 shard_map.109
  1.6 13.3 %all_to_all.10 = bf16[16,4,16,128]{3,2,1,0:T(8,128)(2,1)S(1)} all-to-all(bf16[16,4,16,128]{3,2,1,0:T(8,128)(2,1)S(1)} %shard_map.109), channel_id=1, replica_groups={{0,4,8,12,16,20,24,28,32,36,40,44,48,52,56,60},{64,68,72,76,80,84,88,92..., dimensions={0} | all-to-all | bytes 524288 | tf_op jit(solution)/shard_map/all_to_all | solution.py:505
  15.0 0.5 collective-permute-start
  15.5 4.3 %collective-permute-start.1 = (bf16[6,4,16,128]{3,2,1,0:T(8,128)(2,1)S(1)}, bf16[6,4,16,128]{3,2,1,0:T(8,128)(2,1)S(1)}, u32[]{:S(2)}, u32[]{:S(2)}) collective-permute-start(bf16[6,4,16,128]{3,2,1,0:T(8,128)(2,1)S(1)} %get-tuple-element.26), channel_id=1, source_target_pairs={{64,128},{128,64},{80,144},{144,80},{84,148},{148,84},{68,132},{13... | collective-permute-start | bytes 294920 | tf_op jit(solution)/shard_map/ppermute | solution.py:517
  19.9 1.4 %shard_map.112 = (bf16[9,512,256]{2,1,0:T(8,128)(2,1)S(1)}, bf16[9,512,256]{2,1,0:T(8,128)(2,1)S(1)}, bf16[9,512,256]{2,1,0:T(8,128)(2,1)S(1)}, bf16[9,512,256]{2,1,0:T(8,128)(2,1)S(1)}) custom-call(bf16[32,864]{1,0:T(8,128)(2,1)S(1)} %copy-done.5, bf16[32,864]{1,0:T(8,128)(2,1)S(1)} %copy-done.6, bf16[64,864]{1,0:T(8,128)(2,1)S(1)} %copy-done.4, ...), custom_call_target="tpu_custom_call" | custom-call | bytes 4194304 | tf_op jit(solution)/shard_map/pallas_call | solution.py:481
  21.3 0.0 collective-permute-done.x1
  21.3 1.3 %collective-permute-done.1.x2 = bf16[6,4,16,128]{3,2,1,0:T(8,128)(2,1)S(1)} collective-permute-done((bf16[6,4,16,128]{3,2,1,0:T(8,128)(2,1)S(1)}, bf16[6,4,16,128]{3,2,1,0:T(8,128)(2,1)S(1)}, u32[]{:S(2)}, u32[]{:S(2)}) %collective-permute-start.1) | collective-permute-done | bytes 98336 | tf_op jit(solution)/shard_map/ppermute | solution.py:517
  22.6 0.1 shard_map.111
  22.7 0.1 collective-permute-start.2
  22.8 1.9 %collective-permute-start.3 = (bf16[28,4,8,128]{3,2,1,0:T(8,128)(2,1)S(1)}, bf16[28,4,8,128]{3,2,1,0:T(8,128)(2,1)S(1)}, u32[]{:S(2)}, u32[]{:S(2)}) collective-permute-start(bf16[28,4,8,128]{3,2,1,0:T(8,128)(2,1)S(1)} %get-tuple-element.28), channel_id=1, source_target_pairs={{16,20},{20,16},{4,8},{8,4},{24,28},{28,24},{12,44},{44,12},{60,56... | collective-permute-start | bytes 688136 | tf_op jit(solution)/shard_map/ppermute | solution.py:521
  24.7 3.9 %shard_map.113 = (bf16[26,16,512]{2,1,0:T(8,128)(2,1)S(1)}, bf16[24,16,512]{2,1,0:T(8,128)(2,1)S(1)}) custom-call(bf16[4,4,4,16,128]{4,3,2,1,0:T(8,128)(2,1)S(1)} %bitcast.5, bf16[6,4,16,128]{3,2,1,0:T(8,128)(2,1)S(1)} %collective-permute-done.x1, bf16[6,4,16,128]{3,2,1,0:T(8,128)(2,1)S(1)} %collective-permute-done.1.x2, ...), custom_call_target="tpu_custom_call" | custom-call | flops 3221225472 | bytes 4194304 | tf_op jit(solution)/shard_map/pallas_call | solution.py:481
  28.7 0.0 collective-permute-done.2.z1
  28.7 2.0 %collective-permute-done.3.z2 = bf16[28,4,8,128]{3,2,1,0:T(8,128)(2,1)S(1)} collective-permute-done((bf16[28,4,8,128]{3,2,1,0:T(8,128)(2,1)S(1)}, bf16[28,4,8,128]{3,2,1,0:T(8,128)(2,1)S(1)}, u32[]{:S(2)}, u32[]{:S(2)}) %collective-permute-start.3) | collective-permute-done | bytes 229408 | tf_op jit(solution)/shard_map/ppermute | solution.py:521
  30.7 0.0 copy-start.3
  30.7 7.0 %shard_map.114 = (bf16[3,19,16,512]{3,2,1,0:T(8,128)(2,1)S(1)}, bf16[8,8,512]{2,1,0:T(8,128)(2,1)S(1)}, bf16[6,8,512]{2,1,0:T(8,128)(2,1)S(1)}, bf16[6,8,512]{2,1,0:T(8,128)(2,1)S(1)}) custom-call(bf16[4,4,4,16,128]{4,3,2,1,0:T(8,128)(2,1)S(1)} %bitcast.6, bf16[6,4,16,128]{3,2,1,0:T(8,128)(2,1)S(1)} %collective-permute-done.x1, ...), custom_call_target="tpu_custom_call" | custom-call | flops 6442450944 | bytes 4194304 | tf_op jit(solution)/shard_map/pallas_call | solution.py:481
  37.8 0.1 collective-permute-start.4
  37.9 3.9 %collective-permute-start.5 = (bf16[6,8,512]{2,1,0:T(8,128)(2,1)S(1)}, bf16[6,8,512]{2,1,0:T(8,128)(2,1)S(1)}, u32[]{:S(2)}, u32[]{:S(2)}) collective-permute-start(bf16[6,8,512]{2,1,0:T(8,128)(2,1)S(1)} %get-tuple-element.37), channel_id=1, source_target_pairs={{64,128},{128,64},{80,144},{144,80},{84,148},{148,84},{68,132},{13... | collective-permute-start | bytes 147464 | tf_op jit(solution)/shard_map/ppermute | solution.py:550
  41.8 0.1 copy.13.d2
  41.9 0.1 copy.12.d1
  42.1 0.1 copy.14.p1
  42.2 1.6 %shard_map.116 = (bf16[9,512,256]{2,1,0:T(8,128)(2,1)S(1)}, bf16[9,512,256]{2,1,0:T(8,128)(2,1)S(1)}, bf16[9,512,256]{2,1,0:T(8,128)(2,1)S(1)}, bf16[9,512,256]{...) custom-call(bf16[64,5184]{1,0:T(8,128)(2,1)S(1)} %copy-done, bf16[32,2592]{1,0:T(8,128)(2,1)S(1)} %copy-done.3, ...), custom_call_target="tpu_custom_call" | custom-call | bytes 4194304 | tf_op jit(solution)/shard_map/pallas_call | solution.py:481
  43.8 0.0 collective-permute-done.4.x1
  43.8 0.0 collective-permute-done.5.x2
  43.9 0.1 collective-permute-start.6
  44.0 1.9 %collective-permute-start.7 = (bf16[20,8,512]{2,1,0:T(8,128)(2,1)S(1)}, bf16[20,8,512]{2,1,0:T(8,128)(2,1)S(1)}, u32[]{:S(2)}, u32[]{:S(2)}) collective-permute-start(bf16[20,8,512]{2,1,0:T(8,128)(2,1)S(1)} %shard_map.115), channel_id=1, source_target_pairs={{16,20},{20,16},{4,8},{8,4},{24,28},{28,24},{12,44},{44,12},{60,56... | collective-permute-start | bytes 491528 | tf_op jit(solution)/shard_map/ppermute | solution.py:554
  45.9 0.0 copy-start.7
  45.9 1.1 %shard_map.117.skip_part = f32[16,16,512]{2,1,0:T(8,128)S(1)} custom-call(bf16[3,19,16,512]{3,2,1,0:T(8,128)(2,1)S(1)} %get-tuple-element.38.skip, bf16[9,512,256]{2,1,0:T(8,128)(2,1)S(1)} %get-tuple-element.39.w6s), custom_call_target="tpu_custom_call" | custom-call | flops 2147483648 | bytes 4194304 | tf_op jit(solution)/shard_map/pallas_call | solution.py:481
  47.0 4.1 %collective-permute-done.7.z2 = bf16[20,8,512]{2,1,0:T(8,128)(2,1)S(1)} collective-permute-done((bf16[20,8,512]{2,1,0:T(8,128)(2,1)S(1)}, bf16[20,8,512]{2,1,0:T(8,128)(2,1)S(1)}, u32[]{:S(2)}, u32[]{:S(2)}) %collective-permute-start.7) | collective-permute-done | bytes 163872 | tf_op jit(solution)/shard_map/ppermute | solution.py:554
  51.2 3.9 %shard_map.118 = bf16[4,4,4,16,128]{4,3,2,1,0:T(8,128)(2,1)S(1)} custom-call(bf16[8,8,512]{2,1,0:T(8,128)(2,1)S(1)} %get-tuple-element.35.own, bf16[6,8,512]{2,1,0:T(8,128)(2,1)S(1)} %collective-permute-done.4.x1, bf16[6,8,512]{2,1,0:T(8,128)(2,1)S(1)} %collective-permute-done.5.x2, bf16[20,8,512]{2,1,0:T(8,128)(2,1)S(1)} %collective-permute-done.6.z1, ...), custom_call_target="tpu_custom_call" | custom-call | flops 2147483648 | bytes 4194304 | tf_op jit(solution)/shard_map/pallas_call | solution.py:481
  55.0 12.3 %all_to_all.11.rows_ref = bf16[16,4,16,128]{3,2,1,0:T(8,128)(2,1)S(1)} all-to-all(bf16[16,4,16,128]{3,2,1,0:T(8,128)(2,1)S(1)} %bitcast.2), channel_id=1, replica_groups={{0,4,8,12,16,20,24,28,32,36,40,44,48,52,56,60},{64,68,72,76,80,84,88,92..., dimensions={0} | all-to-all | bytes 524288 | tf_op jit(solution)/shard_map/all_to_all | solution.py:580
  67.3 1.2 %shard_map.119 = bf16[32,4,4,256]{3,2,1,0:T(4,128)(2,1)} custom-call(bf16[16,4,16,128]{3,2,1,0:T(8,128)(2,1)S(1)} %all_to_all.11.rows_ref), custom_call_target="tpu_custom_call" | custom-call | bytes 4194304 | tf_op jit(solution)/shard_map/pallas_call | solution.py:481
  (22 shorter events, 0.1 us)
Async XLA Ops:
  0.0 0.9 %copy-start.1 = (bf16[32,4,4,256]{3,2,1,0:T(4,128)(2,1)S(1)}, bf16[32,4,4,256]{3,2,1,0:T(4,128)(2,1)}, u32[]{:S(2)}) copy-start(bf16[32,4,4,256]{3,2,1,0:T(4,128)(2,1)} %cells_ref.1) | copy-start | bytes 786436
  14.9 4.9 %copy-start.2 = (bf16[64,1728]{1,0:T(8,128)(2,1)S(1)}, bf16[64,1728]{1,0:T(8,128)(2,1)}, u32[]{:S(2)}) copy-start(bf16[64,1728]{1,0:T(8,128)(2,1)} %w4.1) | copy-start | bytes 663556
  14.9 4.9 %copy-start.4 = (bf16[64,864]{1,0:T(8,128)(2,1)S(1)}, bf16[64,864]{1,0:T(8,128)(2,1)}, u32[]{:S(2)}) copy-start(bf16[64,864]{1,0:T(8,128)(2,1)} %w3.1) | copy-start | bytes 331780
  14.9 4.9 %copy-start.5 = (bf16[32,864]{1,0:T(8,128)(2,1)S(1)}, bf16[32,864]{1,0:T(8,128)(2,1)}, u32[]{:S(2)}) copy-start(bf16[32,864]{1,0:T(8,128)(2,1)} %w1.1) | copy-start | bytes 165892
  14.9 4.9 %copy-start.6 = (bf16[32,864]{1,0:T(8,128)(2,1)S(1)}, bf16[32,864]{1,0:T(8,128)(2,1)}, u32[]{:S(2)}) copy-start(bf16[32,864]{1,0:T(8,128)(2,1)} %w2.1) | copy-start | bytes 165892
  15.0 6.3 %collective-permute-start = (bf16[6,4,16,128]{3,2,1,0:T(8,128)(2,1)S(1)}, bf16[6,4,16,128]{3,2,1,0:T(8,128)(2,1)S(1)}, u32[]{:S(2)}, u32[]{:S(2)}) collective-permute-start(bf16[6,4,16,128]{3,2,1,0:T(8,128)(2,1)S(1)} %get-tuple-element.25), channel_id=1, source_target_pairs={{0,64},{64,0},{16,80},{80,16},{20,84},{84,20},{4,68},{68,4},{8,72}... | collective-permute-start | bytes 294920 | tf_op jit(solution)/shard_map/ppermute | solution.py:517
  15.5 7.1 %collective-permute-start.1 = (bf16[6,4,16,128]{3,2,1,0:T(8,128)(2,1)S(1)}, bf16[6,4,16,128]{3,2,1,0:T(8,128)(2,1)S(1)}, u32[]{:S(2)}, u32[]{:S(2)}) collective-permute-start(bf16[6,4,16,128]{3,2,1,0:T(8,128)(2,1)S(1)} %get-tuple-element.26), channel_id=1, source_target_pairs={{64,128},{128,64},{80,144},{144,80},{84,148},{148,84},{68,132},{13... | collective-permute-start | bytes 294920 | tf_op jit(solution)/shard_map/ppermute | solution.py:517
  22.7 6.0 %collective-permute-start.2 = (bf16[28,4,8,128]{3,2,1,0:T(8,128)(2,1)S(1)}, bf16[28,4,8,128]{3,2,1,0:T(8,128)(2,1)S(1)}, u32[]{:S(2)}, u32[]{:S(2)}) collective-permute-start(bf16[28,4,8,128]{3,2,1,0:T(8,128)(2,1)S(1)} %get-tuple-element.27), channel_id=1, source_target_pairs={{0,16},{16,0},{20,4},{4,20},{8,24},{24,8},{28,12},{12,28},{44,60},... | collective-permute-start | bytes 688136 | tf_op jit(solution)/shard_map/ppermute | solution.py:521
  22.8 7.9 %collective-permute-start.3 = (bf16[28,4,8,128]{3,2,1,0:T(8,128)(2,1)S(1)}, bf16[28,4,8,128]{3,2,1,0:T(8,128)(2,1)S(1)}, u32[]{:S(2)}, u32[]{:S(2)}) collective-permute-start(bf16[28,4,8,128]{3,2,1,0:T(8,128)(2,1)S(1)} %get-tuple-element.28), channel_id=1, source_target_pairs={{16,20},{20,16},{4,8},{8,4},{24,28},{28,24},{12,44},{44,12},{60,56... | collective-permute-start | bytes 688136 | tf_op jit(solution)/shard_map/ppermute | solution.py:521
  30.7 11.1 %copy-start.9 = (bf16[128,27]{0,1:T(8,128)(2,1)S(1)}, bf16[128,27]{0,1:T(8,128)(2,1)}, u32[]{:S(2)}) copy-start(bf16[128,27]{0,1:T(8,128)(2,1)} %param.18) | copy-start | bytes 20740
  30.7 11.2 %copy-start.10 = (bf16[64,27]{0,1:T(8,128)(2,1)S(1)}, bf16[64,27]{0,1:T(8,128)(2,1)}, u32[]{:S(2)}) copy-start(bf16[64,27]{0,1:T(8,128)(2,1)} %param.16) | copy-start | bytes 10372
  30.7 11.3 %copy-start.8 = (bf16[128,64]{0,1:T(8,128)(2,1)S(1)}, bf16[128,64]{0,1:T(8,128)(2,1)}, u32[]{:S(2)}) copy-start(bf16[128,64]{0,1:T(8,128)(2,1)} %param.17) | copy-start | bytes 49156
  30.7 11.5 %copy-start = (bf16[64,5184]{1,0:T(8,128)(2,1)S(1)}, bf16[64,5184]{1,0:T(8,128)(2,1)}, u32[]{:S(2)}) copy-start(bf16[64,5184]{1,0:T(8,128)(2,1)} %w5.1) | copy-start | bytes 1990660
  30.7 11.5 %copy-start.3 = (bf16[32,2592]{1,0:T(8,128)(2,1)S(1)}, bf16[32,2592]{1,0:T(8,128)(2,1)}, u32[]{:S(2)}) copy-start(bf16[32,2592]{1,0:T(8,128)(2,1)} %w6.1) | copy-start | bytes 497668
  37.8 6.0 %collective-permute-start.4 = (bf16[6,8,512]{2,1,0:T(8,128)(2,1)S(1)}, bf16[6,8,512]{2,1,0:T(8,128)(2,1)S(1)}, u32[]{:S(2)}, u32[]{:S(2)}) collective-permute-start(bf16[6,8,512]{2,1,0:T(8,128)(2,1)S(1)} %get-tuple-element.36), channel_id=1, source_target_pairs={{0,64},{64,0},{16,80},{80,16},{20,84},{84,20},{4,68},{68,4},{8,72}... | collective-permute-start | bytes 147464 | tf_op jit(solution)/shard_map/ppermute | solution.py:550
  37.9 6.0 %collective-permute-start.5 = (bf16[6,8,512]{2,1,0:T(8,128)(2,1)S(1)}, bf16[6,8,512]{2,1,0:T(8,128)(2,1)S(1)}, u32[]{:S(2)}, u32[]{:S(2)}) collective-permute-start(bf16[6,8,512]{2,1,0:T(8,128)(2,1)S(1)} %get-tuple-element.37), channel_id=1, source_target_pairs={{64,128},{128,64},{80,144},{144,80},{84,148},{148,84},{68,132},{13... | collective-permute-start | bytes 147464 | tf_op jit(solution)/shard_map/ppermute | solution.py:550
  43.9 3.2 %collective-permute-start.6 = (bf16[20,8,512]{2,1,0:T(8,128)(2,1)S(1)}, bf16[20,8,512]{2,1,0:T(8,128)(2,1)S(1)}, u32[]{:S(2)}, u32[]{:S(2)}) collective-permute-start(bf16[20,8,512]{2,1,0:T(8,128)(2,1)S(1)} %shard_map.115), channel_id=1, source_target_pairs={{0,16},{16,0},{20,4},{4,20},{8,24},{24,8},{28,12},{12,28},{44,60},... | collective-permute-start | bytes 491528 | tf_op jit(solution)/shard_map/ppermute | solution.py:554
  44.0 7.2 %collective-permute-start.7 = (bf16[20,8,512]{2,1,0:T(8,128)(2,1)S(1)}, bf16[20,8,512]{2,1,0:T(8,128)(2,1)S(1)}, u32[]{:S(2)}, u32[]{:S(2)}) collective-permute-start(bf16[20,8,512]{2,1,0:T(8,128)(2,1)S(1)} %shard_map.115), channel_id=1, source_target_pairs={{16,20},{20,16},{4,8},{8,4},{24,28},{28,24},{12,44},{44,12},{60,56... | collective-permute-start | bytes 491528 | tf_op jit(solution)/shard_map/ppermute | solution.py:554
  45.9 5.3 %copy-start.7 = (bf16[128,128]{1,0:T(8,128)(2,1)S(1)}, bf16[128,128]{1,0:T(8,128)(2,1)}, u32[]{:S(2)}) copy-start(bf16[128,128]{1,0:T(8,128)(2,1)} %p2.1) | copy-start | bytes 98308

commit v6 on v5

--- a/solution.py
+++ b/solution.py
@@ -10,7 +10,7 @@
 F32 = jnp.float32
 PLANE = ("gx", "gy")
 EVERY = ("gx", "gy", "gz")
-LIMITS = (24, 24, 32, 32)
+LIMITS = (8, 8, 12, 14)
 
 
 def slab_at(z_low, across, core):
@@ -130,18 +130,19 @@
     band(spread_lanes(w4[...], 64), o4, 64, 0, 64, 64, 64)
 
 
-def decoder_weights_kernel(w5, w6, d1, d2, o5u, o5s, o6u, o6s, taps_one, taps_two):
+def fine_weights_kernel(w6, o6u, o6s):
+    fine = spread_lanes(w6[...], 32)
+    band(fine, o6u, 96, 0, 64, 64, 32, grown=True)
+    band(fine, o6s, 96, 64, 32, 32, 32)
+
+
+def half_weights_kernel(w5, d1, d2, o5u, o5s, taps_one, taps_two):
     wide = spread_lanes(w5[...], 64)
     band(wide, o5u, 192, 0, 128, 128, 64, grown=True)
     band(wide, o5s, 192, 128, 64, 64, 64)
-    fine = spread_lanes(w6[...], 32)
-    band(fine, o6u, 96, 0, 64, 64, 32, grown=True)
-    band(fine, o6s, 96, 64, 32, 32, 32)
     for taps, weight in ((taps_one, d1), (taps_two, d2)):
-        same = identity()[: weight.shape[0]]
-        taps[...] = lax.dot_general(
-            weight[...], same, (((0,), (0,)), ((), ())), preferred_element_type=F32
-        )
+        same = identity()[: weight.shape[1]]
+        taps[...] = jnp.dot(weight[...], same, preferred_element_type=F32)
 
 
 def convolve(terms, planes, rows, g):
@@ -424,9 +425,7 @@
     row = lax.broadcasted_iota(jnp.int32, (8, 8, 128), 1) + (4 * s - 2)
     inside = (plane >= 0) & (plane < 16) & (row >= 0) & (row < 256)
     for t in range(4):
-        value = lax.dot_general(
-            spread[t][:, :64], p1[...], (((1,), (1,)), ((), ())), preferred_element_type=F32
-        ).reshape(8, 8, 128)
+        value = jnp.dot(spread[t][:, :64], p1[...], preferred_element_type=F32).reshape(8, 8, 128)
         value = jnp.where(inside, jnp.maximum(value, 0.0), 0.0)
         mixed[:, 0:8, 128 * t : 128 * t + 128] = value.astype(BF).astype(F32)
 
@@ -507,14 +506,17 @@
     w1, w2, w3, w4 = call(encoder_weights_kernel, (bands,) * 4, limit=LIMITS[0])(
         conv_one, conv_two, conv_three, conv_four
     )
+    w6u, w6s = call(fine_weights_kernel, (bands,) * 2, limit=8)(conv_six)
     taps = jax.ShapeDtypeStruct((27, 128), F32)
-    w5u, w5s, w6u, w6s, taps_one, taps_two = call(
-        decoder_weights_kernel, (bands,) * 4 + (taps,) * 2, limit=LIMITS[1]
-    )(conv_five, conv_six, depth_one, depth_two)
+    w5u, w5s, taps_one, taps_two = call(
+        half_weights_kernel, (bands,) * 2 + (taps,) * 2, limit=8
+    )(conv_five, depth_one.T, depth_two.T)
     x_swaps = [swap_pairs(1, 0, parity) for parity in range(2)]
     z_swaps = [swap_pairs(0, 1, parity) for parity in range(2)]
     pieces = call(pick_x_kernel, (shape(6, 4, 16, 128),) * 2, flops=8 << 30)(own)
-    x_got = [lax.ppermute(piece, EVERY, pairs) for piece, pairs in zip(pieces, x_swaps)]
+    x_got = []
+    for turn in range(2):
+        x_got.append(lax.ppermute(pieces[turn], EVERY, x_swaps[turn]))
     pieces = call(pick_z_kernel, (shape(28, 4, 8, 128),) * 2)(own, *x_got)
     z_got = []
     for turn in range(2):
@@ -575,7 +577,7 @@
         limit=LIMITS[3],
     )(
         half_skip, *x_got, *z_got, skip_part,
-        taps_one, point_one, taps_two, point_two, w5u, w5s, w6u,
+        taps_one, point_one.T, taps_two, point_two, w5u, w5s, w6u,
     )
     back = lax.all_to_all(
         rows.reshape(16, 4, 16, 128), PLANE, 0, 0, tiled=True, axis_index_groups=GROUPS

time: 69.3 us -> 69.3 us (level)
    ppermute x2 -> x0, starting transfers between devices: 4.84 us -> none  [forward(): lax.ppermute(piece, EVERY, pairs)]
    ppermute x2 -> x4, starting transfers between devices: 4.03 us -> 8.87 us  [forward(): x_got.append(lax.ppermute(pieces[turn], EVERY, x_swaps[turn]))]
    ppermute x2 -> x4, waiting for transfers between devices: 0.04 us -> 1.59 us  [forward(): x_got.append(lax.ppermute(pieces[turn], EVERY, x_swaps[turn]))]
    ppermute x2 -> x0, waiting for transfers between devices: 1.3 us -> none  [forward(): lax.ppermute(piece, EVERY, pairs)]
    pallas_call x11 -> x12, Pallas kernels: 20.9 us -> 20.9 us  [run(): pl.pallas_call(kernel, out_shape=outs, in_specs=[whole] * len(args), out_...]
  transfers between devices with their start and end apart: 8 -> 8, of which waited for: 3 -> 4; matrix products, arithmetic and copies ran while one was open for 1% -> 0% of each run, Pallas kernels for 12% -> 12%
where the time goes in v6:
time: 69.3 us; the launch traced here: 68.5 us
  blocking collectives  25.6 us (37%)
  Pallas kernels  20.9 us (30%)
  starting transfers between devices  12.9 us (19%)
  waiting for transfers between devices  7.75 us (11%)
  local copies, waits for them, and re-layouts  0.99 us (1%)
    pallas_call x12, Pallas kernels, run(): pl.pallas_call(kernel, out_shape=outs, in_specs=[whole] * len(args), out_...  20.9 us
    all_to_all x1, blocking collectives, forward(): lax.all_to_all(rows, PLANE, 0, 0, tiled=True, axis_index_groups=GROUPS)  13.3 us
    all_to_all x1, blocking collectives, forward(): lax.all_to_all(rows.reshape(16, 4, 16, 128), PLANE, 0, 0, tiled=True, axi...  12.3 us
    ppermute x4, starting transfers between devices, forward(): x_got.append(lax.ppermute(pieces[turn], EVERY, x_swaps[turn]))  8.87 us
    ppermute x2, waiting for transfers between devices, forward(): z_got.append(lax.ppermute(broad, EVERY, z_swaps[turn]))  4.12 us
    ppermute x2, waiting for transfers between devices, forward(): z_got.append(lax.ppermute(pieces[turn], EVERY, z_swaps[turn]))  2.04 us
    ppermute x2, starting transfers between devices, forward(): z_got.append(lax.ppermute(broad, EVERY, z_swaps[turn]))  2.03 us
    ppermute x2, starting transfers between devices, forward(): z_got.append(lax.ppermute(pieces[turn], EVERY, z_swaps[turn]))  2.01 us
  transfers between devices with their start and end apart: 8, of which 4 were waited for; matrix products, arithmetic and copies ran while one was open for 0% of the time, Pallas kernels for 12%

profile of v6, /device:TPU:72, one launch (start us, length us, event | category | flops | bytes accessed | tf_op | source)
XLA Modules:
  0.0 68.5 jit_solution(9620129420007520114)
XLA Ops:
  0.0 0.9 %copy-done.1 = bf16[32,4,4,256]{3,2,1,0:T(4,128)(2,1)S(1)} copy-done((bf16[32,4,4,256]{3,2,1,0:T(4,128)(2,1)S(1)}, bf16[32,4,4,256]{3,2,1,0:T(4,128)(2,1)}, u32[]{:S(2)}) %copy-start.1) | copy-done | bytes 262168
  1.0 0.7 shard_map.109
  1.6 13.3 %all_to_all.10 = bf16[16,4,16,128]{3,2,1,0:T(8,128)(2,1)S(1)} all-to-all(bf16[16,4,16,128]{3,2,1,0:T(8,128)(2,1)S(1)} %shard_map.109), channel_id=1, replica_groups={{0,4,8,12,16,20,24,28,32,36,40,44,48,52,56,60},{64,68,72,76,80,84,88,92..., dimensions={0} | all-to-all | bytes 524288 | tf_op jit(solution)/shard_map/all_to_all | solution.py:504
  15.0 0.5 collective-permute-start
  15.5 4.3 %collective-permute-start.1 = (bf16[6,4,16,128]{3,2,1,0:T(8,128)(2,1)S(1)}, bf16[6,4,16,128]{3,2,1,0:T(8,128)(2,1)S(1)}, u32[]{:S(2)}, u32[]{:S(2)}) collective-permute-start(bf16[6,4,16,128]{3,2,1,0:T(8,128)(2,1)S(1)} %get-tuple-element.26), channel_id=1, source_target_pairs={{64,128},{128,64},{80,144},{144,80},{84,148},{148,84},{68,132},{13... | collective-permute-start | bytes 294920 | tf_op jit(solution)/shard_map/ppermute | solution.py:519
  19.9 1.4 %shard_map.112 = (bf16[9,512,256]{2,1,0:T(8,128)(2,1)S(1)}, bf16[9,512,256]{2,1,0:T(8,128)(2,1)S(1)}, bf16[9,512,256]{2,1,0:T(8,128)(2,1)S(1)}, bf16[9,512,256]{2,1,0:T(8,128)(2,1)S(1)}) custom-call(bf16[32,864]{1,0:T(8,128)(2,1)S(1)} %copy-done.5, bf16[32,864]{1,0:T(8,128)(2,1)S(1)} %copy-done.6, bf16[64,864]{1,0:T(8,128)(2,1)S(1)} %copy-done.4, ...), custom_call_target="tpu_custom_call" | custom-call | bytes 4194304 | tf_op jit(solution)/shard_map/pallas_call | solution.py:480
  21.3 0.0 collective-permute-done.x1
  21.3 1.3 %collective-permute-done.1.x2 = bf16[6,4,16,128]{3,2,1,0:T(8,128)(2,1)S(1)} collective-permute-done((bf16[6,4,16,128]{3,2,1,0:T(8,128)(2,1)S(1)}, bf16[6,4,16,128]{3,2,1,0:T(8,128)(2,1)S(1)}, u32[]{:S(2)}, u32[]{:S(2)}) %collective-permute-start.1) | collective-permute-done | bytes 98336 | tf_op jit(solution)/shard_map/ppermute | solution.py:519
  22.6 0.1 shard_map.111
  22.7 0.1 collective-permute-start.2
  22.8 1.9 %collective-permute-start.3 = (bf16[28,4,8,128]{3,2,1,0:T(8,128)(2,1)S(1)}, bf16[28,4,8,128]{3,2,1,0:T(8,128)(2,1)S(1)}, u32[]{:S(2)}, u32[]{:S(2)}) collective-permute-start(bf16[28,4,8,128]{3,2,1,0:T(8,128)(2,1)S(1)} %get-tuple-element.28), channel_id=1, source_target_pairs={{16,20},{20,16},{4,8},{8,4},{24,28},{28,24},{12,44},{44,12},{60,56... | collective-permute-start | bytes 688136 | tf_op jit(solution)/shard_map/ppermute | solution.py:523
  24.7 3.9 %shard_map.113 = (bf16[26,16,512]{2,1,0:T(8,128)(2,1)S(1)}, bf16[24,16,512]{2,1,0:T(8,128)(2,1)S(1)}) custom-call(bf16[4,4,4,16,128]{4,3,2,1,0:T(8,128)(2,1)S(1)} %bitcast.8, bf16[6,4,16,128]{3,2,1,0:T(8,128)(2,1)S(1)} %collective-permute-done.x1, bf16[6,4,16,128]{3,2,1,0:T(8,128)(2,1)S(1)} %collective-permute-done.1.x2, ...), custom_call_target="tpu_custom_call" | custom-call | flops 3221225472 | bytes 4194304 | tf_op jit(solution)/shard_map/pallas_call | solution.py:480
  28.7 0.0 collective-permute-done.2.z1
  28.7 2.0 %collective-permute-done.3.z2 = bf16[28,4,8,128]{3,2,1,0:T(8,128)(2,1)S(1)} collective-permute-done((bf16[28,4,8,128]{3,2,1,0:T(8,128)(2,1)S(1)}, bf16[28,4,8,128]{3,2,1,0:T(8,128)(2,1)S(1)}, u32[]{:S(2)}, u32[]{:S(2)}) %collective-permute-start.3) | collective-permute-done | bytes 229408 | tf_op jit(solution)/shard_map/ppermute | solution.py:523
  30.7 7.0 %shard_map.114 = (bf16[3,19,16,512]{3,2,1,0:T(8,128)(2,1)S(1)}, bf16[8,8,512]{2,1,0:T(8,128)(2,1)S(1)}, bf16[6,8,512]{2,1,0:T(8,128)(2,1)S(1)}, bf16[6,8,512]{2,1,0:T(8,128)(2,1)S(1)}) custom-call(bf16[4,4,4,16,128]{4,3,2,1,0:T(8,128)(2,1)S(1)} %bitcast.9, bf16[6,4,16,128]{3,2,1,0:T(8,128)(2,1)S(1)} %collective-permute-done.x1, ...), custom_call_target="tpu_custom_call" | custom-call | flops 6442450944 | bytes 4194304 | tf_op jit(solution)/shard_map/pallas_call | solution.py:480
  37.7 0.1 collective-permute-start.4
  37.8 3.9 %collective-permute-start.5 = (bf16[6,8,512]{2,1,0:T(8,128)(2,1)S(1)}, bf16[6,8,512]{2,1,0:T(8,128)(2,1)S(1)}, u32[]{:S(2)}, u32[]{:S(2)}) collective-permute-start(bf16[6,8,512]{2,1,0:T(8,128)(2,1)S(1)} %get-tuple-element.37), channel_id=1, source_target_pairs={{64,128},{128,64},{80,144},{144,80},{84,148},{148,84},{68,132},{13... | collective-permute-start | bytes 147464 | tf_op jit(solution)/shard_map/ppermute | solution.py:552
  41.8 0.0 copy-done.3
  41.8 0.8 %shard_map.116 = (bf16[9,512,256]{2,1,0:T(8,128)(2,1)S(1)}, bf16[9,512,256]{2,1,0:T(8,128)(2,1)S(1)}) custom-call(bf16[32,2592]{1,0:T(8,128)(2,1)S(1)} %copy-done.3), custom_call_target="tpu_custom_call" | custom-call | bytes 4194304 | tf_op jit(solution)/shard_map/pallas_call | solution.py:480
  42.6 0.9 %shard_map.118 = (bf16[9,512,256]{2,1,0:T(8,128)(2,1)S(1)}, bf16[9,512,256]{2,1,0:T(8,128)(2,1)S(1)}, f32[27,128]{1,0:T(8,128)S(1)}, f32[27,128]{1,0:T(8,128)S(1)}) custom-call(bf16[64,5184]{1,0:T(8,128)(2,1)S(1)} %copy-done, bf16[27,64]{1,0:T(8,128)(2,1)S(1)} %bitcast.11, bf16[27,128]{1,0:T(8,128)(2,1)S(1)} %bitcast.12), custom_call_target="tpu_custom_call" | custom-call | bytes 4194304 | tf_op jit(solution)/shard_map/pallas_call | solution.py:480
  43.5 0.0 collective-permute-done.4.x1
  43.5 0.3 collective-permute-done.5.x2
  43.8 0.1 collective-permute-start.6
  43.9 1.9 %collective-permute-start.7 = (bf16[20,8,512]{2,1,0:T(8,128)(2,1)S(1)}, bf16[20,8,512]{2,1,0:T(8,128)(2,1)S(1)}, u32[]{:S(2)}, u32[]{:S(2)}) collective-permute-start(bf16[20,8,512]{2,1,0:T(8,128)(2,1)S(1)} %shard_map.115), channel_id=1, source_target_pairs={{16,20},{20,16},{4,8},{8,4},{24,28},{28,24},{12,44},{44,12},{60,56... | collective-permute-start | bytes 491528 | tf_op jit(solution)/shard_map/ppermute | solution.py:556
  45.9 0.0 copy-start.7
  45.9 0.0 copy-start.8
  45.9 1.1 %shard_map.117.skip_part = f32[16,16,512]{2,1,0:T(8,128)S(1)} custom-call(bf16[3,19,16,512]{3,2,1,0:T(8,128)(2,1)S(1)} %get-tuple-element.38.skip, bf16[9,512,256]{2,1,0:T(8,128)(2,1)S(1)} %get-tuple-element.39.w6s), custom_call_target="tpu_custom_call" | custom-call | flops 2147483648 | bytes 4194304 | tf_op jit(solution)/shard_map/pallas_call | solution.py:480
  47.0 0.0 collective-permute-done.6.z1
  47.0 4.1 %collective-permute-done.7.z2 = bf16[20,8,512]{2,1,0:T(8,128)(2,1)S(1)} collective-permute-done((bf16[20,8,512]{2,1,0:T(8,128)(2,1)S(1)}, bf16[20,8,512]{2,1,0:T(8,128)(2,1)S(1)}, u32[]{:S(2)}, u32[]{:S(2)}) %collective-permute-start.7) | collective-permute-done | bytes 163872 | tf_op jit(solution)/shard_map/ppermute | solution.py:556
  51.2 3.8 %shard_map.119 = bf16[4,4,4,16,128]{4,3,2,1,0:T(8,128)(2,1)S(1)} custom-call(bf16[8,8,512]{2,1,0:T(8,128)(2,1)S(1)} %get-tuple-element.35.own, bf16[6,8,512]{2,1,0:T(8,128)(2,1)S(1)} %collective-permute-done.4.x1, bf16[6,8,512]{2,1,0:T(8,128)(2,1)S(1)} %collective-permute-done.5.x2, bf16[20,8,512]{2,1,0:T(8,128)(2,1)S(1)} %collective-permute-done.6.z1, ...), custom_call_target="tpu_custom_call" | custom-call | flops 2147483648 | bytes 4194304 | tf_op jit(solution)/shard_map/pallas_call | solution.py:480
  55.0 12.3 %all_to_all.11.rows_ref = bf16[16,4,16,128]{3,2,1,0:T(8,128)(2,1)S(1)} all-to-all(bf16[16,4,16,128]{3,2,1,0:T(8,128)(2,1)S(1)} %bitcast.5), channel_id=1, replica_groups={{0,4,8,12,16,20,24,28,32,36,40,44,48,52,56,60},{64,68,72,76,80,84,88,92..., dimensions={0} | all-to-all | bytes 524288 | tf_op jit(solution)/shard_map/all_to_all | solution.py:582
  67.3 1.2 %shard_map.120 = bf16[32,4,4,256]{3,2,1,0:T(4,128)(2,1)} custom-call(bf16[16,4,16,128]{3,2,1,0:T(8,128)(2,1)S(1)} %all_to_all.11.rows_ref), custom_call_target="tpu_custom_call" | custom-call | bytes 4194304 | tf_op jit(solution)/shard_map/pallas_call | solution.py:480
  (20 shorter events, 0.1 us)
Async XLA Ops:
  0.0 0.9 %copy-start.1 = (bf16[32,4,4,256]{3,2,1,0:T(4,128)(2,1)S(1)}, bf16[32,4,4,256]{3,2,1,0:T(4,128)(2,1)}, u32[]{:S(2)}) copy-start(bf16[32,4,4,256]{3,2,1,0:T(4,128)(2,1)} %cells_ref.1) | copy-start | bytes 786436
  14.9 4.9 %copy-start.2 = (bf16[64,1728]{1,0:T(8,128)(2,1)S(1)}, bf16[64,1728]{1,0:T(8,128)(2,1)}, u32[]{:S(2)}) copy-start(bf16[64,1728]{1,0:T(8,128)(2,1)} %w4.1) | copy-start | bytes 663556
  14.9 4.9 %copy-start.4 = (bf16[64,864]{1,0:T(8,128)(2,1)S(1)}, bf16[64,864]{1,0:T(8,128)(2,1)}, u32[]{:S(2)}) copy-start(bf16[64,864]{1,0:T(8,128)(2,1)} %w3.1) | copy-start | bytes 331780
  14.9 4.9 %copy-start.5 = (bf16[32,864]{1,0:T(8,128)(2,1)S(1)}, bf16[32,864]{1,0:T(8,128)(2,1)}, u32[]{:S(2)}) copy-start(bf16[32,864]{1,0:T(8,128)(2,1)} %w1.1) | copy-start | bytes 165892
  14.9 4.9 %copy-start.6 = (bf16[32,864]{1,0:T(8,128)(2,1)S(1)}, bf16[32,864]{1,0:T(8,128)(2,1)}, u32[]{:S(2)}) copy-start(bf16[32,864]{1,0:T(8,128)(2,1)} %w2.1) | copy-start | bytes 165892
  15.0 6.3 %collective-permute-start = (bf16[6,4,16,128]{3,2,1,0:T(8,128)(2,1)S(1)}, bf16[6,4,16,128]{3,2,1,0:T(8,128)(2,1)S(1)}, u32[]{:S(2)}, u32[]{:S(2)}) collective-permute-start(bf16[6,4,16,128]{3,2,1,0:T(8,128)(2,1)S(1)} %get-tuple-element.25), channel_id=1, source_target_pairs={{0,64},{64,0},{16,80},{80,16},{20,84},{84,20},{4,68},{68,4},{8,72}... | collective-permute-start | bytes 294920 | tf_op jit(solution)/shard_map/ppermute | solution.py:519
  15.5 7.1 %collective-permute-start.1 = (bf16[6,4,16,128]{3,2,1,0:T(8,128)(2,1)S(1)}, bf16[6,4,16,128]{3,2,1,0:T(8,128)(2,1)S(1)}, u32[]{:S(2)}, u32[]{:S(2)}) collective-permute-start(bf16[6,4,16,128]{3,2,1,0:T(8,128)(2,1)S(1)} %get-tuple-element.26), channel_id=1, source_target_pairs={{64,128},{128,64},{80,144},{144,80},{84,148},{148,84},{68,132},{13... | collective-permute-start | bytes 294920 | tf_op jit(solution)/shard_map/ppermute | solution.py:519
  22.7 6.0 %collective-permute-start.2 = (bf16[28,4,8,128]{3,2,1,0:T(8,128)(2,1)S(1)}, bf16[28,4,8,128]{3,2,1,0:T(8,128)(2,1)S(1)}, u32[]{:S(2)}, u32[]{:S(2)}) collective-permute-start(bf16[28,4,8,128]{3,2,1,0:T(8,128)(2,1)S(1)} %get-tuple-element.27), channel_id=1, source_target_pairs={{0,16},{16,0},{20,4},{4,20},{8,24},{24,8},{28,12},{12,28},{44,60},... | collective-permute-start | bytes 688136 | tf_op jit(solution)/shard_map/ppermute | solution.py:523
  22.8 7.9 %collective-permute-start.3 = (bf16[28,4,8,128]{3,2,1,0:T(8,128)(2,1)S(1)}, bf16[28,4,8,128]{3,2,1,0:T(8,128)(2,1)S(1)}, u32[]{:S(2)}, u32[]{:S(2)}) collective-permute-start(bf16[28,4,8,128]{3,2,1,0:T(8,128)(2,1)S(1)} %get-tuple-element.28), channel_id=1, source_target_pairs={{16,20},{20,16},{4,8},{8,4},{24,28},{28,24},{12,44},{44,12},{60,56... | collective-permute-start | bytes 688136 | tf_op jit(solution)/shard_map/ppermute | solution.py:523
  30.7 11.1 %copy-start.3 = (bf16[32,2592]{1,0:T(8,128)(2,1)S(1)}, bf16[32,2592]{1,0:T(8,128)(2,1)}, u32[]{:S(2)}) copy-start(bf16[32,2592]{1,0:T(8,128)(2,1)} %w6.1) | copy-start | bytes 497668
  30.7 11.9 %copy-start = (bf16[64,5184]{1,0:T(8,128)(2,1)S(1)}, bf16[64,5184]{1,0:T(8,128)(2,1)}, u32[]{:S(2)}) copy-start(bf16[64,5184]{1,0:T(8,128)(2,1)} %w5.1) | copy-start | bytes 1990660
  30.7 11.9 %copy-start.9 = (bf16[64,27]{0,1:T(8,128)(2,1)S(1)}, bf16[64,27]{0,1:T(8,128)(2,1)}, u32[]{:S(2)}) copy-start(bf16[64,27]{0,1:T(8,128)(2,1)} %param.16) | copy-start | bytes 10372
  30.7 11.9 %copy-start.10 = (bf16[128,27]{0,1:T(8,128)(2,1)S(1)}, bf16[128,27]{0,1:T(8,128)(2,1)}, u32[]{:S(2)}) copy-start(bf16[128,27]{0,1:T(8,128)(2,1)} %param.18) | copy-start | bytes 20740
  37.7 5.8 %collective-permute-start.4 = (bf16[6,8,512]{2,1,0:T(8,128)(2,1)S(1)}, bf16[6,8,512]{2,1,0:T(8,128)(2,1)S(1)}, u32[]{:S(2)}, u32[]{:S(2)}) collective-permute-start(bf16[6,8,512]{2,1,0:T(8,128)(2,1)S(1)} %get-tuple-element.36), channel_id=1, source_target_pairs={{0,64},{64,0},{16,80},{80,16},{20,84},{84,20},{4,68},{68,4},{8,72}... | collective-permute-start | bytes 147464 | tf_op jit(solution)/shard_map/ppermute | solution.py:552
  37.8 6.0 %collective-permute-start.5 = (bf16[6,8,512]{2,1,0:T(8,128)(2,1)S(1)}, bf16[6,8,512]{2,1,0:T(8,128)(2,1)S(1)}, u32[]{:S(2)}, u32[]{:S(2)}) collective-permute-start(bf16[6,8,512]{2,1,0:T(8,128)(2,1)S(1)} %get-tuple-element.37), channel_id=1, source_target_pairs={{64,128},{128,64},{80,144},{144,80},{84,148},{148,84},{68,132},{13... | collective-permute-start | bytes 147464 | tf_op jit(solution)/shard_map/ppermute | solution.py:552
  43.8 3.2 %collective-permute-start.6 = (bf16[20,8,512]{2,1,0:T(8,128)(2,1)S(1)}, bf16[20,8,512]{2,1,0:T(8,128)(2,1)S(1)}, u32[]{:S(2)}, u32[]{:S(2)}) collective-permute-start(bf16[20,8,512]{2,1,0:T(8,128)(2,1)S(1)} %shard_map.115), channel_id=1, source_target_pairs={{0,16},{16,0},{20,4},{4,20},{8,24},{24,8},{28,12},{12,28},{44,60},... | collective-permute-start | bytes 491528 | tf_op jit(solution)/shard_map/ppermute | solution.py:556
  43.9 7.2 %collective-permute-start.7 = (bf16[20,8,512]{2,1,0:T(8,128)(2,1)S(1)}, bf16[20,8,512]{2,1,0:T(8,128)(2,1)S(1)}, u32[]{:S(2)}, u32[]{:S(2)}) collective-permute-start(bf16[20,8,512]{2,1,0:T(8,128)(2,1)S(1)} %shard_map.115), channel_id=1, source_target_pairs={{16,20},{20,16},{4,8},{8,4},{24,28},{28,24},{12,44},{44,12},{60,56... | collective-permute-start | bytes 491528 | tf_op jit(solution)/shard_map/ppermute | solution.py:556
  45.9 5.3 %copy-start.7 = (bf16[128,128]{1,0:T(8,128)(2,1)S(1)}, bf16[128,128]{1,0:T(8,128)(2,1)}, u32[]{:S(2)}) copy-start(bf16[128,128]{1,0:T(8,128)(2,1)} %p2.1) | copy-start | bytes 98308
  45.9 5.3 %copy-start.8 = (bf16[128,64]{0,1:T(8,128)(2,1)S(1)}, bf16[128,64]{0,1:T(8,128)(2,1)}, u32[]{:S(2)}) copy-start(bf16[128,64]{0,1:T(8,128)(2,1)} %param.17) | copy-start | bytes 49156
